TPU v7x, 32 devices: a whole 2x2x4 slice. The times are simulated.
32 devices in a mesh: brick: 8 (over y, x, core), help: 4 (over z).
Axes of the slice: x: 2, y: 2, z: 4, core: 2. Of those that a mesh axis runs over, the one named last changes fastest.
Arguments:
- positions: float32 [3, 2048], P(None, ('brick', 'help')), may hold values from 0 to 1
- velocities: float32 [3, 2048], P(None, ('brick', 'help')), may hold values from -5 to 5
- forces_in: float32 [3, 2048], P(None, ('brick', 'help')), may hold values from -5 to 5
- neighbors: int32 [2048, 128], P(('brick', 'help')), may hold values from -1 to 767, as said below
- w_embed1: float32 [32], replicated, may hold values from -4 to 4
- b_embed1: float32 [32], replicated, may hold values from -3 to 3
- w_embed2: bfloat16 [32, 64], replicated, may hold values from -1 to 1
- b_embed2: float32 [64], replicated, may hold values from -3 to 3
- w_embed3: bfloat16 [64, 128], replicated, may hold values from -0.75 to 0.75
- b_embed3: float32 [128], replicated, may hold values from -3 to 3
- w_fit1: bfloat16 [2048, 240], replicated, may hold values from -0.125 to 0.125
- b_fit1: float32 [240], replicated, may hold values from -3 to 3
- w_fit2: bfloat16 [240, 240], replicated, may hold values from -0.375 to 0.375
- b_fit2: float32 [240], replicated, may hold values from -3 to 3
- w_out: float32 [240], replicated, may hold values from -0.375 to 0.375
Outputs:
- positions_out: float32 [3, 2048], P(None, ('brick', 'help'))
- velocities_out: float32 [3, 2048], P(None, ('brick', 'help'))
- energy: float32 [2048], P(('brick', 'help'))
- forces_out: float32 [3, 2048], P(None, ('brick', 'help'))
Inputs may be any that keep to these rules, and one draw needn't show every extreme that they name: `neighbors`: row i holds atom i's neighbours as table entries: 0 to 255 the atoms of the brick before its own (cyclically), 256 to 511 its own brick, 512 to 767 the brick after; -1 pads. Live entries come first, an entry may repeat, an atom never lists itself. In the first half of the bricks an atom has 96 to 128 live entries, in the other bricks 128 / 4 to 64.
All inputs are finite; a program needn't handle non-finite values.
Results may differ from a plain program's by a relative error of at most 0.011.
Values sent between devices are 32-bit elements; how exact they have to be, the bound alone decides.
No kernel may reach another device: no remote copies, remote signals or barrier semaphores. Data moves between devices by JAX's collectives and lax.ppermute only.
A program may use at most 64 MiB of HBM per device.

v0:
```python
import jax
import jax.numpy as jnp
from jax import lax
from jax.sharding import PartitionSpec as P

NEIGHBOUR_SLOTS = 128
M2 = 16
STEPS = 2


kick_scale = 0.25
time_step = 0.05
highest_precision = lax.Precision.HIGHEST


def extended(value, sides, width):
    for axis, dim in sides:
        size, length = (lax.axis_size(axis), value.shape[dim])
        up = [(i, (i + 1) % size) for i in range(size)]
        down = [(j, i) for i, j in up]
        last = lax.slice_in_dim(value, length - width, length, axis=dim)
        first = lax.slice_in_dim(value, 0, width, axis=dim)
        before = lax.ppermute(last, axis, up)
        after = lax.ppermute(first, axis, down)
        value = jnp.concatenate([before, value, after], axis=dim)
    return value


def pair_terms(displace, live_mask, weights):
    (
        w_embed1,
        b_embed1,
        w_embed2,
        b_embed2,
        w_embed3,
        b_embed3,
        w_fit1,
        b_fit1,
        w_fit2,
        b_fit2,
        w_out,
    ) = weights
    blocks, slot_count = live_mask.shape
    quad_dist = jnp.sum(displace * displace, axis=0) + 0.25
    radius = jnp.sqrt(quad_dist)
    smooth = live_mask / radius
    environment_matrix = jnp.concatenate(
        [smooth[None], live_mask[None] * displace / quad_dist[None]], axis=0
    ).astype(jnp.bfloat16)
    flat_smooth = smooth.reshape(1, -1)
    hidden_first = jnp.tanh(w_embed1[:, None] * flat_smooth + b_embed1[:, None])
    pre_second = (
        jnp.dot(w_embed2.T, hidden_first.astype(jnp.bfloat16), preferred_element_type=jnp.float32)
        + b_embed2[:, None]
    )
    tanh_second = jnp.tanh(pre_second)
    hidden_second = jnp.concatenate([hidden_first, hidden_first], axis=0) + tanh_second
    pre_third = (
        jnp.dot(w_embed3.T, hidden_second.astype(jnp.bfloat16), preferred_element_type=jnp.float32)
        + b_embed3[:, None]
    )
    tanh_third = jnp.tanh(pre_third)
    embedding = (jnp.concatenate([hidden_second, hidden_second], axis=0) + tanh_third).astype(
        jnp.bfloat16
    )
    embedding_width = embedding.shape[0]
    embedding_rows = embedding.reshape(embedding_width, blocks, slot_count)
    descriptor_tensor = (
        jnp.einsum(
            "srj,lrj->rsl", environment_matrix, embedding_rows, preferred_element_type=jnp.float32
        )
        / NEIGHBOUR_SLOTS
    )
    axis_part = descriptor_tensor[:, :, :M2]
    descriptor = jnp.einsum(
        "bce,bck->bek", descriptor_tensor, axis_part, precision=highest_precision
    )
    flat_descr = descriptor.reshape(blocks, -1).astype(jnp.bfloat16)
    fit_hidden = jnp.tanh(jnp.dot(flat_descr, w_fit1, preferred_element_type=jnp.float32) + b_fit1)
    pre_out = (
        jnp.dot(fit_hidden.astype(jnp.bfloat16), w_fit2, preferred_element_type=jnp.float32)
        + b_fit2
    )
    tanh_out = jnp.tanh(pre_out)
    energy = jnp.dot(fit_hidden + tanh_out, w_out, precision=highest_precision)
    grad_out = (w_out[None, :] * (1.0 - tanh_out * tanh_out)).astype(jnp.bfloat16)
    grad_fit = w_out[None, :] + jnp.dot(grad_out, w_fit2.T, preferred_element_type=jnp.float32)
    grad_act = (grad_fit * (1.0 - fit_hidden * fit_hidden)).astype(jnp.bfloat16)
    grad_descr = jnp.dot(grad_act, w_fit1.T, preferred_element_type=jnp.float32).reshape(
        blocks, embedding_width, -1
    )
    grad_tensor = jnp.einsum("bek,bck->bce", grad_descr, axis_part, precision=highest_precision)
    extra_grad = jnp.einsum(
        "bek,bce->bck", grad_descr, descriptor_tensor, precision=highest_precision
    )
    grad_tensor = grad_tensor + jnp.pad(
        extra_grad, ((0, 0), (0, 0), (0, embedding_width - extra_grad.shape[2]))
    )
    descriptor_product_gradient = grad_tensor.astype(jnp.bfloat16)
    environment_gradient = (
        jnp.einsum(
            "ohm,hdo->dhm",
            embedding_rows,
            descriptor_product_gradient,
            preferred_element_type=jnp.float32,
        )
        / NEIGHBOUR_SLOTS
    )
    embedding_gradient = (
        jnp.einsum(
            "zmj,mzr->rmj",
            environment_matrix,
            descriptor_product_gradient,
            preferred_element_type=jnp.float32,
        ).reshape(embedding_width, -1)
        / NEIGHBOUR_SLOTS
    )
    grad_third = (embedding_gradient * (1.0 - tanh_third * tanh_third)).astype(jnp.bfloat16)
    half_width = embedding_width // 2
    grad_hidden2 = (
        embedding_gradient[:half_width]
        + embedding_gradient[half_width:]
        + jnp.dot(w_embed3, grad_third, preferred_element_type=jnp.float32)
    )
    grad_second = (grad_hidden2 * (1.0 - tanh_second * tanh_second)).astype(jnp.bfloat16)
    quarter = half_width // 2
    grad_hidden1 = (
        grad_hidden2[:quarter]
        + grad_hidden2[quarter:]
        + jnp.dot(w_embed2, grad_second, preferred_element_type=jnp.float32)
    )
    grad_smooth = (
        jnp.dot(
            w_embed1,
            grad_hidden1 * (1.0 - hidden_first * hidden_first),
            precision=highest_precision,
        ).reshape(blocks, slot_count)
        + environment_gradient[0]
    )
    radial = jnp.sum(environment_gradient[1:] * displace, axis=0)
    factor = -grad_smooth / (radius * quad_dist) - 2.0 * radial / (quad_dist * quad_dist)
    pair_grad = live_mask[None] * (
        displace * factor[None] + environment_gradient[1:] / quad_dist[None]
    )
    return (energy, pair_grad)


def ghost_table(coords):
    stacked = coords[:, None, :]
    brick_pos = lax.all_gather(stacked, "help", axis=2, tiled=True)
    gathered = extended(brick_pos, (("brick", 1),), 1)
    return gathered.reshape(3, -1)


def return_forces(gathered):
    reduced = lax.psum_scatter(gathered, "help", scatter_dimension=2, tiled=True)
    padded = extended(reduced, (("brick", 1),), 1)
    returned = padded[:, 0] + padded[:, 2] + padded[:, 4]
    return returned


def evaluate(coords, neighbors, weights):
    ghost = ghost_table(coords)
    brick_len = ghost.shape[1] // 3
    atom_count = coords.shape[1]
    safe_index = jnp.maximum(neighbors, 0)
    live_mask = (neighbors >= 0).astype(jnp.float32)
    shift_x = (safe_index // brick_len - 1).astype(jnp.float32)
    block_size = 32
    block_count = atom_count // block_size

    def one_block(pieces):
        own_pos, table_index, offset, mask_rows = pieces
        neighbour_pos = jnp.take(ghost, table_index, axis=1)
        displace = neighbour_pos - own_pos[:, :, None]
        displace = (
            jnp.concatenate([displace[:1] + offset[None], displace[1:]], axis=0) * mask_rows[None]
        )
        return pair_terms(displace, mask_rows, weights)

    own_blocks = coords.reshape(3, block_count, block_size).transpose(1, 0, 2)
    energy, pair_grads = lax.map(
        one_block,
        (
            own_blocks,
            safe_index.reshape(block_count, block_size, -1),
            shift_x.reshape(block_count, block_size, -1),
            live_mask.reshape(block_count, block_size, -1),
        ),
    )
    pair_grads = pair_grads.transpose(1, 0, 2, 3).reshape(3, atom_count, -1)
    energy_rows = energy.reshape(-1)
    gathered = jnp.zeros((3, 3 * brick_len), jnp.float32).at[:, safe_index].add(pair_grads)
    returned = return_forces(gathered.reshape(3, 3, brick_len))
    return (energy_rows, jnp.sum(pair_grads, axis=2) - returned)


def local(
    positions,
    velocities,
    forces_in,
    neighbors,
    w_embed1,
    b_embed1,
    w_embed2,
    b_embed2,
    w_embed3,
    b_embed3,
    w_fit1,
    b_fit1,
    w_fit2,
    b_fit2,
    w_out,
):
    weights = (
        w_embed1,
        b_embed1,
        w_embed2,
        b_embed2,
        w_embed3,
        b_embed3,
        w_fit1,
        b_fit1,
        w_fit2,
        b_fit2,
        w_out,
    )
    coords = positions
    speed = velocities
    force_now = forces_in
    energy = jnp.zeros((positions.shape[1],), jnp.float32)
    for md_step in range(STEPS):
        speed = speed + kick_scale * force_now
        coords = coords + time_step * speed
        energy, force_now = evaluate(coords, neighbors, weights)
        speed = speed + kick_scale * force_now
    return (coords, speed, energy, force_now)


def solution(mesh):
    return jax.shard_map(
        local,
        mesh=mesh,
        in_specs=(
            P(None, ("brick", "help")),
            P(None, ("brick", "help")),
            P(None, ("brick", "help")),
            P(("brick", "help"), None),
            P(),
            P(),
            P(),
            P(),
            P(),
            P(),
            P(),
            P(),
            P(),
            P(),
            P(),
        ),
        out_specs=(
            P(None, ("brick", "help")),
            P(None, ("brick", "help")),
            P(("brick", "help")),
            P(None, ("brick", "help")),
        ),
        check_vma=False,
    )
```

profile of v0, /device:TPU:0, one launch (start us, length us, event | category | flops | bytes accessed | tf_op | source)
XLA Modules:
  0.0 359.2 jit_solution(11644134132301394717)
XLA Ops:
  7.9 13.6 %all-gather.2 = f32[4,64,3]{1,2,0:T(4,128)S(1)} all-gather(f32[1,64,3]{1,2,0:T(4,128)S(1)} %bitcast.479), channel_id=2, replica_groups=mesh['brick'=8,'help'=4] {'help'}, dimensions={0}, use_global_device_ids=true | all-gather | bytes 3840 | tf_op jit(solution)/shard_map/all_gather | solution.py:150
  26.5 71.5 %while.26 = (s32[]{:T(128)}, f32[2,3,32,128]{3,1,2,0:T(4,128)}, f32[2,32,128]{2,0,1:T(2,128)S(1)}, s32[2,32,128]{2,1,0:T(8,128)}, f32[3,768]{0,1:T(8,128)S(1)}, ...) while((s32[]{:T(128)}, f32[2,3,32,128]{3,1,2,0:T(4,128)}, ...), condition=%wide.region_3.5_spmd, body=%wide.region_0.4_spmd.sunk | while | flops 271267840 | bytes 53851500 | solution.py:182
  27.4 10.8 %gather_fusion = f32[4096,3]{1,0:T(8,128)S(1)} fusion(f32[3,768]{0,1:T(8,128)S(1)} %get-tuple-element.963, s32[4096]{0:T(1024)S(1)} %bitcast_clamp_fusion.4), kind=kCustom, calls=%fused_computation.clone.clone.1 | custom fusion | bytes 114688 | tf_op jit(solution)/shard_map/while/body/eval_jaxpr/jit(_take)/gather | solution.py:174
  40.7 2.1 maximum_add_fusion.6
  51.0 1.5 fusion.267
  52.5 1.8 copy.234
  63.1 10.8 %gather_fusion = f32[4096,3]{1,0:T(8,128)S(1)} fusion(f32[3,768]{0,1:T(8,128)S(1)} %get-tuple-element.963, s32[4096]{0:T(1024)S(1)} %bitcast_clamp_fusion.4), kind=kCustom, calls=%fused_computation.clone.clone.1 | custom fusion | bytes 114688 | tf_op jit(solution)/shard_map/while/body/eval_jaxpr/jit(_take)/gather | solution.py:174
  76.5 2.1 maximum_add_fusion.6
  84.2 1.4 fusion.265
  86.7 1.5 fusion.267
  88.3 1.8 copy.234
  98.0 3.5 copy.144
  101.6 45.1 %scatter_custom_fusion = f32[3,768]{0,1:T(8,128)S(1)} fusion(s32[8192]{0:T(1024)} %get-tuple-element.670, f32[8192,3]{1,0:T(8,128)} %bitcast.458, f32[]{:T(128)} %constant.160.clone.1), kind=kCustom, calls=%fused_computation.189 | custom fusion | flops 24576 | bytes 9728 | tf_op jit(solution)/shard_map/scatter-add | solution.py:193
  147.9 24.6 %reduce-scatter.7.cloned.1.call-done = f32[64,9]{1,0:T(8,128)} async-done(((f32[256,9]{1,0:T(8,128)}), f32[64,9]{1,0:T(8,128)}) %reduce-scatter.7.cloned.1.call-update) | async-done | bytes 2320
  174.8 2.7 collective-permute-done.2
  178.1 11.9 %all-gather.3 = f32[4,64,3]{1,2,0:T(4,128)S(1)} all-gather(f32[1,64,3]{1,2,0:T(4,128)S(1)} %bitcast.480), channel_id=3, replica_groups=mesh['brick'=8,'help'=4] {'help'}, dimensions={0}, use_global_device_ids=true | all-gather | bytes 3840 | tf_op jit(solution)/shard_map/all_gather | solution.py:150
  191.5 2.8 collective-permute-done.4
  195.9 77.6 %while.27 = (s32[]{:T(128)}, f32[2,32]{1,0:T(2,128)}, f32[2,3,32,128]{3,1,2,0:T(4,128)}, f32[2,32,128]{2,0,1:T(2,128)S(1)}, s32[2,32,128]{2,1,0:T(8,128)}, /*ind...) while((s32[]{:T(128)}, f32[2,32]{1,0:T(2,128)}, ...), condition=%wide.region_10.12_spmd, body=%wide.region_7.11_spmd.sunk | while | flops 271367680 | bytes 45020100 | solution.py:182
  196.7 11.8 %gather_fusion.1 = f32[4096,3]{1,0:T(8,128)S(1)} fusion(f32[3,768]{0,1:T(8,128)} %get-tuple-element.1025, s32[4096]{0:T(1024)S(1)} %bitcast_clamp_fusion.5), kind=kCustom, calls=%fused_computation.1.clone.clone.1 | custom fusion | bytes 114688 | tf_op jit(solution)/shard_map/while/body/eval_jaxpr/jit(_take)/gather | solution.py:174
  211.1 2.1 maximum_add_fusion.7
  222.5 2.4 fusion.307
  224.8 1.7 copy.242
  227.4 1.6 fusion.310
  235.5 11.8 %gather_fusion.1 = f32[4096,3]{1,0:T(8,128)S(1)} fusion(f32[3,768]{0,1:T(8,128)} %get-tuple-element.1025, s32[4096]{0:T(1024)S(1)} %bitcast_clamp_fusion.5), kind=kCustom, calls=%fused_computation.1.clone.clone.1 | custom fusion | bytes 114688 | tf_op jit(solution)/shard_map/while/body/eval_jaxpr/jit(_take)/gather | solution.py:174
  249.9 2.1 maximum_add_fusion.7
  261.2 2.4 fusion.307
  263.6 1.7 copy.242
  266.2 1.6 fusion.310
  273.5 3.5 copy.152
  277.0 45.1 %scatter_custom_fusion.1 = f32[3,768]{0,1:T(8,128)S(1)} fusion(s32[8192]{0:T(1024)} %get-tuple-element.670, f32[8192,3]{1,0:T(8,128)} %bitcast.457, f32[]{:T(128)} %constant.160.clone.1), kind=kCustom, calls=%fused_computation.187 | custom fusion | flops 24576 | bytes 9728 | tf_op jit(solution)/shard_map/scatter-add | solution.py:193
  323.3 23.4 %reduce-scatter.9.cloned.1.call-done = f32[64,9]{1,0:T(8,128)} async-done(((f32[256,9]{1,0:T(8,128)}), f32[64,9]{1,0:T(8,128)}) %reduce-scatter.9.cloned.1.call-update) | async-done | bytes 2320
  349.9 1.8 collective-permute-done.6
  (417 shorter events, 92.3 us)
Async XLA Ops:
  7.2 165.3 %reduce-scatter.7.cloned.1.call-start = ((), (), s32[]{:S(2)}) async-start(), calls=%async_computation.2 | async-start | bytes 163840
  7.9 18.6 %copy-start.58 = (f32[3,64]{1,0:T(4,128)}, f32[3,64]{1,0:T(4,128)S(1)}, u32[]{:S(2)}) copy-start(f32[3,64]{1,0:T(4,128)S(1)} %multiply_add_fusion.2) | copy-start | bytes 2308
  21.6 2.8 collective-permute-start.1
  21.7 4.0 %collective-permute-start = (f32[3,1,256]{2,0,1:T(4,128)S(1)}, f32[3,1,256]{2,0,1:T(4,128)S(1)}, u32[]{:S(2)}, u32[]{:S(2)}) collective-permute-start(f32[3,1,256]{2,0,1:T(4,128)S(1)} %bitcast.482), channel_id=1, source_target_pairs={{0,4},{4,8},{8,12},{12,16},{16,20},{20,24},{24,28},{28,0},{1,5},{5... | collective-permute-start | bytes 9224 | tf_op jit(solution)/shard_map/ppermute | solution.py:23
  26.5 16.3 %copy-start.14 = (f32[3,768]{0,1:T(8,128)}, f32[3,768]{0,1:T(8,128)S(1)}, u32[]{:S(2)}) copy-start(f32[3,768]{0,1:T(8,128)S(1)} %get-tuple-element.963) | copy-start | bytes 27652 | tf_op jit(solution)/shard_map/while
  26.5 16.3 %copy-start.36 = (f32[2,32,128]{2,0,1:T(2,128)}, f32[2,32,128]{2,0,1:T(2,128)S(1)}, u32[]{:S(2)}) copy-start(f32[2,32,128]{2,0,1:T(2,128)S(1)} %get-tuple-element.961) | copy-start | bytes 98308 | tf_op jit(solution)/shard_map/while
  26.5 16.3 %copy-start.40 = (f32[2,32,128]{2,0,1:T(2,128)}, f32[2,32,128]{2,0,1:T(2,128)S(1)}, u32[]{:S(2)}) copy-start(f32[2,32,128]{2,0,1:T(2,128)S(1)} %get-tuple-element.965) | copy-start | bytes 98308 | tf_op jit(solution)/shard_map/while
  26.5 16.3 %copy-start.56 = (f32[2,3,32]{2,1,0:T(4,128)}, f32[2,3,32]{2,1,0:T(4,128)S(1)}, u32[]{:S(2)}) copy-start(f32[2,3,32]{2,1,0:T(4,128)S(1)} %get-tuple-element.964) | copy-start | bytes 2308 | tf_op jit(solution)/shard_map/while
  62.3 16.3 %copy-start.14 = (f32[3,768]{0,1:T(8,128)}, f32[3,768]{0,1:T(8,128)S(1)}, u32[]{:S(2)}) copy-start(f32[3,768]{0,1:T(8,128)S(1)} %get-tuple-element.963) | copy-start | bytes 27652 | tf_op jit(solution)/shard_map/while
  62.3 16.3 %copy-start.36 = (f32[2,32,128]{2,0,1:T(2,128)}, f32[2,32,128]{2,0,1:T(2,128)S(1)}, u32[]{:S(2)}) copy-start(f32[2,32,128]{2,0,1:T(2,128)S(1)} %get-tuple-element.961) | copy-start | bytes 98308 | tf_op jit(solution)/shard_map/while
  62.3 16.3 %copy-start.40 = (f32[2,32,128]{2,0,1:T(2,128)}, f32[2,32,128]{2,0,1:T(2,128)S(1)}, u32[]{:S(2)}) copy-start(f32[2,32,128]{2,0,1:T(2,128)S(1)} %get-tuple-element.965) | copy-start | bytes 98308 | tf_op jit(solution)/shard_map/while
  101.5 72.6 %copy-start.49 = (f32[2,3,32,128]{3,1,2,0:T(4,128)S(1)}, f32[2,3,32,128]{3,1,2,0:T(4,128)}, u32[]{:S(2)}) copy-start(f32[2,3,32,128]{3,1,2,0:T(4,128)} %get-tuple-element.460) | copy-start | bytes 294916
  101.5 76.0 %copy-start.59 = (f32[3,64]{1,0:T(4,128)S(1)}, f32[3,64]{1,0:T(4,128)}, u32[]{:S(2)}) copy-start(f32[3,64]{1,0:T(4,128)} %copy-done.58) | copy-start | bytes 2308
  101.5 76.0 %copy-start.62 = (f32[3,64]{1,0:T(4,128)S(1)}, f32[3,64]{1,0:T(4,128)}, u32[]{:S(2)}) copy-start(f32[3,64]{1,0:T(4,128)} %param.22) | copy-start | bytes 2308
  101.5 76.0 %copy-start.63 = (f32[3,64]{1,0:T(4,128)S(1)}, f32[3,64]{1,0:T(4,128)}, u32[]{:S(2)}) copy-start(f32[3,64]{1,0:T(4,128)} %param.23) | copy-start | bytes 2308
  101.5 94.4 %copy-start.1 = (bf16[2048,240]{0,1:T(8,128)(2,1)S(1)}, bf16[2048,240]{0,1:T(8,128)(2,1)}, u32[]{:S(2)}) copy-start(bf16[2048,240]{0,1:T(8,128)(2,1)} %get-tuple-element.1043) | copy-start | bytes 2949124
  101.5 94.4 %copy-start.8 = (bf16[240,240]{1,0:T(8,128)(2,1)S(1)}, bf16[240,240]{1,0:T(8,128)(2,1)}, u32[]{:S(2)}) copy-start(bf16[240,240]{1,0:T(8,128)(2,1)} %get-tuple-element.1044) | copy-start | bytes 345604
  101.5 94.4 %copy-start.35 = (bf16[32,64]{1,0:T(8,128)(2,1)S(1)}, bf16[32,64]{1,0:T(8,128)(2,1)}, u32[]{:S(2)}) copy-start(bf16[32,64]{1,0:T(8,128)(2,1)} %get-tuple-element.1045) | copy-start | bytes 12292
  147.9 198.8 %reduce-scatter.9.cloned.1.call-start = ((), (), s32[]{:S(2)}) async-start(), calls=%async_computation.3 | async-start | bytes 163840
  173.5 1.3 collective-permute-start.3
  173.6 3.9 %collective-permute-start.2 = (f32[3,1,64]{2,0,1:T(4,128)S(1)}, f32[3,1,64]{2,0,1:T(4,128)S(1)}, u32[]{:S(2)}, u32[]{:S(2)}) collective-permute-start(f32[3,1,64]{2,0,1:T(4,128)S(1)} %copy.169), channel_id=1, source_target_pairs={{0,4},{4,8},{8,12},{12,16},{16,20},{20,24},{24,28},{28,0},{1,5},{5... | collective-permute-start | bytes 2312 | tf_op jit(solution)/shard_map/ppermute | solution.py:23
  178.1 17.8 %copy-start.60 = (f32[3,64]{1,0:T(4,128)}, f32[3,64]{1,0:T(4,128)S(1)}, u32[]{:S(2)}) copy-start(f32[3,64]{1,0:T(4,128)S(1)} %get-tuple-element.650) | copy-start | bytes 2308
  190.1 1.3 collective-permute-start.5
  190.1 4.2 %collective-permute-start.4 = (f32[3,1,256]{2,0,1:T(4,128)S(1)}, f32[3,1,256]{2,0,1:T(4,128)S(1)}, u32[]{:S(2)}, u32[]{:S(2)}) collective-permute-start(f32[3,1,256]{2,0,1:T(4,128)S(1)} %bitcast.485), channel_id=1, source_target_pairs={{0,4},{4,8},{8,12},{12,16},{16,20},{20,24},{24,28},{28,0},{1,5},{5... | collective-permute-start | bytes 9224 | tf_op jit(solution)/shard_map/ppermute | solution.py:23
  196.0 17.2 %copy-start.38 = (f32[2,32,128]{2,0,1:T(2,128)}, f32[2,32,128]{2,0,1:T(2,128)S(1)}, u32[]{:S(2)}) copy-start(f32[2,32,128]{2,0,1:T(2,128)S(1)} %get-tuple-element.1023) | copy-start | bytes 98308 | tf_op jit(solution)/shard_map/while
  196.0 17.2 %copy-start.42 = (f32[2,32,128]{2,0,1:T(2,128)}, f32[2,32,128]{2,0,1:T(2,128)S(1)}, u32[]{:S(2)}) copy-start(f32[2,32,128]{2,0,1:T(2,128)S(1)} %get-tuple-element.1027) | copy-start | bytes 98308 | tf_op jit(solution)/shard_map/while
  234.8 17.2 %copy-start.38 = (f32[2,32,128]{2,0,1:T(2,128)}, f32[2,32,128]{2,0,1:T(2,128)S(1)}, u32[]{:S(2)}) copy-start(f32[2,32,128]{2,0,1:T(2,128)S(1)} %get-tuple-element.1023) | copy-start | bytes 98308 | tf_op jit(solution)/shard_map/while
  234.8 17.2 %copy-start.42 = (f32[2,32,128]{2,0,1:T(2,128)}, f32[2,32,128]{2,0,1:T(2,128)S(1)}, u32[]{:S(2)}) copy-start(f32[2,32,128]{2,0,1:T(2,128)S(1)} %get-tuple-element.1027) | copy-start | bytes 98308 | tf_op jit(solution)/shard_map/while
  277.0 71.3 %copy-start.46 = (f32[2,3,32,128]{3,1,2,0:T(4,128)S(1)}, f32[2,3,32,128]{3,1,2,0:T(4,128)}, u32[]{:S(2)}) copy-start(f32[2,3,32,128]{3,1,2,0:T(4,128)} %get-tuple-element.461) | copy-start | bytes 294916
  277.0 74.7 %copy-start.61 = (f32[3,64]{1,0:T(4,128)S(1)}, f32[3,64]{1,0:T(4,128)}, u32[]{:S(2)}) copy-start(f32[3,64]{1,0:T(4,128)} %get-tuple-element.651) | copy-start | bytes 2308
  347.8 2.2 collective-permute-start.7
  347.9 3.9 %collective-permute-start.6 = (f32[3,1,64]{2,0,1:T(4,128)S(1)}, f32[3,1,64]{2,0,1:T(4,128)S(1)}, u32[]{:S(2)}, u32[]{:S(2)}) collective-permute-start(f32[3,1,64]{2,0,1:T(4,128)S(1)} %copy.172), channel_id=1, source_target_pairs={{0,4},{4,8},{8,12},{12,16},{16,20},{20,24},{24,28},{28,0},{1,5},{5... | collective-permute-start | bytes 2312 | tf_op jit(solution)/shard_map/ppermute | solution.py:23
  (95 other events, 311.7 us)
Sparse Core Ops, SparseCore 0:
  148.0 24.4 reduce-scatter.6
  323.4 23.2 reduce-scatter.8
where the time goes:
time: 362 us; the launch traced here: 359 us
  other arithmetic  107 us (30%)
  local copies, waits for them, and re-layouts  87 us (24%)
  matrix products  64.1 us (18%)
  waiting for transfers between devices  57.7 us (16%)
  blocking collectives  25.5 us (7%)
  between operations  14.2 us (4%)
    scatter-add x2, other arithmetic, evaluate(): jnp.zeros((3, 3 * brick_len), jnp.float32).at[:, safe_index].add(pair_grads)  90.2 us
    unnamed x4, waiting for transfers between devices  48 us
    gather x8, local copies, waits for them, and re-layouts, one_block(): neighbour_pos = jnp.take(ghost, table_index, axis=1)  47.5 us
    all_gather x2, blocking collectives, ghost_table(): brick_pos = lax.all_gather(stacked, 'help', axis=2, tiled=True)  25.5 us
    while x212, local copies, waits for them, and re-layouts  8.73 us
    ppermute x4, waiting for transfers between devices, extended(): before = lax.ppermute(last, axis, up)  8.48 us
    dot_general x4, matrix products, pair_terms(): jnp.dot(w_embed2.T, hidden_first.astype(jnp.bfloat16), preferred_element_...  8.38 us
    dot_general x4, matrix products, pair_terms(): jnp.dot(grad_act, w_fit1.T, preferred_element_type=jnp.float32)  7.82 us
  transfers between devices with their start and end apart: 10, of which 8 were waited for; matrix products, arithmetic and copies ran while one was open for 1% of the time, Pallas kernels for 0%

commit v1 on v0

v1 whole, which is shorter than its diff:
```python
import functools

import jax
import jax.numpy as jnp
from jax import lax
from jax.experimental import pallas as pl
from jax.experimental.pallas import tpu as pltpu
from jax.sharding import PartitionSpec as P

STEPS = 2

kick_scale = 0.25
time_step = 0.05
LANES = 128
f32 = jnp.float32
bf16 = jnp.bfloat16
NN = (((1,), (0,)), ((), ()))
NT = (((1,), (1,)), ((), ()))
TN = (((0,), (0,)), ((), ()))


def mm(a, b, dims=NN):
    return lax.dot_general(a, b, dims, preferred_element_type=f32)


def split2(x):
    high = x.astype(bf16).astype(f32)
    return high, x - high


def eval_kernel(
    rank_ref,
    before_ref,
    brick_ref,
    after_ref,
    own_ref,
    nbr_ref,
    w1_ref,
    b1_ref,
    w2t_ref,
    w2_ref,
    b2_ref,
    w3t_ref,
    w3_ref,
    b3_ref,
    f1_ref,
    c1_ref,
    f2_ref,
    c2_ref,
    out_ref,
    energy_ref,
    to_before_ref,
    to_brick_ref,
    to_after_ref,
    s_s,
    r_s,
    t_s,
    d_s,
    h1_s,
    u2_s,
    u3_s,
    g_s,
    z_s,
    dr_s,
    hi_s,
    lo_s,
    gr_s,
    des_s,
):
    atoms, slots = nbr_ref.shape
    brick_len = brick_ref.shape[1]
    per = brick_len // LANES
    e1 = w1_ref.shape[0]
    e2 = w2_ref.shape[1]
    e3 = w3_ref.shape[1]
    m2 = f1_ref.shape[0] // e3
    inv_slots = 1.0 / slots
    pairs = atoms // 2

    nbr = nbr_ref[...]
    live = nbr >= 0
    mask = jnp.where(live, 1.0, 0.0).astype(f32)
    index = jnp.maximum(nbr, 0)
    low = index & (LANES - 1)
    high = lax.shift_right_logical(index, 7)
    sub = lax.broadcasted_iota(jnp.int32, (atoms, slots), 0)
    coords = [jnp.zeros((atoms, slots), f32)] * 3
    for part, table in enumerate((before_ref, brick_ref, after_ref)):
        for chunk in range(per):
            hit = high == part * per + chunk
            for c in range(3):
                row = table[c : c + 1, chunk * LANES : (chunk + 1) * LANES]
                found = jnp.take_along_axis(
                    jnp.broadcast_to(row, (atoms, LANES)), low, axis=1, mode="promise_in_bounds"
                )
                coords[c] = jnp.where(hit, found, coords[c])
    shift = (
        jnp.where(high >= per, 1.0, 0.0) + jnp.where(high >= 2 * per, 1.0, 0.0) - 1.0
    ).astype(f32)
    disp = []
    for c in range(3):
        row = own_ref[c : c + 1, :]
        mine = jnp.take_along_axis(
            jnp.broadcast_to(row, (atoms, LANES)), sub, axis=1, mode="promise_in_bounds"
        )
        delta = coords[c] - mine
        if c == 0:
            delta = delta + shift
        disp.append(delta * mask)
    quad = disp[0] * disp[0] + disp[1] * disp[1] + disp[2] * disp[2] + 0.25
    radius = jnp.sqrt(quad)
    smooth = mask / radius
    inv_quad = 1.0 / quad
    s_s[...] = smooth
    r_s[pl.ds(0, atoms, stride=4), :] = smooth
    for c in range(3):
        r_s[pl.ds(c + 1, atoms, stride=4), :] = disp[c] * inv_quad
    hi_s[...] = high
    lo_s[...] = low

    w1 = jnp.broadcast_to(w1_ref[...], (e1, LANES))
    b1 = jnp.broadcast_to(b1_ref[...], (e1, LANES))
    w1 = jnp.concatenate([w1, w1], axis=1)
    b1 = jnp.concatenate([b1, b1], axis=1)
    row8 = lax.broadcasted_iota(jnp.int32, (8, LANES), 0)

    def both(value):
        left = jnp.where(row8 < 4, value, 0.0)
        right = jnp.where(row8 >= 4, value, 0.0)
        return jnp.concatenate([left, right], axis=1)

    def forward(p, carry):
        base = pl.multiple_of(p * 8, 8)
        s_row = jnp.concatenate(
            [
                jnp.broadcast_to(s_s[pl.ds(2 * p, 1), :], (e1, LANES)),
                jnp.broadcast_to(s_s[pl.ds(2 * p + 1, 1), :], (e1, LANES)),
            ],
            axis=1,
        )
        h1 = jnp.tanh(w1 * s_row + b1)
        t2 = jnp.tanh(mm(w2t_ref[...], h1.astype(bf16)) + b2_ref[...])
        h2 = jnp.concatenate([h1, h1], axis=0) + t2
        t3 = jnp.tanh(mm(w3t_ref[...], h2.astype(bf16)) + b3_ref[...])
        g = (jnp.concatenate([h2, h2], axis=0) + t3).astype(bf16)
        h1_s[p] = h1
        u2_s[p] = 1.0 - t2 * t2
        u3_s[p] = 1.0 - t3 * t3
        g_s[p] = g
        r2 = both(r_s[pl.ds(base, 8), :]).astype(bf16)
        t_s[pl.ds(base, 8), :] = mm(r2, g, NT) * inv_slots
        return carry

    lax.fori_loop(0, pairs, forward, 0)

    tens = [t_s[pl.ds(c, atoms, stride=4), :] for c in range(4)]
    for k in range(m2):
        total = tens[0] * jnp.broadcast_to(tens[0][:, k : k + 1], (atoms, e3))
        for c in range(1, 4):
            total = total + tens[c] * jnp.broadcast_to(tens[c][:, k : k + 1], (atoms, e3))
        des_s[:, k * e3 : (k + 1) * e3] = total.astype(bf16)
    wide = out_ref[...]
    y1 = jnp.tanh(mm(des_s[...], f1_ref[...]) + c1_ref[...])
    t4 = jnp.tanh(mm(y1.astype(bf16), f2_ref[...]) + c2_ref[...])
    energy_ref[...] = lax.dot_general(
        wide, y1 + t4, NT, precision=lax.Precision.HIGHEST, preferred_element_type=f32
    )
    dz2 = (wide * (1.0 - t4 * t4)).astype(bf16)
    dy1 = wide + mm(dz2, f2_ref[...], NT)
    dz1 = (dy1 * (1.0 - y1 * y1)).astype(bf16)
    lane = lax.broadcasted_iota(jnp.int32, (atoms, e3), 1)
    grads = [jnp.zeros((atoms, e3), f32)] * 4
    for k in range(m2):
        dd = mm(dz1, f1_ref[k * e3 : (k + 1) * e3, :], NT)
        for c in range(4):
            other = jnp.sum(dd * tens[c], axis=1, keepdims=True)
            grads[c] = (
                grads[c]
                + dd * jnp.broadcast_to(tens[c][:, k : k + 1], (atoms, e3))
                + jnp.where(lane == k, other, 0.0)
            )
    for c in range(4):
        d_s[pl.ds(c, atoms, stride=4), :] = grads[c].astype(bf16).astype(f32) * inv_slots

    def backward(p, carry):
        base = pl.multiple_of(p * 8, 8)
        dt = d_s[pl.ds(base, 8), :].astype(bf16)
        r2 = both(r_s[pl.ds(base, 8), :]).astype(bf16)
        dr = mm(dt, g_s[p])
        dr_s[pl.ds(base, 8), :] = jnp.where(row8 < 4, dr[:, :LANES], dr[:, LANES:])
        dg = mm(dt, r2, TN)
        da3 = (dg * u3_s[p]).astype(bf16)
        dh2 = dg[: e3 // 2] + dg[e3 // 2 :] + mm(w3_ref[...], da3)
        da2 = (dh2 * u2_s[p]).astype(bf16)
        dh1 = dh2[: e2 // 2] + dh2[e2 // 2 :] + mm(w2_ref[...], da2)
        h1 = h1_s[p]
        part = dh1 * (1.0 - h1 * h1) * w1
        z = part[0:8]
        for i in range(1, e1 // 8):
            z = z + part[8 * i : 8 * i + 8]
        wide_base = pl.multiple_of(p * 16, 16)
        z_s[pl.ds(wide_base, 8), :] = z[:, :LANES]
        z_s[pl.ds(wide_base + 8, 8), :] = z[:, LANES:]
        return carry

    lax.fori_loop(0, pairs, backward, 0)

    ds = dr_s[pl.ds(0, atoms, stride=4), :]
    for i in range(8):
        ds = ds + z_s[pl.ds(i, atoms, stride=8), :]
    drs = [dr_s[pl.ds(c + 1, atoms, stride=4), :] for c in range(3)]
    radial = drs[0] * disp[0] + drs[1] * disp[1] + drs[2] * disp[2]
    factor = -ds / (radius * quad) - 2.0 * radial * (inv_quad * inv_quad)
    ones = jnp.ones((8, LANES), bf16)
    zero = jnp.zeros((atoms, LANES), f32)
    sums = []
    for c in range(3):
        pull = mask * (disp[c] * factor + drs[c] * inv_quad)
        upper, lower = split2(pull)
        gr_s[pl.ds(c, atoms, stride=8), :] = upper
        gr_s[pl.ds(c + 3, atoms, stride=8), :] = lower
        both_parts = mm(ones, upper.astype(bf16), NT) + mm(ones, lower.astype(bf16), NT)
        sums.append(both_parts[0:1])
    gr_s[pl.ds(6, atoms, stride=8), :] = zero
    gr_s[pl.ds(7, atoms, stride=8), :] = zero
    mine = jnp.concatenate(sums, axis=0)

    place = lax.broadcasted_iota(jnp.int32, (LANES, LANES), 0)
    chunks = 3 * per

    def scatter(p, total):
        rows = []
        hots = []
        for i in range(2):
            atom = 2 * p + i
            values = gr_s[pl.ds(pl.multiple_of(atom * 8, 8), 8), :]
            upper = jnp.broadcast_to(hi_s[pl.ds(atom, 1), :], (8, LANES))
            lower = jnp.broadcast_to(lo_s[pl.ds(atom, 1), :], (LANES, LANES))
            rows.append(
                jnp.concatenate(
                    [jnp.where(upper == a, values, 0.0) for a in range(chunks)], axis=0
                )
            )
            hots.append(jnp.where(lower == place, 1.0, 0.0).astype(bf16))
        lhs = jnp.concatenate(rows, axis=1).astype(bf16)
        return total + mm(lhs, jnp.concatenate(hots, axis=1), NT)

    total = lax.fori_loop(0, pairs, scatter, jnp.zeros((8 * chunks, LANES), f32))
    rank = rank_ref[0]
    spot = lax.broadcasted_iota(jnp.int32, (3, brick_len), 1) // atoms
    placed = jnp.where(
        spot == rank, jnp.concatenate([mine] * (brick_len // atoms), axis=1), 0.0
    )
    for part, target in enumerate((to_before_ref, to_brick_ref, to_after_ref)):
        pieces = []
        for chunk in range(per):
            at = 8 * (part * per + chunk)
            pieces.append(total[at : at + 3] + total[at + 3 : at + 6])
        whole = -jnp.concatenate(pieces, axis=1)
        target[...] = whole + placed if part == 1 else whole


def prepare(weights, lanes):
    w1, b1, w2, b2, w3, b3, f1, c1, f2, c2, out = weights
    e3 = w3.shape[1]
    fit = out.shape[0]
    pad = -fit % LANES
    m2 = f1.shape[0] // e3
    f1 = jnp.pad(f1.reshape(e3, m2, fit).transpose(1, 0, 2), ((0, 0), (0, 0), (0, pad)))
    return (
        w1[:, None],
        b1[:, None],
        w2.T,
        w2,
        b2[:, None],
        w3.T,
        w3,
        b3[:, None],
        f1.reshape(m2 * e3, fit + pad),
        jnp.pad(c1, (0, pad))[None],
        jnp.pad(f2, ((0, pad), (0, pad))),
        jnp.pad(c2, (0, pad))[None],
        jnp.pad(out, (0, pad))[None],
    )


def evaluate(rank, before, brick, after, own, neighbors, prepared):
    atoms, slots = neighbors.shape
    brick_len = brick.shape[1]
    e1 = prepared[0].shape[0]
    e2 = prepared[3].shape[1]
    e3 = prepared[6].shape[1]
    pairs = atoms // 2
    wide = 2 * slots
    own = jnp.concatenate([own, own], axis=1)[:, :LANES]
    vmem = pl.BlockSpec(memory_space=pltpu.VMEM)
    piece = jax.ShapeDtypeStruct((3, brick_len), f32)
    return pl.pallas_call(
        eval_kernel,
        out_shape=(jax.ShapeDtypeStruct((1, atoms), f32), piece, piece, piece),
        in_specs=[pl.BlockSpec(memory_space=pltpu.SMEM)] + [vmem] * (5 + len(prepared)),
        out_specs=[vmem] * 4,
        scratch_shapes=[
            pltpu.VMEM((atoms, slots), f32),
            pltpu.VMEM((4 * atoms, slots), f32),
            pltpu.VMEM((4 * atoms, e3), f32),
            pltpu.VMEM((4 * atoms, e3), f32),
            pltpu.VMEM((pairs, e1, wide), f32),
            pltpu.VMEM((pairs, e2, wide), f32),
            pltpu.VMEM((pairs, e3, wide), f32),
            pltpu.VMEM((pairs, e3, wide), bf16),
            pltpu.VMEM((8 * atoms, slots), f32),
            pltpu.VMEM((4 * atoms, slots), f32),
            pltpu.VMEM((atoms, slots), jnp.int32),
            pltpu.VMEM((atoms, slots), jnp.int32),
            pltpu.VMEM((8 * atoms, slots), f32),
            pltpu.VMEM((atoms, prepared[8].shape[0]), bf16),
        ],
        compiler_params=pltpu.CompilerParams(vmem_limit_bytes=40 * 1024 * 1024),
        name="evaluate",
    )(rank, before, brick, after, own, neighbors, *prepared)


def ring(size, step):
    return [(i, (i + step) % size) for i in range(size)]


def flip(size, bit):
    return [(i, i ^ bit) for i in range(size)]


def gather_help(value):
    size = lax.axis_size("help")
    rank = lax.axis_index("help")
    if size & (size - 1):
        return lax.all_gather(value, "help", axis=1, tiled=True)
    bit = 1
    while bit < size:
        other = lax.ppermute(value, "help", flip(size, bit))
        upper = (rank & bit) != 0
        value = jnp.where(
            upper,
            jnp.concatenate([other, value], axis=1),
            jnp.concatenate([value, other], axis=1),
        )
        bit *= 2
    return value


def sum_help(value):
    size = lax.axis_size("help")
    if size & (size - 1):
        return lax.psum(value, "help")
    bit = 1
    while bit < size:
        value = value + lax.ppermute(value, "help", flip(size, bit))
        bit *= 2
    return value


def exchange(up, down):
    size = lax.axis_size("brick")
    return lax.ppermute(up, "brick", ring(size, 1)), lax.ppermute(down, "brick", ring(size, -1))


def local(positions, velocities, forces_in, neighbors, *weights):
    prepared = prepare(weights, LANES)
    atoms = positions.shape[1]
    rank = lax.axis_index("help")
    ranks = rank.reshape(1).astype(jnp.int32)
    at = rank * atoms
    speed = velocities + kick_scale * forces_in
    coords = positions + time_step * speed
    state = gather_help(jnp.concatenate([coords, speed], axis=0))
    brick_pos, brick_speed = state[:3], state[3:]
    own = coords
    for md_step in range(STEPS):
        before, after = exchange(brick_pos, brick_pos)
        energy, to_before, to_brick, to_after = evaluate(
            ranks, before, brick_pos, after, own, neighbors, prepared
        )
        from_before, from_after = exchange(to_after, to_before)
        force = sum_help(to_brick + from_before + from_after)
        brick_speed = brick_speed + kick_scale * force
        if md_step + 1 < STEPS:
            brick_speed = brick_speed + kick_scale * force
            brick_pos = brick_pos + time_step * brick_speed
            own = lax.dynamic_slice_in_dim(brick_pos, at, atoms, axis=1)
    out = lax.dynamic_slice_in_dim(
        jnp.concatenate([brick_speed, force], axis=0), at, atoms, axis=1
    )
    return (own, out[:3], energy.reshape(atoms), out[3:])


def solution(mesh):
    spread = ("brick", "help")
    cols = P(None, spread)
    return jax.shard_map(
        local,
        mesh=mesh,
        in_specs=(cols, cols, cols, P(spread, None)) + (P(),) * 11,
        out_specs=(cols, cols, P(spread), cols),
        check_vma=False,
    )
```

time: 362 us -> 125 us (0.35)
  other arithmetic: 107 us -> 1.07 us
  local copies, waits for them, and re-layouts: 87 us -> 8.44 us
  Pallas kernels: 0 us -> 74 us
  matrix products: 64.1 us -> 0 us
  waiting for transfers between devices: 57.7 us -> 13.6 us
  blocking collectives: 25.5 us -> 0 us
  starting transfers between devices: 2.13 us -> 26.4 us
  between operations: 14.2 us -> 0.75 us
    scatter-add x2 -> x0, other arithmetic: 90.2 us -> none  [evaluate(): jnp.zeros((3, 3 * brick_len), jnp.float32).at[:, safe_index].add(pair_grads)]
    pallas_call x0 -> x2, Pallas kernels: none -> 74 us  [evaluate(): pl.pallas_call(eval_kernel, out_shape=(jax.ShapeDtypeStruct((1, atoms), f...]
    dot_general x58 -> x0, matrix products: 64.1 us -> none  [the longest x4 8.38 us: pair_terms(): jnp.dot(w_embed2.T, hidden_first.astype(jnp.bfloat16), preferred_element_...]
    unnamed x4 -> x0, waiting for transfers between devices: 48 us -> none
    gather x8 -> x0, local copies, waits for them, and re-layouts: 47.5 us -> none  [one_block(): neighbour_pos = jnp.take(ghost, table_index, axis=1)]
    all_gather x2 -> x0, blocking collectives: 25.5 us -> none  [ghost_table(): brick_pos = lax.all_gather(stacked, 'help', axis=2, tiled=True)]
    ppermute x8 -> x14, starting transfers between devices: 2.06 us -> 26.4 us  [the longest x4 10.6 us: exchange(): lax.ppermute(down, 'brick', ring(size, -1))]
    reshape x11 -> x0, local copies, waits for them, and re-layouts: 15.3 us -> none  [the longest x2 7 us: evaluate(): pair_grads = pair_grads.transpose(1, 0, 2, 3).reshape(3, atom_count, -1)]
  transfers between devices with their start and end apart: 10 -> 14, of which waited for: 8 -> 9; matrix products, arithmetic and copies ran while one was open for 1% -> 2% of each run, Pallas kernels for 0% -> 0%
where the time goes in v1:
time: 125 us; the launch traced here: 124 us
  Pallas kernels  74 us (59%)
  starting transfers between devices  26.4 us (21%)
  waiting for transfers between devices  13.6 us (11%)
  local copies, waits for them, and re-layouts  8.44 us (7%)
    pallas_call x2, Pallas kernels, evaluate(): pl.pallas_call(eval_kernel, out_shape=(jax.ShapeDtypeStruct((1, atoms), f...  74 us
    ppermute x4, starting transfers between devices, exchange(): lax.ppermute(down, 'brick', ring(size, -1))  10.6 us
    ppermute x4, starting transfers between devices, sum_help(): value = value + lax.ppermute(value, 'help', flip(size, bit))  9.65 us
    unnamed x28, local copies, waits for them, and re-layouts  7.18 us
    ppermute x4, waiting for transfers between devices, sum_help(): value = value + lax.ppermute(value, 'help', flip(size, bit))  6.57 us
    ppermute x2, starting transfers between devices, gather_help(): other = lax.ppermute(value, 'help', flip(size, bit))  6.15 us
    ppermute x4, waiting for transfers between devices, exchange(): lax.ppermute(up, 'brick', ring(size, 1))  3.71 us
    ppermute x2, waiting for transfers between devices, gather_help(): other = lax.ppermute(value, 'help', flip(size, bit))  3.17 us
  transfers between devices with their start and end apart: 14, of which 9 were waited for; matrix products, arithmetic and copies ran while one was open for 2% of the time, Pallas kernels for 0%

profile of v1, /device:TPU:0, one launch (start us, length us, event | category | flops | bytes accessed | tf_op | source)
XLA Modules:
  0.0 124.2 jit_solution(1316901289851635743)
XLA Ops:
  0.6 0.7 multiply_add_fusion.2
  1.4 3.1 %collective-permute-start = (f32[6,64]{1,0:T(8,128)S(1)}, f32[6,64]{1,0:T(8,128)S(1)}, u32[]{:S(2)}, u32[]{:S(2)}) collective-permute-start(f32[6,64]{1,0:T(8,128)S(1)} %pad_maximum_fusion), channel_id=1, source_target_pairs={{0,1},{1,0},{2,3},{3,2},{4,5},{5,4},{6,7},{7,6},{8,9},{9,8},{10,11... | collective-permute-start | bytes 4616 | tf_op jit(solution)/shard_map/ppermute | solution.py:339
  4.5 1.6 %collective-permute-done = f32[6,64]{1,0:T(8,128)S(1)} collective-permute-done((f32[6,64]{1,0:T(8,128)S(1)}, f32[6,64]{1,0:T(8,128)S(1)}, u32[]{:S(2)}, u32[]{:S(2)}) %collective-permute-start) | collective-permute-done | bytes 1568 | tf_op jit(solution)/shard_map/ppermute | solution.py:339
  6.1 3.0 %collective-permute-start.1 = (f32[6,128]{1,0:T(8,128)S(1)}, f32[6,128]{1,0:T(8,128)S(1)}, u32[]{:S(2)}, u32[]{:S(2)}) collective-permute-start(f32[6,128]{1,0:T(8,128)S(1)} %maximum_select_fusion.1), channel_id=1, source_target_pairs={{0,2},{1,3},{2,0},{3,1},{4,6},{5,7},{6,4},{7,5},{8,10},{9,11},{10,... | collective-permute-start | bytes 9224 | tf_op jit(solution)/shard_map/ppermute | solution.py:339
  9.2 1.6 %collective-permute-done.1 = f32[6,128]{1,0:T(8,128)S(1)} collective-permute-done((f32[6,128]{1,0:T(8,128)S(1)}, f32[6,128]{1,0:T(8,128)S(1)}, u32[]{:S(2)}, u32[]{:S(2)}) %collective-permute-start.1) | collective-permute-done | bytes 3104 | tf_op jit(solution)/shard_map/ppermute | solution.py:339
  10.8 2.6 %collective-permute-start.3 = (f32[3,256]{1,0:T(4,128)S(1)}, f32[3,256]{1,0:T(4,128)S(1)}, u32[]{:S(2)}, u32[]{:S(2)}) collective-permute-start(f32[3,256]{1,0:T(4,128)S(1)} %slice.16.brick_ref), channel_id=1, source_target_pairs={{0,28},{4,0},{8,4},{12,8},{16,12},{20,16},{24,20},{28,24},{1,29},{... | collective-permute-start | bytes 9224 | tf_op jit(solution)/shard_map/ppermute | solution.py:363
  13.5 1.5 %copy.32 = bf16[2048,240]{1,0:T(8,128)(2,1)S(1)} copy(bf16[2048,240]{0,1:T(8,128)(2,1)} %param.25) | data formatting | bytes 1966080 | tf_op args[10]
  15.5 0.7 copy-done.3
  16.3 0.6 copy-done.8
  17.0 0.6 copy-done
  17.7 0.7 copy-done.9
  18.5 0.6 copy-done.2
  19.4 0.6 copy-done.5
  20.0 0.7 copy-done.6
  20.7 0.7 copy-done.7
  21.4 37.0 %evaluate.2 = (f32[1,64]{1,0:T(1,128)}, f32[3,256]{1,0:T(4,128)S(1)}, f32[3,256]{1,0:T(4,128)S(1)}, f32[3,256]{1,0:T(4,128)S(1)}) custom-call(s32[1]{0:T(128)} %bitcast.rank_ref, f32[3,256]{1,0:T(4,128)S(1)} %collective-permute-done.2.before_ref, f32[3,256]{1,0:T(4,128)S(1)} %slice.16.brick_ref, f32[3,256]{1,0:T(4,128)S(1)} %collective-permute-done.3.after_ref, ...), custom_call_target="tpu_custom_call" | custom-call | tf_op jit(solution)/shard_map/evaluate/pallas_call | solution.py:298
  58.4 2.6 %collective-permute-start.5 = (f32[3,256]{1,0:T(4,128)S(1)}, f32[3,256]{1,0:T(4,128)S(1)}, u32[]{:S(2)}, u32[]{:S(2)}) collective-permute-start(f32[3,256]{1,0:T(4,128)S(1)} %get-tuple-element.13), channel_id=1, source_target_pairs={{0,28},{4,0},{8,4},{12,8},{16,12},{20,16},{24,20},{28,24},{1,29},{... | collective-permute-start | bytes 9224 | tf_op jit(solution)/shard_map/ppermute | solution.py:363
  61.0 1.3 %collective-permute-done.4 = f32[3,256]{1,0:T(4,128)S(1)} collective-permute-done((f32[3,256]{1,0:T(4,128)S(1)}, f32[3,256]{1,0:T(4,128)S(1)}, u32[]{:S(2)}, u32[]{:S(2)}) %collective-permute-start.4) | collective-permute-done | bytes 3104 | tf_op jit(solution)/shard_map/ppermute | solution.py:363
  62.3 1.9 %collective-permute-start.6 = (f32[3,256]{1,0:T(4,128)S(1)}, f32[3,256]{1,0:T(4,128)S(1)}, u32[]{:S(2)}, u32[]{:S(2)}) collective-permute-start(f32[3,256]{1,0:T(4,128)S(1)} %add_add_fusion.2), channel_id=1, source_target_pairs={{0,1},{1,0},{2,3},{3,2},{4,5},{5,4},{6,7},{7,6},{8,9},{9,8},{10,11... | collective-permute-start | bytes 9224 | tf_op jit(solution)/shard_map/ppermute | solution.py:356
  64.2 1.7 %collective-permute-done.6 = f32[3,256]{1,0:T(4,128)S(1)} collective-permute-done((f32[3,256]{1,0:T(4,128)S(1)}, f32[3,256]{1,0:T(4,128)S(1)}, u32[]{:S(2)}, u32[]{:S(2)}) %collective-permute-start.6) | collective-permute-done | bytes 3104 | tf_op jit(solution)/shard_map/ppermute | solution.py:356
  65.9 2.9 %collective-permute-start.7 = (f32[3,256]{1,0:T(4,128)S(1)}, f32[3,256]{1,0:T(4,128)S(1)}, u32[]{:S(2)}, u32[]{:S(2)}) collective-permute-start(f32[3,256]{1,0:T(4,128)S(1)} %add.60), channel_id=1, source_target_pairs={{0,2},{1,3},{2,0},{3,1},{4,6},{5,7},{6,4},{7,5},{8,10},{9,11},{10,... | collective-permute-start | bytes 9224 | tf_op jit(solution)/shard_map/ppermute | solution.py:356
  68.9 1.6 %collective-permute-done.7 = f32[3,256]{1,0:T(4,128)S(1)} collective-permute-done((f32[3,256]{1,0:T(4,128)S(1)}, f32[3,256]{1,0:T(4,128)S(1)}, u32[]{:S(2)}, u32[]{:S(2)}) %collective-permute-start.7) | collective-permute-done | bytes 3104 | tf_op jit(solution)/shard_map/ppermute | solution.py:356
  70.5 2.6 %collective-permute-start.9 = (f32[3,256]{1,0:T(4,128)S(1)}, f32[3,256]{1,0:T(4,128)S(1)}, u32[]{:S(2)}, u32[]{:S(2)}) collective-permute-start(f32[3,256]{1,0:T(4,128)S(1)} %multiply_add_fusion.1.brick_ref), channel_id=1, source_target_pairs={{0,28},{4,0},{8,4},{12,8},{16,12},{20,16},{24,20},{28,24},{1,29},{... | collective-permute-start | bytes 9224 | tf_op jit(solution)/shard_map/ppermute | solution.py:363
  73.3 1.1 collective-permute-done.8.before_ref
  74.4 37.0 %evaluate.3 = (f32[1,64]{1,0:T(1,128)}, f32[3,256]{1,0:T(4,128)S(1)}, f32[3,256]{1,0:T(4,128)S(1)}, f32[3,256]{1,0:T(4,128)S(1)}) custom-call(s32[1]{0:T(128)} %bitcast.rank_ref, f32[3,256]{1,0:T(4,128)S(1)} %collective-permute-done.8.before_ref, f32[3,256]{1,0:T(4,128)S(1)} %multiply_add_fusion.1.brick_ref, f32[3,256]{1,0:T(4,128)S(1)} %collective-permute-done.9.after_ref, ...), custom_call_target="tpu_custom_call" | custom-call | tf_op jit(solution)/shard_map/evaluate/pallas_call | solution.py:298
  111.4 2.6 %collective-permute-start.11 = (f32[3,256]{1,0:T(4,128)S(1)}, f32[3,256]{1,0:T(4,128)S(1)}, u32[]{:S(2)}, u32[]{:S(2)}) collective-permute-start(f32[3,256]{1,0:T(4,128)S(1)} %get-tuple-element.16), channel_id=1, source_target_pairs={{0,28},{4,0},{8,4},{12,8},{16,12},{20,16},{24,20},{28,24},{1,29},{... | collective-permute-start | bytes 9224 | tf_op jit(solution)/shard_map/ppermute | solution.py:363
  114.1 1.3 %collective-permute-done.10 = f32[3,256]{1,0:T(4,128)S(1)} collective-permute-done((f32[3,256]{1,0:T(4,128)S(1)}, f32[3,256]{1,0:T(4,128)S(1)}, u32[]{:S(2)}, u32[]{:S(2)}) %collective-permute-start.10) | collective-permute-done | bytes 3104 | tf_op jit(solution)/shard_map/ppermute | solution.py:363
  115.4 1.9 %collective-permute-start.12 = (f32[3,256]{1,0:T(4,128)S(1)}, f32[3,256]{1,0:T(4,128)S(1)}, u32[]{:S(2)}, u32[]{:S(2)}) collective-permute-start(f32[3,256]{1,0:T(4,128)S(1)} %add_add_fusion.1), channel_id=1, source_target_pairs={{0,1},{1,0},{2,3},{3,2},{4,5},{5,4},{6,7},{7,6},{8,9},{9,8},{10,11... | collective-permute-start | bytes 9224 | tf_op jit(solution)/shard_map/ppermute | solution.py:356
  117.3 1.7 %collective-permute-done.12 = f32[3,256]{1,0:T(4,128)S(1)} collective-permute-done((f32[3,256]{1,0:T(4,128)S(1)}, f32[3,256]{1,0:T(4,128)S(1)}, u32[]{:S(2)}, u32[]{:S(2)}) %collective-permute-start.12) | collective-permute-done | bytes 3104 | tf_op jit(solution)/shard_map/ppermute | solution.py:356
  119.0 2.9 %collective-permute-start.13 = (f32[3,256]{1,0:T(4,128)S(1)}, f32[3,256]{1,0:T(4,128)S(1)}, u32[]{:S(2)}, u32[]{:S(2)}) collective-permute-start(f32[3,256]{1,0:T(4,128)S(1)} %add.68), channel_id=1, source_target_pairs={{0,2},{1,3},{2,0},{3,1},{4,6},{5,7},{6,4},{7,5},{8,10},{9,11},{10,... | collective-permute-start | bytes 9224 | tf_op jit(solution)/shard_map/ppermute | solution.py:356
  121.9 1.6 %collective-permute-done.13 = f32[3,256]{1,0:T(4,128)S(1)} collective-permute-done((f32[3,256]{1,0:T(4,128)S(1)}, f32[3,256]{1,0:T(4,128)S(1)}, u32[]{:S(2)}, u32[]{:S(2)}) %collective-permute-start.13) | collective-permute-done | bytes 3104 | tf_op jit(solution)/shard_map/ppermute | solution.py:356
  123.6 0.6 fusion.1
  (51 shorter events, 1.7 us)
Async XLA Ops:
  1.4 4.7 %collective-permute-start = (f32[6,64]{1,0:T(8,128)S(1)}, f32[6,64]{1,0:T(8,128)S(1)}, u32[]{:S(2)}, u32[]{:S(2)}) collective-permute-start(f32[6,64]{1,0:T(8,128)S(1)} %pad_maximum_fusion), channel_id=1, source_target_pairs={{0,1},{1,0},{2,3},{3,2},{4,5},{5,4},{6,7},{7,6},{8,9},{9,8},{10,11... | collective-permute-start | bytes 4616 | tf_op jit(solution)/shard_map/ppermute | solution.py:339
  6.1 4.6 %collective-permute-start.1 = (f32[6,128]{1,0:T(8,128)S(1)}, f32[6,128]{1,0:T(8,128)S(1)}, u32[]{:S(2)}, u32[]{:S(2)}) collective-permute-start(f32[6,128]{1,0:T(8,128)S(1)} %maximum_select_fusion.1), channel_id=1, source_target_pairs={{0,2},{1,3},{2,0},{3,1},{4,6},{5,7},{6,4},{7,5},{8,10},{9,11},{10,... | collective-permute-start | bytes 9224 | tf_op jit(solution)/shard_map/ppermute | solution.py:339
  10.8 10.6 %collective-permute-start.2 = (f32[3,256]{1,0:T(4,128)S(1)}, f32[3,256]{1,0:T(4,128)S(1)}, u32[]{:S(2)}, u32[]{:S(2)}) collective-permute-start(f32[3,256]{1,0:T(4,128)S(1)} %slice.16.brick_ref), channel_id=1, source_target_pairs={{0,4},{4,8},{8,12},{12,16},{16,20},{20,24},{24,28},{28,0},{1,5},{5... | collective-permute-start | bytes 9224 | tf_op jit(solution)/shard_map/ppermute | solution.py:363
  10.8 10.6 %collective-permute-start.3 = (f32[3,256]{1,0:T(4,128)S(1)}, f32[3,256]{1,0:T(4,128)S(1)}, u32[]{:S(2)}, u32[]{:S(2)}) collective-permute-start(f32[3,256]{1,0:T(4,128)S(1)} %slice.16.brick_ref), channel_id=1, source_target_pairs={{0,28},{4,0},{8,4},{12,8},{16,12},{20,16},{24,20},{28,24},{1,29},{... | collective-permute-start | bytes 9224 | tf_op jit(solution)/shard_map/ppermute | solution.py:363
  15.3 0.9 copy-start.3
  16.2 0.7 copy-start.8
  16.9 0.7 copy-start
  17.6 1.6 %copy-start.10 = (f32[32]{0:T(128)S(1)}, f32[32]{0:T(128)}, u32[]{:S(2)}) copy-start(f32[32]{0:T(128)} %param.19) | copy-start | bytes 388
  17.7 0.7 copy-start.9
  18.4 0.7 copy-start.2
  18.4 0.9 copy-start.11
  19.2 2.2 %copy-start.1 = (s32[64,128]{1,0:T(8,128)S(1)}, s32[64,128]{1,0:T(8,128)}, u32[]{:S(2)}) copy-start(s32[64,128]{1,0:T(8,128)} %nbr_ref.3) | copy-start | bytes 98308
  19.3 0.7 copy-start.5
  20.0 0.7 copy-start.6
  20.7 0.7 copy-start.7
  58.4 3.9 %collective-permute-start.4 = (f32[3,256]{1,0:T(4,128)S(1)}, f32[3,256]{1,0:T(4,128)S(1)}, u32[]{:S(2)}, u32[]{:S(2)}) collective-permute-start(f32[3,256]{1,0:T(4,128)S(1)} %get-tuple-element.12), channel_id=1, source_target_pairs={{0,4},{4,8},{8,12},{12,16},{16,20},{20,24},{24,28},{28,0},{1,5},{5... | collective-permute-start | bytes 9224 | tf_op jit(solution)/shard_map/ppermute | solution.py:363
  58.4 4.0 %collective-permute-start.5 = (f32[3,256]{1,0:T(4,128)S(1)}, f32[3,256]{1,0:T(4,128)S(1)}, u32[]{:S(2)}, u32[]{:S(2)}) collective-permute-start(f32[3,256]{1,0:T(4,128)S(1)} %get-tuple-element.13), channel_id=1, source_target_pairs={{0,28},{4,0},{8,4},{12,8},{16,12},{20,16},{24,20},{28,24},{1,29},{... | collective-permute-start | bytes 9224 | tf_op jit(solution)/shard_map/ppermute | solution.py:363
  62.3 3.6 %collective-permute-start.6 = (f32[3,256]{1,0:T(4,128)S(1)}, f32[3,256]{1,0:T(4,128)S(1)}, u32[]{:S(2)}, u32[]{:S(2)}) collective-permute-start(f32[3,256]{1,0:T(4,128)S(1)} %add_add_fusion.2), channel_id=1, source_target_pairs={{0,1},{1,0},{2,3},{3,2},{4,5},{5,4},{6,7},{7,6},{8,9},{9,8},{10,11... | collective-permute-start | bytes 9224 | tf_op jit(solution)/shard_map/ppermute | solution.py:356
  65.9 4.5 %collective-permute-start.7 = (f32[3,256]{1,0:T(4,128)S(1)}, f32[3,256]{1,0:T(4,128)S(1)}, u32[]{:S(2)}, u32[]{:S(2)}) collective-permute-start(f32[3,256]{1,0:T(4,128)S(1)} %add.60), channel_id=1, source_target_pairs={{0,2},{1,3},{2,0},{3,1},{4,6},{5,7},{6,4},{7,5},{8,10},{9,11},{10,... | collective-permute-start | bytes 9224 | tf_op jit(solution)/shard_map/ppermute | solution.py:356
  70.5 3.9 %collective-permute-start.8 = (f32[3,256]{1,0:T(4,128)S(1)}, f32[3,256]{1,0:T(4,128)S(1)}, u32[]{:S(2)}, u32[]{:S(2)}) collective-permute-start(f32[3,256]{1,0:T(4,128)S(1)} %multiply_add_fusion.1.brick_ref), channel_id=1, source_target_pairs={{0,4},{4,8},{8,12},{12,16},{16,20},{20,24},{24,28},{28,0},{1,5},{5... | collective-permute-start | bytes 9224 | tf_op jit(solution)/shard_map/ppermute | solution.py:363
  70.5 4.0 %collective-permute-start.9 = (f32[3,256]{1,0:T(4,128)S(1)}, f32[3,256]{1,0:T(4,128)S(1)}, u32[]{:S(2)}, u32[]{:S(2)}) collective-permute-start(f32[3,256]{1,0:T(4,128)S(1)} %multiply_add_fusion.1.brick_ref), channel_id=1, source_target_pairs={{0,28},{4,0},{8,4},{12,8},{16,12},{20,16},{24,20},{28,24},{1,29},{... | collective-permute-start | bytes 9224 | tf_op jit(solution)/shard_map/ppermute | solution.py:363
  73.2 38.2 %copy-start.4 = (f32[3,64]{1,0:T(4,128)}, f32[3,64]{1,0:T(4,128)S(1)}, u32[]{:S(2)}) copy-start(f32[3,64]{1,0:T(4,128)S(1)} %constant_dynamic-slice_fusion) | copy-start | bytes 2308
  111.4 3.9 %collective-permute-start.10 = (f32[3,256]{1,0:T(4,128)S(1)}, f32[3,256]{1,0:T(4,128)S(1)}, u32[]{:S(2)}, u32[]{:S(2)}) collective-permute-start(f32[3,256]{1,0:T(4,128)S(1)} %get-tuple-element.15), channel_id=1, source_target_pairs={{0,4},{4,8},{8,12},{12,16},{16,20},{20,24},{24,28},{28,0},{1,5},{5... | collective-permute-start | bytes 9224 | tf_op jit(solution)/shard_map/ppermute | solution.py:363
  111.4 4.0 %collective-permute-start.11 = (f32[3,256]{1,0:T(4,128)S(1)}, f32[3,256]{1,0:T(4,128)S(1)}, u32[]{:S(2)}, u32[]{:S(2)}) collective-permute-start(f32[3,256]{1,0:T(4,128)S(1)} %get-tuple-element.16), channel_id=1, source_target_pairs={{0,28},{4,0},{8,4},{12,8},{16,12},{20,16},{24,20},{28,24},{1,29},{... | collective-permute-start | bytes 9224 | tf_op jit(solution)/shard_map/ppermute | solution.py:363
  115.4 3.6 %collective-permute-start.12 = (f32[3,256]{1,0:T(4,128)S(1)}, f32[3,256]{1,0:T(4,128)S(1)}, u32[]{:S(2)}, u32[]{:S(2)}) collective-permute-start(f32[3,256]{1,0:T(4,128)S(1)} %add_add_fusion.1), channel_id=1, source_target_pairs={{0,1},{1,0},{2,3},{3,2},{4,5},{5,4},{6,7},{7,6},{8,9},{9,8},{10,11... | collective-permute-start | bytes 9224 | tf_op jit(solution)/shard_map/ppermute | solution.py:356
  119.0 4.5 %collective-permute-start.13 = (f32[3,256]{1,0:T(4,128)S(1)}, f32[3,256]{1,0:T(4,128)S(1)}, u32[]{:S(2)}, u32[]{:S(2)}) collective-permute-start(f32[3,256]{1,0:T(4,128)S(1)} %add.68), channel_id=1, source_target_pairs={{0,2},{1,3},{2,0},{3,1},{4,6},{5,7},{6,4},{7,5},{8,10},{9,11},{10,... | collective-permute-start | bytes 9224 | tf_op jit(solution)/shard_map/ppermute | solution.py:356

commit v2 on v1

--- a/solution.py
+++ b/solution.py
@@ -12,6 +12,7 @@
 kick_scale = 0.25
 time_step = 0.05
 LANES = 128
+GROUP = 4
 f32 = jnp.float32
 bf16 = jnp.bfloat16
 NN = (((1,), (0,)), ((), ()))
@@ -57,9 +58,14 @@
     t_s,
     d_s,
     h1_s,
+    h2_s,
     u2_s,
     u3_s,
     g_s,
+    da3_s,
+    dg_s,
+    da2_s,
+    dh2_s,
     z_s,
     dr_s,
     hi_s,
@@ -118,40 +124,52 @@
     hi_s[...] = high
     lo_s[...] = low
 
+    width = GROUP * slots
+    groups = atoms // GROUP
     w1 = jnp.broadcast_to(w1_ref[...], (e1, LANES))
     b1 = jnp.broadcast_to(b1_ref[...], (e1, LANES))
-    w1 = jnp.concatenate([w1, w1], axis=1)
-    b1 = jnp.concatenate([b1, b1], axis=1)
-    row8 = lax.broadcasted_iota(jnp.int32, (8, LANES), 0)
-
-    def both(value):
-        left = jnp.where(row8 < 4, value, 0.0)
-        right = jnp.where(row8 >= 4, value, 0.0)
-        return jnp.concatenate([left, right], axis=1)
-
-    def forward(p, carry):
-        base = pl.multiple_of(p * 8, 8)
-        s_row = jnp.concatenate(
-            [
-                jnp.broadcast_to(s_s[pl.ds(2 * p, 1), :], (e1, LANES)),
-                jnp.broadcast_to(s_s[pl.ds(2 * p + 1, 1), :], (e1, LANES)),
-            ],
-            axis=1,
-        )
-        h1 = jnp.tanh(w1 * s_row + b1)
+    row16 = lax.broadcasted_iota(jnp.int32, (4 * GROUP, LANES), 0) // 4
+
+    def spread(value):
+        return jnp.concatenate(
+            [jnp.where(row16 == a, value, 0.0) for a in range(GROUP)], axis=1
+        ).astype(bf16)
+
+    def collect(value):
+        total = value[:, :LANES]
+        for a in range(1, GROUP):
+            total = jnp.where(row16 == a, value[:, a * LANES : (a + 1) * LANES], total)
+        return total
+
+    def at(step, lag):
+        return jnp.clip(step - lag, 0, groups - 1)
+
+    def rows16(group):
+        return pl.ds(pl.multiple_of(group * 4 * GROUP, 4 * GROUP), 4 * GROUP)
+
+    def forward(step, carry):
+        j = at(step, 3)
+        t_s[rows16(j), :] = mm(spread(r_s[rows16(j), :]), g_s[j], NT) * inv_slots
+
+        j = at(step, 2)
+        h2 = h2_s[j]
+        t3 = jnp.tanh(mm(w3t_ref[...], h2.astype(bf16)) + b3_ref[...])
+        g_s[j] = (jnp.concatenate([h2, h2], axis=0) + t3).astype(bf16)
+        u3_s[j] = 1.0 - t3 * t3
+
+        j = at(step, 1)
+        h1 = h1_s[j]
         t2 = jnp.tanh(mm(w2t_ref[...], h1.astype(bf16)) + b2_ref[...])
-        h2 = jnp.concatenate([h1, h1], axis=0) + t2
-        t3 = jnp.tanh(mm(w3t_ref[...], h2.astype(bf16)) + b3_ref[...])
-        g = (jnp.concatenate([h2, h2], axis=0) + t3).astype(bf16)
-        h1_s[p] = h1
-        u2_s[p] = 1.0 - t2 * t2
-        u3_s[p] = 1.0 - t3 * t3
-        g_s[p] = g
-        r2 = both(r_s[pl.ds(base, 8), :]).astype(bf16)
-        t_s[pl.ds(base, 8), :] = mm(r2, g, NT) * inv_slots
+        h2_s[j] = jnp.concatenate([h1, h1], axis=0) + t2
+        u2_s[j] = 1.0 - t2 * t2
+
+        j = at(step, 0)
+        for a in range(GROUP):
+            s_row = jnp.broadcast_to(s_s[pl.ds(GROUP * j + a, 1), :], (e1, LANES))
+            h1_s[j, :, a * LANES : (a + 1) * LANES] = jnp.tanh(w1 * s_row + b1)
         return carry
 
-    lax.fori_loop(0, pairs, forward, 0)
+    lax.fori_loop(0, groups + 3, forward, 0)
 
     tens = [t_s[pl.ds(c, atoms, stride=4), :] for c in range(4)]
     for k in range(m2):
@@ -182,28 +200,32 @@
     for c in range(4):
         d_s[pl.ds(c, atoms, stride=4), :] = grads[c].astype(bf16).astype(f32) * inv_slots
 
-    def backward(p, carry):
-        base = pl.multiple_of(p * 8, 8)
-        dt = d_s[pl.ds(base, 8), :].astype(bf16)
-        r2 = both(r_s[pl.ds(base, 8), :]).astype(bf16)
-        dr = mm(dt, g_s[p])
-        dr_s[pl.ds(base, 8), :] = jnp.where(row8 < 4, dr[:, :LANES], dr[:, LANES:])
-        dg = mm(dt, r2, TN)
-        da3 = (dg * u3_s[p]).astype(bf16)
-        dh2 = dg[: e3 // 2] + dg[e3 // 2 :] + mm(w3_ref[...], da3)
-        da2 = (dh2 * u2_s[p]).astype(bf16)
-        dh1 = dh2[: e2 // 2] + dh2[e2 // 2 :] + mm(w2_ref[...], da2)
-        h1 = h1_s[p]
-        part = dh1 * (1.0 - h1 * h1) * w1
-        z = part[0:8]
-        for i in range(1, e1 // 8):
-            z = z + part[8 * i : 8 * i + 8]
-        wide_base = pl.multiple_of(p * 16, 16)
-        z_s[pl.ds(wide_base, 8), :] = z[:, :LANES]
-        z_s[pl.ds(wide_base + 8, 8), :] = z[:, LANES:]
+    def backward(step, carry):
+        j = at(step, 2)
+        dh1 = dh2_s[j] + mm(w2_ref[...], da2_s[j])
+        h1 = h1_s[j]
+        part = dh1 * (1.0 - h1 * h1)
+        for a in range(GROUP):
+            z = None
+            for i in range(0, e1, 8):
+                term = part[i : i + 8, a * LANES : (a + 1) * LANES] * w1[i : i + 8]
+                z = term if z is None else z + term
+            z_s[pl.ds(pl.multiple_of((GROUP * j + a) * 8, 8), 8), :] = z
+
+        j = at(step, 1)
+        dh2 = dg_s[j] + mm(w3_ref[...], da3_s[j])
+        da2_s[j] = (dh2 * u2_s[j]).astype(bf16)
+        dh2_s[j] = dh2[: e2 // 2] + dh2[e2 // 2 :]
+
+        j = at(step, 0)
+        dt = d_s[rows16(j), :].astype(bf16)
+        dr_s[rows16(j), :] = collect(mm(dt, g_s[j]))
+        dg = mm(dt, spread(r_s[rows16(j), :]), TN)
+        da3_s[j] = (dg * u3_s[j]).astype(bf16)
+        dg_s[j] = dg[: e3 // 2] + dg[e3 // 2 :]
         return carry
 
-    lax.fori_loop(0, pairs, backward, 0)
+    lax.fori_loop(0, groups + 2, backward, 0)
 
     ds = dr_s[pl.ds(0, atoms, stride=4), :]
     for i in range(8):
@@ -245,7 +267,7 @@
         lhs = jnp.concatenate(rows, axis=1).astype(bf16)
         return total + mm(lhs, jnp.concatenate(hots, axis=1), NT)
 
-    total = lax.fori_loop(0, pairs, scatter, jnp.zeros((8 * chunks, LANES), f32))
+    total = lax.fori_loop(0, pairs, scatter, jnp.zeros((8 * chunks, LANES), f32), unroll=4)
     rank = rank_ref[0]
     spot = lax.broadcasted_iota(jnp.int32, (3, brick_len), 1) // atoms
     placed = jnp.where(
@@ -290,8 +312,8 @@
     e1 = prepared[0].shape[0]
     e2 = prepared[3].shape[1]
     e3 = prepared[6].shape[1]
-    pairs = atoms // 2
-    wide = 2 * slots
+    groups = atoms // GROUP
+    wide = GROUP * slots
     own = jnp.concatenate([own, own], axis=1)[:, :LANES]
     vmem = pl.BlockSpec(memory_space=pltpu.VMEM)
     piece = jax.ShapeDtypeStruct((3, brick_len), f32)
@@ -305,10 +327,15 @@
             pltpu.VMEM((4 * atoms, slots), f32),
             pltpu.VMEM((4 * atoms, e3), f32),
             pltpu.VMEM((4 * atoms, e3), f32),
-            pltpu.VMEM((pairs, e1, wide), f32),
-            pltpu.VMEM((pairs, e2, wide), f32),
-            pltpu.VMEM((pairs, e3, wide), f32),
-            pltpu.VMEM((pairs, e3, wide), bf16),
+            pltpu.VMEM((groups, e1, wide), f32),
+            pltpu.VMEM((groups, e2, wide), f32),
+            pltpu.VMEM((groups, e2, wide), f32),
+            pltpu.VMEM((groups, e3, wide), f32),
+            pltpu.VMEM((groups, e3, wide), bf16),
+            pltpu.VMEM((groups, e3, wide), bf16),
+            pltpu.VMEM((groups, e2, wide), f32),
+            pltpu.VMEM((groups, e2, wide), bf16),
+            pltpu.VMEM((groups, e1, wide), f32),
             pltpu.VMEM((8 * atoms, slots), f32),
             pltpu.VMEM((4 * atoms, slots), f32),
             pltpu.VMEM((atoms, slots), jnp.int32),

time: 125 us -> 77.2 us (0.62)
  Pallas kernels: 74 us -> 26.6 us
    pallas_call x2, Pallas kernels: 74 us -> 26.6 us  [evaluate(): pl.pallas_call(eval_kernel, out_shape=(jax.ShapeDtypeStruct((1, atoms), f...]
  transfers between devices with their start and end apart: 14 -> 14, of which waited for: 9 -> 9; matrix products, arithmetic and copies ran while one was open for 2% -> 4% of each run, Pallas kernels for 0% -> 0%
where the time goes in v2:
time: 77.2 us; the launch traced here: 76.8 us
  Pallas kernels  26.6 us (34%)
  starting transfers between devices  26.4 us (34%)
  waiting for transfers between devices  13.6 us (18%)
  local copies, waits for them, and re-layouts  8.44 us (11%)
  other arithmetic  1.07 us (1%)
    pallas_call x2, Pallas kernels, evaluate(): pl.pallas_call(eval_kernel, out_shape=(jax.ShapeDtypeStruct((1, atoms), f...  26.6 us
    ppermute x4, starting transfers between devices, exchange(): lax.ppermute(down, 'brick', ring(size, -1))  10.6 us
    ppermute x4, starting transfers between devices, sum_help(): value = value + lax.ppermute(value, 'help', flip(size, bit))  9.65 us
    unnamed x28, local copies, waits for them, and re-layouts  7.18 us
    ppermute x4, waiting for transfers between devices, sum_help(): value = value + lax.ppermute(value, 'help', flip(size, bit))  6.57 us
    ppermute x2, starting transfers between devices, gather_help(): other = lax.ppermute(value, 'help', flip(size, bit))  6.15 us
    ppermute x4, waiting for transfers between devices, exchange(): lax.ppermute(up, 'brick', ring(size, 1))  3.71 us
    ppermute x2, waiting for transfers between devices, gather_help(): other = lax.ppermute(value, 'help', flip(size, bit))  3.17 us
  transfers between devices with their start and end apart: 14, of which 9 were waited for; matrix products, arithmetic and copies ran while one was open for 4% of the time, Pallas kernels for 0%

profile of v2, /device:TPU:0, one launch (start us, length us, event | category | flops | bytes accessed | tf_op | source)
XLA Modules:
  0.0 76.8 jit_solution(16795722856018308269)
XLA Ops:
  0.6 0.7 multiply_add_fusion.2
  1.4 3.1 %collective-permute-start = (f32[6,64]{1,0:T(8,128)S(1)}, f32[6,64]{1,0:T(8,128)S(1)}, u32[]{:S(2)}, u32[]{:S(2)}) collective-permute-start(f32[6,64]{1,0:T(8,128)S(1)} %pad_maximum_fusion), channel_id=1, source_target_pairs={{0,1},{1,0},{2,3},{3,2},{4,5},{5,4},{6,7},{7,6},{8,9},{9,8},{10,11... | collective-permute-start | bytes 4616 | tf_op jit(solution)/shard_map/ppermute | solution.py:366
  4.5 1.6 %collective-permute-done = f32[6,64]{1,0:T(8,128)S(1)} collective-permute-done((f32[6,64]{1,0:T(8,128)S(1)}, f32[6,64]{1,0:T(8,128)S(1)}, u32[]{:S(2)}, u32[]{:S(2)}) %collective-permute-start) | collective-permute-done | bytes 1568 | tf_op jit(solution)/shard_map/ppermute | solution.py:366
  6.1 3.0 %collective-permute-start.1 = (f32[6,128]{1,0:T(8,128)S(1)}, f32[6,128]{1,0:T(8,128)S(1)}, u32[]{:S(2)}, u32[]{:S(2)}) collective-permute-start(f32[6,128]{1,0:T(8,128)S(1)} %maximum_select_fusion.1), channel_id=1, source_target_pairs={{0,2},{1,3},{2,0},{3,1},{4,6},{5,7},{6,4},{7,5},{8,10},{9,11},{10,... | collective-permute-start | bytes 9224 | tf_op jit(solution)/shard_map/ppermute | solution.py:366
  9.2 1.6 %collective-permute-done.1 = f32[6,128]{1,0:T(8,128)S(1)} collective-permute-done((f32[6,128]{1,0:T(8,128)S(1)}, f32[6,128]{1,0:T(8,128)S(1)}, u32[]{:S(2)}, u32[]{:S(2)}) %collective-permute-start.1) | collective-permute-done | bytes 3104 | tf_op jit(solution)/shard_map/ppermute | solution.py:366
  10.8 2.6 %collective-permute-start.3 = (f32[3,256]{1,0:T(4,128)S(1)}, f32[3,256]{1,0:T(4,128)S(1)}, u32[]{:S(2)}, u32[]{:S(2)}) collective-permute-start(f32[3,256]{1,0:T(4,128)S(1)} %slice.16.brick_ref), channel_id=1, source_target_pairs={{0,28},{4,0},{8,4},{12,8},{16,12},{20,16},{24,20},{28,24},{1,29},{... | collective-permute-start | bytes 9224 | tf_op jit(solution)/shard_map/ppermute | solution.py:390
  13.5 1.5 %copy.32 = bf16[2048,240]{1,0:T(8,128)(2,1)S(1)} copy(bf16[2048,240]{0,1:T(8,128)(2,1)} %param.25) | data formatting | bytes 1966080 | tf_op args[10]
  15.5 0.7 copy-done.3
  16.3 0.6 copy-done.8
  17.0 0.6 copy-done
  17.7 0.7 copy-done.9
  18.5 0.6 copy-done.2
  19.4 0.6 copy-done.5
  20.0 0.7 copy-done.6
  20.7 0.7 copy-done.7
  21.4 13.3 %evaluate.2 = (f32[1,64]{1,0:T(1,128)}, f32[3,256]{1,0:T(4,128)S(1)}, f32[3,256]{1,0:T(4,128)S(1)}, f32[3,256]{1,0:T(4,128)S(1)}) custom-call(s32[1]{0:T(128)} %bitcast.rank_ref, f32[3,256]{1,0:T(4,128)S(1)} %collective-permute-done.2.before_ref, f32[3,256]{1,0:T(4,128)S(1)} %slice.16.brick_ref, f32[3,256]{1,0:T(4,128)S(1)} %collective-permute-done.3.after_ref, ...), custom_call_target="tpu_custom_call" | custom-call | tf_op jit(solution)/shard_map/evaluate/pallas_call | solution.py:320
  34.7 2.6 %collective-permute-start.5 = (f32[3,256]{1,0:T(4,128)S(1)}, f32[3,256]{1,0:T(4,128)S(1)}, u32[]{:S(2)}, u32[]{:S(2)}) collective-permute-start(f32[3,256]{1,0:T(4,128)S(1)} %get-tuple-element.13), channel_id=1, source_target_pairs={{0,28},{4,0},{8,4},{12,8},{16,12},{20,16},{24,20},{28,24},{1,29},{... | collective-permute-start | bytes 9224 | tf_op jit(solution)/shard_map/ppermute | solution.py:390
  37.3 1.3 %collective-permute-done.4 = f32[3,256]{1,0:T(4,128)S(1)} collective-permute-done((f32[3,256]{1,0:T(4,128)S(1)}, f32[3,256]{1,0:T(4,128)S(1)}, u32[]{:S(2)}, u32[]{:S(2)}) %collective-permute-start.4) | collective-permute-done | bytes 3104 | tf_op jit(solution)/shard_map/ppermute | solution.py:390
  38.6 1.9 %collective-permute-start.6 = (f32[3,256]{1,0:T(4,128)S(1)}, f32[3,256]{1,0:T(4,128)S(1)}, u32[]{:S(2)}, u32[]{:S(2)}) collective-permute-start(f32[3,256]{1,0:T(4,128)S(1)} %add_add_fusion.2), channel_id=1, source_target_pairs={{0,1},{1,0},{2,3},{3,2},{4,5},{5,4},{6,7},{7,6},{8,9},{9,8},{10,11... | collective-permute-start | bytes 9224 | tf_op jit(solution)/shard_map/ppermute | solution.py:383
  40.6 1.7 %collective-permute-done.6 = f32[3,256]{1,0:T(4,128)S(1)} collective-permute-done((f32[3,256]{1,0:T(4,128)S(1)}, f32[3,256]{1,0:T(4,128)S(1)}, u32[]{:S(2)}, u32[]{:S(2)}) %collective-permute-start.6) | collective-permute-done | bytes 3104 | tf_op jit(solution)/shard_map/ppermute | solution.py:383
  42.3 2.9 %collective-permute-start.7 = (f32[3,256]{1,0:T(4,128)S(1)}, f32[3,256]{1,0:T(4,128)S(1)}, u32[]{:S(2)}, u32[]{:S(2)}) collective-permute-start(f32[3,256]{1,0:T(4,128)S(1)} %add.60), channel_id=1, source_target_pairs={{0,2},{1,3},{2,0},{3,1},{4,6},{5,7},{6,4},{7,5},{8,10},{9,11},{10,... | collective-permute-start | bytes 9224 | tf_op jit(solution)/shard_map/ppermute | solution.py:383
  45.2 1.6 %collective-permute-done.7 = f32[3,256]{1,0:T(4,128)S(1)} collective-permute-done((f32[3,256]{1,0:T(4,128)S(1)}, f32[3,256]{1,0:T(4,128)S(1)}, u32[]{:S(2)}, u32[]{:S(2)}) %collective-permute-start.7) | collective-permute-done | bytes 3104 | tf_op jit(solution)/shard_map/ppermute | solution.py:383
  46.8 2.6 %collective-permute-start.9 = (f32[3,256]{1,0:T(4,128)S(1)}, f32[3,256]{1,0:T(4,128)S(1)}, u32[]{:S(2)}, u32[]{:S(2)}) collective-permute-start(f32[3,256]{1,0:T(4,128)S(1)} %multiply_add_fusion.1.brick_ref), channel_id=1, source_target_pairs={{0,28},{4,0},{8,4},{12,8},{16,12},{20,16},{24,20},{28,24},{1,29},{... | collective-permute-start | bytes 9224 | tf_op jit(solution)/shard_map/ppermute | solution.py:390
  49.6 1.1 %collective-permute-done.8.before_ref = f32[3,256]{1,0:T(4,128)S(1)} collective-permute-done((f32[3,256]{1,0:T(4,128)S(1)}, f32[3,256]{1,0:T(4,128)S(1)}, u32[]{:S(2)}, u32[]{:S(2)}) %collective-permute-start.8) | collective-permute-done | bytes 3104 | tf_op jit(solution)/shard_map/ppermute | solution.py:390
  50.7 13.3 %evaluate.3 = (f32[1,64]{1,0:T(1,128)}, f32[3,256]{1,0:T(4,128)S(1)}, f32[3,256]{1,0:T(4,128)S(1)}, f32[3,256]{1,0:T(4,128)S(1)}) custom-call(s32[1]{0:T(128)} %bitcast.rank_ref, f32[3,256]{1,0:T(4,128)S(1)} %collective-permute-done.8.before_ref, f32[3,256]{1,0:T(4,128)S(1)} %multiply_add_fusion.1.brick_ref, f32[3,256]{1,0:T(4,128)S(1)} %collective-permute-done.9.after_ref, ...), custom_call_target="tpu_custom_call" | custom-call | tf_op jit(solution)/shard_map/evaluate/pallas_call | solution.py:320
  64.0 2.6 %collective-permute-start.11 = (f32[3,256]{1,0:T(4,128)S(1)}, f32[3,256]{1,0:T(4,128)S(1)}, u32[]{:S(2)}, u32[]{:S(2)}) collective-permute-start(f32[3,256]{1,0:T(4,128)S(1)} %get-tuple-element.16), channel_id=1, source_target_pairs={{0,28},{4,0},{8,4},{12,8},{16,12},{20,16},{24,20},{28,24},{1,29},{... | collective-permute-start | bytes 9224 | tf_op jit(solution)/shard_map/ppermute | solution.py:390
  66.7 1.3 %collective-permute-done.10 = f32[3,256]{1,0:T(4,128)S(1)} collective-permute-done((f32[3,256]{1,0:T(4,128)S(1)}, f32[3,256]{1,0:T(4,128)S(1)}, u32[]{:S(2)}, u32[]{:S(2)}) %collective-permute-start.10) | collective-permute-done | bytes 3104 | tf_op jit(solution)/shard_map/ppermute | solution.py:390
  68.0 1.9 %collective-permute-start.12 = (f32[3,256]{1,0:T(4,128)S(1)}, f32[3,256]{1,0:T(4,128)S(1)}, u32[]{:S(2)}, u32[]{:S(2)}) collective-permute-start(f32[3,256]{1,0:T(4,128)S(1)} %add_add_fusion.1), channel_id=1, source_target_pairs={{0,1},{1,0},{2,3},{3,2},{4,5},{5,4},{6,7},{7,6},{8,9},{9,8},{10,11... | collective-permute-start | bytes 9224 | tf_op jit(solution)/shard_map/ppermute | solution.py:383
  69.9 1.7 %collective-permute-done.12 = f32[3,256]{1,0:T(4,128)S(1)} collective-permute-done((f32[3,256]{1,0:T(4,128)S(1)}, f32[3,256]{1,0:T(4,128)S(1)}, u32[]{:S(2)}, u32[]{:S(2)}) %collective-permute-start.12) | collective-permute-done | bytes 3104 | tf_op jit(solution)/shard_map/ppermute | solution.py:383
  71.6 2.9 %collective-permute-start.13 = (f32[3,256]{1,0:T(4,128)S(1)}, f32[3,256]{1,0:T(4,128)S(1)}, u32[]{:S(2)}, u32[]{:S(2)}) collective-permute-start(f32[3,256]{1,0:T(4,128)S(1)} %add.68), channel_id=1, source_target_pairs={{0,2},{1,3},{2,0},{3,1},{4,6},{5,7},{6,4},{7,5},{8,10},{9,11},{10,... | collective-permute-start | bytes 9224 | tf_op jit(solution)/shard_map/ppermute | solution.py:383
  74.5 1.6 %collective-permute-done.13 = f32[3,256]{1,0:T(4,128)S(1)} collective-permute-done((f32[3,256]{1,0:T(4,128)S(1)}, f32[3,256]{1,0:T(4,128)S(1)}, u32[]{:S(2)}, u32[]{:S(2)}) %collective-permute-start.13) | collective-permute-done | bytes 3104 | tf_op jit(solution)/shard_map/ppermute | solution.py:383
  76.2 0.6 fusion.1
  (51 shorter events, 1.7 us)
Async XLA Ops:
  1.4 4.7 %collective-permute-start = (f32[6,64]{1,0:T(8,128)S(1)}, f32[6,64]{1,0:T(8,128)S(1)}, u32[]{:S(2)}, u32[]{:S(2)}) collective-permute-start(f32[6,64]{1,0:T(8,128)S(1)} %pad_maximum_fusion), channel_id=1, source_target_pairs={{0,1},{1,0},{2,3},{3,2},{4,5},{5,4},{6,7},{7,6},{8,9},{9,8},{10,11... | collective-permute-start | bytes 4616 | tf_op jit(solution)/shard_map/ppermute | solution.py:366
  6.1 4.6 %collective-permute-start.1 = (f32[6,128]{1,0:T(8,128)S(1)}, f32[6,128]{1,0:T(8,128)S(1)}, u32[]{:S(2)}, u32[]{:S(2)}) collective-permute-start(f32[6,128]{1,0:T(8,128)S(1)} %maximum_select_fusion.1), channel_id=1, source_target_pairs={{0,2},{1,3},{2,0},{3,1},{4,6},{5,7},{6,4},{7,5},{8,10},{9,11},{10,... | collective-permute-start | bytes 9224 | tf_op jit(solution)/shard_map/ppermute | solution.py:366
  10.8 10.6 %collective-permute-start.2 = (f32[3,256]{1,0:T(4,128)S(1)}, f32[3,256]{1,0:T(4,128)S(1)}, u32[]{:S(2)}, u32[]{:S(2)}) collective-permute-start(f32[3,256]{1,0:T(4,128)S(1)} %slice.16.brick_ref), channel_id=1, source_target_pairs={{0,4},{4,8},{8,12},{12,16},{16,20},{20,24},{24,28},{28,0},{1,5},{5... | collective-permute-start | bytes 9224 | tf_op jit(solution)/shard_map/ppermute | solution.py:390
  10.8 10.6 %collective-permute-start.3 = (f32[3,256]{1,0:T(4,128)S(1)}, f32[3,256]{1,0:T(4,128)S(1)}, u32[]{:S(2)}, u32[]{:S(2)}) collective-permute-start(f32[3,256]{1,0:T(4,128)S(1)} %slice.16.brick_ref), channel_id=1, source_target_pairs={{0,28},{4,0},{8,4},{12,8},{16,12},{20,16},{24,20},{28,24},{1,29},{... | collective-permute-start | bytes 9224 | tf_op jit(solution)/shard_map/ppermute | solution.py:390
  15.3 0.9 %copy-start.3 = (bf16[240,240]{1,0:T(8,128)(2,1)S(1)}, bf16[240,240]{1,0:T(8,128)(2,1)}, u32[]{:S(2)}) copy-start(bf16[240,240]{1,0:T(8,128)(2,1)} %param.27) | copy-start | bytes 345604
  16.2 0.7 copy-start.8
  16.9 0.7 copy-start
  17.6 1.6 %copy-start.10 = (f32[32]{0:T(128)S(1)}, f32[32]{0:T(128)}, u32[]{:S(2)}) copy-start(f32[32]{0:T(128)} %param.19) | copy-start | bytes 388
  17.7 0.7 copy-start.9
  18.4 0.7 copy-start.2
  18.4 0.9 %copy-start.11 = (f32[32]{0:T(128)S(1)}, f32[32]{0:T(128)}, u32[]{:S(2)}) copy-start(f32[32]{0:T(128)} %param.20) | copy-start | bytes 388
  19.2 2.2 %copy-start.1 = (s32[64,128]{1,0:T(8,128)S(1)}, s32[64,128]{1,0:T(8,128)}, u32[]{:S(2)}) copy-start(s32[64,128]{1,0:T(8,128)} %nbr_ref.3) | copy-start | bytes 98308
  19.3 0.7 copy-start.5
  20.0 0.7 copy-start.6
  20.7 0.7 copy-start.7
  34.7 3.9 %collective-permute-start.4 = (f32[3,256]{1,0:T(4,128)S(1)}, f32[3,256]{1,0:T(4,128)S(1)}, u32[]{:S(2)}, u32[]{:S(2)}) collective-permute-start(f32[3,256]{1,0:T(4,128)S(1)} %get-tuple-element.12), channel_id=1, source_target_pairs={{0,4},{4,8},{8,12},{12,16},{16,20},{20,24},{24,28},{28,0},{1,5},{5... | collective-permute-start | bytes 9224 | tf_op jit(solution)/shard_map/ppermute | solution.py:390
  34.7 4.0 %collective-permute-start.5 = (f32[3,256]{1,0:T(4,128)S(1)}, f32[3,256]{1,0:T(4,128)S(1)}, u32[]{:S(2)}, u32[]{:S(2)}) collective-permute-start(f32[3,256]{1,0:T(4,128)S(1)} %get-tuple-element.13), channel_id=1, source_target_pairs={{0,28},{4,0},{8,4},{12,8},{16,12},{20,16},{24,20},{28,24},{1,29},{... | collective-permute-start | bytes 9224 | tf_op jit(solution)/shard_map/ppermute | solution.py:390
  38.6 3.6 %collective-permute-start.6 = (f32[3,256]{1,0:T(4,128)S(1)}, f32[3,256]{1,0:T(4,128)S(1)}, u32[]{:S(2)}, u32[]{:S(2)}) collective-permute-start(f32[3,256]{1,0:T(4,128)S(1)} %add_add_fusion.2), channel_id=1, source_target_pairs={{0,1},{1,0},{2,3},{3,2},{4,5},{5,4},{6,7},{7,6},{8,9},{9,8},{10,11... | collective-permute-start | bytes 9224 | tf_op jit(solution)/shard_map/ppermute | solution.py:383
  42.3 4.5 %collective-permute-start.7 = (f32[3,256]{1,0:T(4,128)S(1)}, f32[3,256]{1,0:T(4,128)S(1)}, u32[]{:S(2)}, u32[]{:S(2)}) collective-permute-start(f32[3,256]{1,0:T(4,128)S(1)} %add.60), channel_id=1, source_target_pairs={{0,2},{1,3},{2,0},{3,1},{4,6},{5,7},{6,4},{7,5},{8,10},{9,11},{10,... | collective-permute-start | bytes 9224 | tf_op jit(solution)/shard_map/ppermute | solution.py:383
  46.8 3.9 %collective-permute-start.8 = (f32[3,256]{1,0:T(4,128)S(1)}, f32[3,256]{1,0:T(4,128)S(1)}, u32[]{:S(2)}, u32[]{:S(2)}) collective-permute-start(f32[3,256]{1,0:T(4,128)S(1)} %multiply_add_fusion.1.brick_ref), channel_id=1, source_target_pairs={{0,4},{4,8},{8,12},{12,16},{16,20},{20,24},{24,28},{28,0},{1,5},{5... | collective-permute-start | bytes 9224 | tf_op jit(solution)/shard_map/ppermute | solution.py:390
  46.8 4.0 %collective-permute-start.9 = (f32[3,256]{1,0:T(4,128)S(1)}, f32[3,256]{1,0:T(4,128)S(1)}, u32[]{:S(2)}, u32[]{:S(2)}) collective-permute-start(f32[3,256]{1,0:T(4,128)S(1)} %multiply_add_fusion.1.brick_ref), channel_id=1, source_target_pairs={{0,28},{4,0},{8,4},{12,8},{16,12},{20,16},{24,20},{28,24},{1,29},{... | collective-permute-start | bytes 9224 | tf_op jit(solution)/shard_map/ppermute | solution.py:390
  49.5 14.5 %copy-start.4 = (f32[3,64]{1,0:T(4,128)}, f32[3,64]{1,0:T(4,128)S(1)}, u32[]{:S(2)}) copy-start(f32[3,64]{1,0:T(4,128)S(1)} %constant_dynamic-slice_fusion) | copy-start | bytes 2308
  64.0 3.9 %collective-permute-start.10 = (f32[3,256]{1,0:T(4,128)S(1)}, f32[3,256]{1,0:T(4,128)S(1)}, u32[]{:S(2)}, u32[]{:S(2)}) collective-permute-start(f32[3,256]{1,0:T(4,128)S(1)} %get-tuple-element.15), channel_id=1, source_target_pairs={{0,4},{4,8},{8,12},{12,16},{16,20},{20,24},{24,28},{28,0},{1,5},{5... | collective-permute-start | bytes 9224 | tf_op jit(solution)/shard_map/ppermute | solution.py:390
  64.0 4.0 %collective-permute-start.11 = (f32[3,256]{1,0:T(4,128)S(1)}, f32[3,256]{1,0:T(4,128)S(1)}, u32[]{:S(2)}, u32[]{:S(2)}) collective-permute-start(f32[3,256]{1,0:T(4,128)S(1)} %get-tuple-element.16), channel_id=1, source_target_pairs={{0,28},{4,0},{8,4},{12,8},{16,12},{20,16},{24,20},{28,24},{1,29},{... | collective-permute-start | bytes 9224 | tf_op jit(solution)/shard_map/ppermute | solution.py:390
  68.0 3.6 %collective-permute-start.12 = (f32[3,256]{1,0:T(4,128)S(1)}, f32[3,256]{1,0:T(4,128)S(1)}, u32[]{:S(2)}, u32[]{:S(2)}) collective-permute-start(f32[3,256]{1,0:T(4,128)S(1)} %add_add_fusion.1), channel_id=1, source_target_pairs={{0,1},{1,0},{2,3},{3,2},{4,5},{5,4},{6,7},{7,6},{8,9},{9,8},{10,11... | collective-permute-start | bytes 9224 | tf_op jit(solution)/shard_map/ppermute | solution.py:383
  71.6 4.5 %collective-permute-start.13 = (f32[3,256]{1,0:T(4,128)S(1)}, f32[3,256]{1,0:T(4,128)S(1)}, u32[]{:S(2)}, u32[]{:S(2)}) collective-permute-start(f32[3,256]{1,0:T(4,128)S(1)} %add.68), channel_id=1, source_target_pairs={{0,2},{1,3},{2,0},{3,1},{4,6},{5,7},{6,4},{7,5},{8,10},{9,11},{10,... | collective-permute-start | bytes 9224 | tf_op jit(solution)/shard_map/ppermute | solution.py:383

commit v3 on v2

v3 whole, which is shorter than its diff:
```python
import functools

import jax
import jax.numpy as jnp
from jax import lax
from jax.experimental import pallas as pl
from jax.experimental.pallas import tpu as pltpu
from jax.sharding import PartitionSpec as P

STEPS = 2

kick_scale = 0.25
time_step = 0.05
LANES = 128
PAIRS = 4
GROUP = 2 * PAIRS
f32 = jnp.float32
bf16 = jnp.bfloat16
NN = (((1,), (0,)), ((), ()))
NT = (((1,), (1,)), ((), ()))
TN = (((0,), (0,)), ((), ()))


def mm(a, b, dims=NN):
    return lax.dot_general(a, b, dims, preferred_element_type=f32)


def split2(x):
    high = x.astype(bf16).astype(f32)
    return high, x - high


def eval_kernel(
    rank_ref,
    before_ref,
    brick_ref,
    after_ref,
    own_ref,
    low_ref,
    high_ref,
    w1_ref,
    b1_ref,
    w2t_ref,
    w2_ref,
    b2_ref,
    w3t_ref,
    w3_ref,
    b3_ref,
    f1_ref,
    c1_ref,
    f2_ref,
    c2_ref,
    out_ref,
    energy_ref,
    to_before_ref,
    to_brick_ref,
    to_after_ref,
    s_s,
    r_s,
    t_s,
    d_s,
    h1_s,
    h2_s,
    u2_s,
    u3_s,
    g_s,
    da3_s,
    dg_s,
    da2_s,
    dh2_s,
    z_s,
    dr_s,
    gr_s,
    des_s,
):
    atoms, slots = low_ref.shape
    brick_len = brick_ref.shape[1]
    per = brick_len // LANES
    e1 = w1_ref.shape[0]
    e2 = b2_ref.shape[0] // PAIRS
    e3 = b3_ref.shape[0] // PAIRS
    m2 = f1_ref.shape[0] // e3
    inv_slots = 1.0 / slots
    pairs = atoms // 2

    low = low_ref[...]
    high = high_ref[...]
    mask = jnp.where(high >= 0, 1.0, 0.0).astype(f32)
    sub = lax.broadcasted_iota(jnp.int32, (atoms, slots), 0)
    coords = [jnp.zeros((atoms, slots), f32)] * 3
    for part, table in enumerate((before_ref, brick_ref, after_ref)):
        for chunk in range(per):
            hit = high == part * per + chunk
            for c in range(3):
                row = table[c : c + 1, chunk * LANES : (chunk + 1) * LANES]
                found = jnp.take_along_axis(
                    jnp.broadcast_to(row, (atoms, LANES)), low, axis=1, mode="promise_in_bounds"
                )
                coords[c] = jnp.where(hit, found, coords[c])
    shift = (
        jnp.where(high >= per, 1.0, 0.0) + jnp.where(high >= 2 * per, 1.0, 0.0) - 1.0
    ).astype(f32)
    disp = []
    for c in range(3):
        row = own_ref[c : c + 1, :]
        mine = jnp.take_along_axis(
            jnp.broadcast_to(row, (atoms, LANES)), sub, axis=1, mode="promise_in_bounds"
        )
        delta = coords[c] - mine
        if c == 0:
            delta = delta + shift
        disp.append(delta * mask)
    quad = disp[0] * disp[0] + disp[1] * disp[1] + disp[2] * disp[2] + 0.25
    radius = jnp.sqrt(quad)
    smooth = mask / radius
    inv_quad = 1.0 / quad
    s_s[...] = smooth
    r_s[pl.ds(0, atoms, stride=4), :] = smooth
    for c in range(3):
        r_s[pl.ds(c + 1, atoms, stride=4), :] = disp[c] * inv_quad

    groups = atoms // GROUP
    wide = 2 * slots
    half = 2 * e3
    w1 = w1_ref[...]
    b1 = b1_ref[...]
    row16 = lax.broadcasted_iota(jnp.int32, (16, LANES), 0)
    row32 = lax.broadcasted_iota(jnp.int32, (32, LANES), 0)

    def twice(value):
        return jnp.concatenate([value, value], axis=1)

    def choose(picks, value):
        return jnp.concatenate([jnp.where(p, value, 0.0) for p in picks], axis=1).astype(bf16)

    first16 = (row16 & 4) == 0
    first32 = (row32 & 4) == 0
    upper16 = row16 < 8
    blocks32 = [(row32 >> 3) == q for q in range(PAIRS)]

    def rows(group, size, part=0):
        start = group * (4 * GROUP) + part
        return pl.ds(start if isinstance(start, int) else pl.multiple_of(start, 16), size)

    def stacked(value, size, parts):
        return jnp.concatenate(
            [value[size * q : size * (q + 1)] for q in range(PAIRS) for _ in range(parts)], axis=0
        )

    def folded(value, size):
        return jnp.concatenate(
            [
                value[2 * size * q : 2 * size * q + size] + value[2 * size * q + size : 2 * size * (q + 1)]
                for q in range(PAIRS)
            ],
            axis=0,
        )

    def first_layer(j):
        for q in range(PAIRS):
            for a in range(2):
                s_row = jnp.broadcast_to(s_s[pl.ds(GROUP * j + 2 * q + a, 1), :], (e1, LANES))
                h1_s[j, q * e1 : (q + 1) * e1, a * LANES : (a + 1) * LANES] = jnp.tanh(
                    w1 * s_row + b1
                )

    def second_layer(j):
        h1 = h1_s[j]
        t2 = jnp.tanh(mm(w2t_ref[...], h1.astype(bf16)) + twice(b2_ref[...]))
        h2_s[j] = stacked(h1, e1, 2) + t2
        u2_s[j] = 1.0 - t2 * t2

    def third_layer(j):
        h2 = h2_s[j]
        t3 = jnp.tanh(mm(w3t_ref[...], h2.astype(bf16)) + twice(b3_ref[...]))
        g_s[j] = (stacked(h2, e2, 2) + t3).astype(bf16)
        u3_s[j] = 1.0 - t3 * t3

    def tensor(j):
        for h in range(PAIRS // 2):
            lhs = choose((first16, ~first16), r_s[rows(j, 16, 16 * h), :])
            t = mm(lhs, g_s[j, half * h : half * (h + 1), :], NT) * inv_slots
            t_s[rows(j, 16, 16 * h), :] = jnp.where(upper16, t[:, :e3], t[:, e3:])

    def pipeline(stages):
        depth = len(stages) - 1

        def run(step, valid):
            for lag in range(depth, -1, -1):
                if valid(lag):
                    stages[lag](step - lag)

        for step in range(depth):
            run(step, lambda lag: lag <= step)

        def body(step, carry):
            run(step, lambda lag: True)
            return carry

        lax.fori_loop(depth, groups, body, 0)
        for step in range(groups, groups + depth):
            run(step, lambda lag: step - lag < groups)

    pipeline([first_layer, second_layer, third_layer, tensor])

    tens = [t_s[pl.ds(c, atoms, stride=4), :] for c in range(4)]
    for k in range(m2):
        total = tens[0] * jnp.broadcast_to(tens[0][:, k : k + 1], (atoms, e3))
        for c in range(1, 4):
            total = total + tens[c] * jnp.broadcast_to(tens[c][:, k : k + 1], (atoms, e3))
        des_s[:, k * e3 : (k + 1) * e3] = total.astype(bf16)
    readout = out_ref[...]
    y1 = jnp.tanh(mm(des_s[...], f1_ref[...]) + c1_ref[...])
    t4 = jnp.tanh(mm(y1.astype(bf16), f2_ref[...]) + c2_ref[...])
    energy_ref[...] = lax.dot_general(
        readout, y1 + t4, NT, precision=lax.Precision.HIGHEST, preferred_element_type=f32
    )
    dz2 = (readout * (1.0 - t4 * t4)).astype(bf16)
    dy1 = readout + mm(dz2, f2_ref[...], NT)
    dz1 = (dy1 * (1.0 - y1 * y1)).astype(bf16)
    lane = lax.broadcasted_iota(jnp.int32, (atoms, e3), 1)
    grads = [jnp.zeros((atoms, e3), f32)] * 4
    for k in range(m2):
        dd = mm(dz1, f1_ref[k * e3 : (k + 1) * e3, :], NT)
        for c in range(4):
            other = jnp.sum(dd * tens[c], axis=1, keepdims=True)
            grads[c] = (
                grads[c]
                + dd * jnp.broadcast_to(tens[c][:, k : k + 1], (atoms, e3))
                + jnp.where(lane == k, other, 0.0)
            )
    for c in range(4):
        d_s[pl.ds(c, atoms, stride=4), :] = grads[c].astype(bf16).astype(f32) * inv_slots

    def third_back(j):
        dt = d_s[rows(j, 32), :]
        for h in range(PAIRS // 2):
            lhs = choose((upper16, ~upper16), dt[16 * h : 16 * (h + 1)])
            dr = mm(lhs, g_s[j, half * h : half * (h + 1), :])
            dr_s[rows(j, 16, 16 * h), :] = jnp.where(first16, dr[:, :LANES], dr[:, LANES:])
        spread = choose((first32, ~first32), r_s[rows(j, 32), :])
        dg = mm(choose(blocks32, dt), spread, TN)
        da3_s[j] = (dg * u3_s[j]).astype(bf16)
        dg_s[j] = folded(dg, e2)

    def second_back(j):
        back = jnp.concatenate(
            [mm(w3_ref[...], da3_s[j, half * h : half * (h + 1), :]) for h in range(PAIRS // 2)],
            axis=0,
        )
        dh2 = dg_s[j] + back
        da2_s[j] = (dh2 * u2_s[j]).astype(bf16)
        dh2_s[j] = folded(dh2, e1)

    def first_back(j):
        dh1 = dh2_s[j] + mm(w2_ref[...], da2_s[j])
        h1 = h1_s[j]
        part = dh1 * (1.0 - h1 * h1)
        for q in range(PAIRS):
            for a in range(2):
                z = None
                for i in range(0, e1, 8):
                    at = q * e1 + i
                    term = part[at : at + 8, a * LANES : (a + 1) * LANES] * w1[i : i + 8]
                    z = term if z is None else z + term
                start = (GROUP * j + 2 * q + a) * 8
                z_s[pl.ds(start if isinstance(start, int) else pl.multiple_of(start, 8), 8), :] = z

    pipeline([third_back, second_back, first_back])

    ds = dr_s[pl.ds(0, atoms, stride=4), :]
    for i in range(8):
        ds = ds + z_s[pl.ds(i, atoms, stride=8), :]
    drs = [dr_s[pl.ds(c + 1, atoms, stride=4), :] for c in range(3)]
    radial = drs[0] * disp[0] + drs[1] * disp[1] + drs[2] * disp[2]
    factor = -ds / (radius * quad) - 2.0 * radial * (inv_quad * inv_quad)
    ones = jnp.ones((8, LANES), bf16)
    zero = jnp.zeros((atoms, LANES), f32)
    sums = []
    for c in range(3):
        pull = mask * (disp[c] * factor + drs[c] * inv_quad)
        upper, lower = split2(pull)
        gr_s[pl.ds(c, atoms, stride=8), :] = upper
        gr_s[pl.ds(c + 3, atoms, stride=8), :] = lower
        both_parts = mm(ones, upper.astype(bf16), NT) + mm(ones, lower.astype(bf16), NT)
        sums.append(both_parts[0:1])
    gr_s[pl.ds(6, atoms, stride=8), :] = zero
    gr_s[pl.ds(7, atoms, stride=8), :] = zero
    mine = jnp.concatenate(sums, axis=0)

    place = lax.broadcasted_iota(jnp.int32, (LANES, LANES), 0)
    chunks = 3 * per

    def scatter(p, total):
        rows = []
        hots = []
        for i in range(2):
            atom = 2 * p + i
            values = gr_s[pl.ds(pl.multiple_of(atom * 8, 8), 8), :]
            upper = jnp.broadcast_to(high_ref[pl.ds(atom, 1), :], (8, LANES))
            lower = jnp.broadcast_to(low_ref[pl.ds(atom, 1), :], (LANES, LANES))
            rows.append(
                jnp.concatenate(
                    [jnp.where(upper == a, values, 0.0) for a in range(chunks)], axis=0
                )
            )
            hots.append(jnp.where(lower == place, 1.0, 0.0).astype(bf16))
        lhs = jnp.concatenate(rows, axis=1).astype(bf16)
        return total + mm(lhs, jnp.concatenate(hots, axis=1), NT)

    total = lax.fori_loop(0, pairs, scatter, jnp.zeros((8 * chunks, LANES), f32), unroll=4)
    rank = rank_ref[0]
    spot = lax.broadcasted_iota(jnp.int32, (3, brick_len), 1) // atoms
    placed = jnp.where(
        spot == rank, jnp.concatenate([mine] * (brick_len // atoms), axis=1), 0.0
    )
    for part, target in enumerate((to_before_ref, to_brick_ref, to_after_ref)):
        pieces = []
        for chunk in range(per):
            at = 8 * (part * per + chunk)
            pieces.append(total[at : at + 3] + total[at + 3 : at + 6])
        whole = -jnp.concatenate(pieces, axis=1)
        target[...] = whole + placed if part == 1 else whole


def column(row):
    size = row.shape[1]
    shape = (size, size)
    same = lax.broadcasted_iota(jnp.int32, shape, 0) == lax.broadcasted_iota(jnp.int32, shape, 1)
    picked = jnp.sum(jnp.where(same, jnp.broadcast_to(row, shape), 0.0), axis=1, keepdims=True)
    return jnp.broadcast_to(picked, (size, LANES))


def diagonal(target, block, copies):
    tall, long = block.shape
    target[...] = jnp.zeros(target.shape, target.dtype)
    for q in range(copies):
        target[q * tall : (q + 1) * tall, q * long : (q + 1) * long] = block


def prepare_kernel(*refs):
    count = 5
    raw = refs[:count]
    low_o, high_o, w1_o, b1_o, w2t_o, w2_o, b2_o, w3t_o, w3_o, b3_o, f1_o, c1_o, c2_o, out_o = refs[
        count : count + 14
    ]
    here = refs[count + 14 : 2 * count + 14]
    wide_s, sems = refs[2 * count + 14 :]
    copies = [pltpu.make_async_copy(raw[i], here[i], sems.at[i]) for i in range(count)]
    for copy in copies:
        copy.start()
    for copy in copies:
        copy.wait()
    nbr, w2, w3, f1, small = here
    index = nbr[...]
    low_o[...] = index & (LANES - 1)
    high_o[...] = lax.shift_right_arithmetic(index, 7)
    e1, e2 = w2.shape
    e3 = w3.shape[1]
    fit = f1.shape[0]
    rows = f1.shape[1]
    m2 = rows // e3
    vectors = []
    start = 0
    for size in (e1, e1, e2, e3, fit, fit, fit):
        vectors.append(small[:, start : start + size])
        start += size + -size % LANES
    w1, b1, b2, b3, c1, c2, out = vectors
    w1_o[...] = column(w1)
    b1_o[...] = column(b1)
    b2_o[...] = jnp.concatenate([column(b2)] * PAIRS, axis=0)
    b3_o[...] = jnp.concatenate([column(b3)] * PAIRS, axis=0)
    diagonal(w2_o, w2[...], PAIRS)
    diagonal(w3_o, w3[...], PAIRS // 2)
    diagonal(w2t_o, w2[...].astype(f32).T.astype(bf16), PAIRS)
    diagonal(w3t_o, w3[...].astype(f32).T.astype(bf16), PAIRS)
    c1_o[...] = c1
    c2_o[...] = c2
    out_o[...] = out
    for part in range(0, fit, LANES):
        upto = min(LANES, fit - part)
        for start in range(0, rows, LANES):
            block = f1[part : part + upto, start : start + LANES].astype(f32)
            if upto < LANES:
                block = jnp.concatenate([block, jnp.zeros((LANES - upto, LANES), f32)], axis=0)
            wide_s[start : start + LANES, :] = block.T
        for k in range(m2):
            picked = wide_s[pl.ds(k, e3, stride=m2), :]
            f1_o[k * e3 : (k + 1) * e3, part : part + upto] = picked[:, :upto].astype(bf16)


def prepare(neighbors, weights):
    w1, b1, w2, b2, w3, b3, f1, c1, f2, c2, out = weights
    e1, e2, e3 = w1.shape[0], w2.shape[1], w3.shape[1]
    fit = out.shape[0]
    small = jnp.concatenate(
        [jnp.pad(v, (0, -v.shape[0] % LANES)) for v in (w1, b1, b2, b3, c1, c2, out)]
    )
    raw = (neighbors, w2, w3, f1.T, small[None])
    shape = jax.ShapeDtypeStruct
    outs = (
        shape(neighbors.shape, jnp.int32),
        shape(neighbors.shape, jnp.int32),
        shape((e1, LANES), f32),
        shape((e1, LANES), f32),
        shape((PAIRS * e2, PAIRS * e1), bf16),
        shape((PAIRS * e1, PAIRS * e2), bf16),
        shape((PAIRS * e2, LANES), f32),
        shape((PAIRS * e3, PAIRS * e2), bf16),
        shape((PAIRS // 2 * e2, PAIRS // 2 * e3), bf16),
        shape((PAIRS * e3, LANES), f32),
        shape((f1.shape[0], fit), bf16),
        shape((1, fit), f32),
        shape((1, fit), f32),
        shape((1, fit), f32),
    )
    made = pl.pallas_call(
        prepare_kernel,
        out_shape=outs,
        in_specs=[pl.BlockSpec(memory_space=pltpu.HBM)] * len(raw),
        out_specs=[pl.BlockSpec(memory_space=pltpu.VMEM)] * len(outs),
        scratch_shapes=[pltpu.VMEM(x.shape, x.dtype) for x in raw]
        + [pltpu.VMEM((f1.shape[0], LANES), f32), pltpu.SemaphoreType.DMA((len(raw),))],
        compiler_params=pltpu.CompilerParams(vmem_limit_bytes=16 * 1024 * 1024),
        cost_estimate=pl.CostEstimate(flops=4_000_000, bytes_accessed=2_500_000, transcendentals=0),
        name="prepare",
    )(*raw)
    return (*made[:12], f2, *made[12:])


def evaluate(rank, before, brick, after, own, prepared):
    atoms, slots = prepared[0].shape
    brick_len = brick.shape[1]
    e1 = prepared[2].shape[0]
    e2 = prepared[4].shape[0] // PAIRS
    e3 = prepared[7].shape[0] // PAIRS
    groups = atoms // GROUP
    wide = 2 * slots
    own = jnp.concatenate([own, own], axis=1)[:, :LANES]
    vmem = pl.BlockSpec(memory_space=pltpu.VMEM)
    piece = jax.ShapeDtypeStruct((3, brick_len), f32)
    return pl.pallas_call(
        eval_kernel,
        out_shape=(jax.ShapeDtypeStruct((1, atoms), f32), piece, piece, piece),
        in_specs=[pl.BlockSpec(memory_space=pltpu.SMEM)] + [vmem] * (4 + len(prepared)),
        out_specs=[vmem] * 4,
        scratch_shapes=[
            pltpu.VMEM((atoms, slots), f32),
            pltpu.VMEM((4 * atoms, slots), f32),
            pltpu.VMEM((4 * atoms, e3), f32),
            pltpu.VMEM((4 * atoms, e3), f32),
            pltpu.VMEM((groups, PAIRS * e1, wide), f32),
            pltpu.VMEM((groups, PAIRS * e2, wide), f32),
            pltpu.VMEM((groups, PAIRS * e2, wide), f32),
            pltpu.VMEM((groups, PAIRS * e3, wide), f32),
            pltpu.VMEM((groups, PAIRS * e3, wide), bf16),
            pltpu.VMEM((groups, PAIRS * e3, wide), bf16),
            pltpu.VMEM((groups, PAIRS * e2, wide), f32),
            pltpu.VMEM((groups, PAIRS * e2, wide), bf16),
            pltpu.VMEM((groups, PAIRS * e1, wide), f32),
            pltpu.VMEM((8 * atoms, slots), f32),
            pltpu.VMEM((4 * atoms, slots), f32),
            pltpu.VMEM((8 * atoms, slots), f32),
            pltpu.VMEM((atoms, prepared[10].shape[0]), bf16),
        ],
        compiler_params=pltpu.CompilerParams(vmem_limit_bytes=40 * 1024 * 1024),
        name="evaluate",
    )(rank, before, brick, after, own, *prepared)


def ring(size, step):
    return [(i, (i + step) % size) for i in range(size)]


def flip(size, bit):
    return [(i, i ^ bit) for i in range(size)]


def few(size):
    return size <= 8 and size & (size - 1) == 0


def from_others(value, size):
    return [value] + [lax.ppermute(value, "help", flip(size, k)) for k in range(1, size)]


def gather_help(value):
    size = lax.axis_size("help")
    rank = lax.axis_index("help")
    if not few(size):
        return lax.all_gather(value, "help", axis=1, tiled=True)
    blocks = from_others(value, size)
    bit = 1
    while len(blocks) > 1:
        upper = (rank & bit) != 0
        blocks = [
            jnp.where(
                upper, jnp.concatenate([b, a], axis=1), jnp.concatenate([a, b], axis=1)
            )
            for a, b in zip(blocks[::2], blocks[1::2])
        ]
        bit *= 2
    return blocks[0]


def sum_help(value):
    size = lax.axis_size("help")
    if not few(size):
        return lax.psum(value, "help")
    blocks = from_others(value, size)
    while len(blocks) > 1:
        blocks = [a + b for a, b in zip(blocks[::2], blocks[1::2])]
    return blocks[0]


def exchange(up, down):
    size = lax.axis_size("brick")
    if size % 2:
        return lax.ppermute(up, "brick", ring(size, 1)), lax.ppermute(down, "brick", ring(size, -1))
    odd = (lax.axis_index("brick") & 1) == 1
    inner = lax.ppermute(jnp.where(odd, down, up), "brick", flip(size, 1))
    pairs = [(i, (i + 1) % size if i % 2 else (i - 1) % size) for i in range(size)]
    outer = lax.ppermute(jnp.where(odd, up, down), "brick", pairs)
    return jnp.where(odd, inner, outer), jnp.where(odd, outer, inner)


def local(positions, velocities, forces_in, neighbors, *weights):
    prepared = prepare(neighbors, weights)
    atoms = positions.shape[1]
    rank = lax.axis_index("help")
    ranks = rank.reshape(1).astype(jnp.int32)
    at = rank * atoms
    speed = velocities + kick_scale * forces_in
    coords = positions + time_step * speed
    state = gather_help(jnp.concatenate([coords, speed], axis=0))
    state, prepared = lax.optimization_barrier((state, prepared))
    brick_pos, brick_speed = state[:3], state[3:]
    own = coords
    for md_step in range(STEPS):
        before, after = exchange(brick_pos, brick_pos)
        energy, to_before, to_brick, to_after = evaluate(
            ranks, before, brick_pos, after, own, prepared
        )
        from_before, from_after = exchange(to_after, to_before)
        force = sum_help(to_brick + from_before + from_after)
        brick_speed = brick_speed + kick_scale * force
        if md_step + 1 < STEPS:
            brick_speed = brick_speed + kick_scale * force
            brick_pos = brick_pos + time_step * brick_speed
            own = lax.dynamic_slice_in_dim(brick_pos, at, atoms, axis=1)
    out = lax.dynamic_slice_in_dim(
        jnp.concatenate([brick_speed, force], axis=0), at, atoms, axis=1
    )
    return (own, out[:3], energy.reshape(atoms), out[3:])


def solution(mesh):
    spread = ("brick", "help")
    cols = P(None, spread)
    return jax.shard_map(
        local,
        mesh=mesh,
        in_specs=(cols, cols, cols, P(spread, None)) + (P(),) * 11,
        out_specs=(cols, cols, P(spread), cols),
        check_vma=False,
    )
```

time: 77.2 us -> 66.8 us (0.87)
  Pallas kernels: 26.6 us -> 21.2 us
  starting transfers between devices: 26.4 us -> 24.1 us
  local copies, waits for them, and re-layouts: 8.44 us -> 6.43 us
  waiting for transfers between devices: 13.6 us -> 12.8 us
    pallas_call x2, Pallas kernels: 26.6 us -> 19.6 us  [evaluate(): pl.pallas_call(eval_kernel, out_shape=(jax.ShapeDtypeStruct((1, atoms), f...]
    ppermute x14 -> x17, starting transfers between devices: 26.4 us -> 24.1 us  [the longest x9 14.6 us: from_others(): lax.ppermute(value, 'help', flip(size, k))]
    pallas_call x0 -> x1, Pallas kernels: none -> 1.65 us  [prepare(): pl.pallas_call(prepare_kernel, out_shape=outs, in_specs=[pl.BlockSpec(mem...]
    unnamed x28 -> x22, local copies, waits for them, and re-layouts: 7.18 us -> 5.75 us
    ppermute x14 -> x17, waiting for transfers between devices: 13.6 us -> 12.8 us  [the longest x9 7 us: from_others(): lax.ppermute(value, 'help', flip(size, k))]
  transfers between devices with their start and end apart: 14 -> 17, of which waited for: 9 -> 8; matrix products, arithmetic and copies ran while one was open for 4% -> 6% of each run, Pallas kernels for 0% -> 2%
where the time goes in v3:
time: 66.8 us; the launch traced here: 66.4 us
  starting transfers between devices  24.1 us (36%)
  Pallas kernels  21.2 us (32%)
  waiting for transfers between devices  12.8 us (19%)
  local copies, waits for them, and re-layouts  6.43 us (10%)
  other arithmetic  1.18 us (2%)
  between operations  0.77 us (1%)
    pallas_call x2, Pallas kernels, evaluate(): pl.pallas_call(eval_kernel, out_shape=(jax.ShapeDtypeStruct((1, atoms), f...  19.6 us
    ppermute x9, starting transfers between devices, from_others(): lax.ppermute(value, 'help', flip(size, k))  14.6 us
    ppermute x4, starting transfers between devices, exchange(): outer = lax.ppermute(jnp.where(odd, up, down), 'brick', pairs)  9.39 us
    ppermute x9, waiting for transfers between devices, from_others(): lax.ppermute(value, 'help', flip(size, k))  7 us
    ppermute x4, waiting for transfers between devices, exchange(): outer = lax.ppermute(jnp.where(odd, up, down), 'brick', pairs)  5.77 us
    unnamed x22, local copies, waits for them, and re-layouts  5.75 us
    pallas_call x1, Pallas kernels, prepare(): pl.pallas_call(prepare_kernel, out_shape=outs, in_specs=[pl.BlockSpec(mem...  1.65 us
  transfers between devices with their start and end apart: 17, of which 8 were waited for; matrix products, arithmetic and copies ran while one was open for 6% of the time, Pallas kernels for 2%

profile of v3, /device:TPU:0, one launch (start us, length us, event | category | flops | bytes accessed | tf_op | source)
XLA Modules:
  0.0 66.4 jit_solution(17627582980777216154)
XLA Ops:
  0.6 0.7 %multiply_add_fusion.2 = (f32[3,64]{1,0:T(4,128)S(1)}, f32[3,64]{1,0:T(4,128)S(1)}) fusion(f32[3,64]{1,0:T(4,128)} %param.15, f32[3,64]{1,0:T(4,128)} %param.16, f32[3,64]{1,0:T(4,128)} %param.17), kind=kLoop, calls=%fused_computation.22 | loop fusion | flops 768 | bytes 3840 | tf_op jit(solution)/shard_map/add | solution.py:534
  1.4 5.1 %collective-permute-start = (f32[6,64]{1,0:T(8,128)S(1)}, f32[6,64]{1,0:T(8,128)S(1)}, u32[]{:S(2)}, u32[]{:S(2)}) collective-permute-start(f32[6,64]{1,0:T(8,128)S(1)} %pad_maximum_fusion), channel_id=1, source_target_pairs={{0,3},{1,2},{2,1},{3,0},{4,7},{5,6},{6,5},{7,4},{8,11},{9,10},{10,... | collective-permute-start | bytes 4616 | tf_op jit(solution)/shard_map/ppermute | solution.py:484
  6.5 0.6 collective-permute-start.2
  7.2 0.7 constant_dynamic-update-slice_fusion.6
  7.8 0.7 constant_dynamic-update-slice_fusion.5
  8.5 0.7 constant_dynamic-update-slice_fusion.4
  9.1 0.7 constant_dynamic-update-slice_fusion.3
  9.8 0.7 %constant_dynamic-update-slice_fusion.2 = f32[1280]{0:T(1024)S(1)} fusion(f32[1280]{0:T(1024)S(1)} %constant_dynamic-update-slice_fusion.3, f32[240]{0:T(256)} %param.26), kind=kLoop, calls=%fused_computation.10 | loop fusion | bytes 1984
  10.6 0.6 copy-done.3
  11.3 1.2 %copy-done = bf16[2048,240]{0,1:T(8,128)(2,1)S(1)} copy-done((bf16[2048,240]{0,1:T(8,128)(2,1)S(1)}, bf16[2048,240]{0,1:T(8,128)(2,1)}, u32[]{:S(2)}) %copy-start) | copy-done | bytes 983064
  12.5 1.7 %prepare.1 = (s32[64,128]{1,0:T(8,128)S(1)}, s32[64,128]{1,0:T(8,128)S(1)}, f32[32,128]{1,0:T(8,128)S(1)}, f32[32,128]{1,0:T(8,128)S(1)}, bf16[256,128]{1,0:T(8,...) custom-call(s32[64,128]{1,0:T(8,128)S(1)} %copy-done.2, ...), custom_call_target="tpu_custom_call" | custom-call | flops 4000000 | bytes 2500000 | tf_op jit(solution)/shard_map/prepare/pallas_call | solution.py:417
  14.4 2.7 %collective-permute-start.4 = (f32[3,256]{1,0:T(4,128)S(1)}, f32[3,256]{1,0:T(4,128)S(1)}, u32[]{:S(2)}, u32[]{:S(2)}) collective-permute-start(f32[3,256]{1,0:T(4,128)S(1)} %slice.12.brick_ref), channel_id=1, source_target_pairs={{0,28},{4,8},{8,4},{12,16},{16,12},{20,24},{24,20},{28,0},{1,29},{... | collective-permute-start | bytes 9224 | tf_op jit(solution)/shard_map/ppermute | solution.py:523
  17.2 1.3 %collective-permute-done.4 = f32[3,256]{1,0:T(4,128)S(1)} collective-permute-done((f32[3,256]{1,0:T(4,128)S(1)}, f32[3,256]{1,0:T(4,128)S(1)}, u32[]{:S(2)}, u32[]{:S(2)}) %collective-permute-start.4) | collective-permute-done | bytes 3104 | tf_op jit(solution)/shard_map/ppermute | solution.py:523
  18.4 9.8 %evaluate.2 = (f32[1,64]{1,0:T(1,128)}, f32[3,256]{1,0:T(4,128)S(1)}, f32[3,256]{1,0:T(4,128)S(1)}, f32[3,256]{1,0:T(4,128)S(1)}) custom-call(s32[1]{0:T(128)} %bitcast.1.rank_ref, f32[3,256]{1,0:T(4,128)S(1)} %get-tuple-element.91.before_ref, f32[3,256]{1,0:T(4,128)S(1)} %slice.12.brick_ref, f32[3,256]{1,0:T(4,128)S(1)} %get-tuple-element.90.after_ref, ...), custom_call_target="tpu_custom_call" | custom-call | tf_op jit(solution)/shard_map/evaluate/pallas_call | solution.py:442
  28.2 2.6 %collective-permute-start.6 = (f32[3,256]{1,0:T(4,128)S(1)}, f32[3,256]{1,0:T(4,128)S(1)}, u32[]{:S(2)}, u32[]{:S(2)}) collective-permute-start(f32[3,256]{1,0:T(4,128)S(1)} %get-tuple-element.89), channel_id=1, source_target_pairs={{0,28},{4,8},{8,4},{12,16},{16,12},{20,24},{24,20},{28,0},{1,29},{... | collective-permute-start | bytes 9224 | tf_op jit(solution)/shard_map/ppermute | solution.py:523
  30.8 1.3 %collective-permute-done.6 = f32[3,256]{1,0:T(4,128)S(1)} collective-permute-done((f32[3,256]{1,0:T(4,128)S(1)}, f32[3,256]{1,0:T(4,128)S(1)}, u32[]{:S(2)}, u32[]{:S(2)}) %collective-permute-start.6) | collective-permute-done | bytes 3104 | tf_op jit(solution)/shard_map/ppermute | solution.py:523
  32.2 1.4 %collective-permute-start.7 = (f32[3,256]{1,0:T(4,128)S(1)}, f32[3,256]{1,0:T(4,128)S(1)}, u32[]{:S(2)}, u32[]{:S(2)}) collective-permute-start(f32[3,256]{1,0:T(4,128)S(1)} %select_add_fusion.1), channel_id=1, source_target_pairs={{0,1},{1,0},{2,3},{3,2},{4,5},{5,4},{6,7},{7,6},{8,9},{9,8},{10,11... | collective-permute-start | bytes 9224 | tf_op jit(solution)/shard_map/ppermute | solution.py:484
  33.5 2.9 %collective-permute-start.8 = (f32[3,256]{1,0:T(4,128)S(1)}, f32[3,256]{1,0:T(4,128)S(1)}, u32[]{:S(2)}, u32[]{:S(2)}) collective-permute-start(f32[3,256]{1,0:T(4,128)S(1)} %select_add_fusion.1), channel_id=1, source_target_pairs={{0,2},{1,3},{2,0},{3,1},{4,6},{5,7},{6,4},{7,5},{8,10},{9,11},{10,... | collective-permute-start | bytes 9224 | tf_op jit(solution)/shard_map/ppermute | solution.py:484
  36.5 0.1 collective-permute-start.9
  36.6 1.5 %collective-permute-done.8 = f32[3,256]{1,0:T(4,128)S(1)} collective-permute-done((f32[3,256]{1,0:T(4,128)S(1)}, f32[3,256]{1,0:T(4,128)S(1)}, u32[]{:S(2)}, u32[]{:S(2)}) %collective-permute-start.8) | collective-permute-done | bytes 3104 | tf_op jit(solution)/shard_map/ppermute | solution.py:484
  38.1 3.8 %collective-permute-done.9 = f32[3,256]{1,0:T(4,128)S(1)} collective-permute-done((f32[3,256]{1,0:T(4,128)S(1)}, f32[3,256]{1,0:T(4,128)S(1)}, u32[]{:S(2)}, u32[]{:S(2)}) %collective-permute-start.9) | collective-permute-done | bytes 3104 | tf_op jit(solution)/shard_map/ppermute | solution.py:484
  42.0 2.1 %collective-permute-start.11 = (f32[3,256]{1,0:T(4,128)S(1)}, f32[3,256]{1,0:T(4,128)S(1)}, u32[]{:S(2)}, u32[]{:S(2)}) collective-permute-start(f32[3,256]{1,0:T(4,128)S(1)} %get-tuple-element.80.brick_ref), channel_id=1, source_target_pairs={{0,28},{4,8},{8,4},{12,16},{16,12},{20,24},{24,20},{28,0},{1,29},{... | collective-permute-start | bytes 9224 | tf_op jit(solution)/shard_map/ppermute | solution.py:523
  44.2 0.5 copy-done.5
  44.7 1.3 %collective-permute-done.11 = f32[3,256]{1,0:T(4,128)S(1)} collective-permute-done((f32[3,256]{1,0:T(4,128)S(1)}, f32[3,256]{1,0:T(4,128)S(1)}, u32[]{:S(2)}, u32[]{:S(2)}) %collective-permute-start.11) | collective-permute-done | bytes 3104 | tf_op jit(solution)/shard_map/ppermute | solution.py:523
  46.0 9.8 %evaluate.3 = (f32[1,64]{1,0:T(1,128)}, f32[3,256]{1,0:T(4,128)S(1)}, f32[3,256]{1,0:T(4,128)S(1)}, f32[3,256]{1,0:T(4,128)S(1)}) custom-call(s32[1]{0:T(128)} %bitcast.1.rank_ref, f32[3,256]{1,0:T(4,128)S(1)} %get-tuple-element.87.before_ref, f32[3,256]{1,0:T(4,128)S(1)} %get-tuple-element.80.brick_ref, f32[3,256]{1,0:T(4,128)S(1)} %get-tuple-element.86.after_ref, ...), custom_call_target="tpu_custom_call" | custom-call | tf_op jit(solution)/shard_map/evaluate/pallas_call | solution.py:442
  55.8 2.0 %collective-permute-start.13 = (f32[3,256]{1,0:T(4,128)S(1)}, f32[3,256]{1,0:T(4,128)S(1)}, u32[]{:S(2)}, u32[]{:S(2)}) collective-permute-start(f32[3,256]{1,0:T(4,128)S(1)} %get-tuple-element.85), channel_id=1, source_target_pairs={{0,28},{4,8},{8,4},{12,16},{16,12},{20,24},{24,20},{28,0},{1,29},{... | collective-permute-start | bytes 9224 | tf_op jit(solution)/shard_map/ppermute | solution.py:523
  57.8 1.9 %collective-permute-done.13 = f32[3,256]{1,0:T(4,128)S(1)} collective-permute-done((f32[3,256]{1,0:T(4,128)S(1)}, f32[3,256]{1,0:T(4,128)S(1)}, u32[]{:S(2)}, u32[]{:S(2)}) %collective-permute-start.13) | collective-permute-done | bytes 3104 | tf_op jit(solution)/shard_map/ppermute | solution.py:523
  59.7 0.7 %collective-permute-start.15 = (f32[3,256]{1,0:T(4,128)S(1)}, f32[3,256]{1,0:T(4,128)S(1)}, u32[]{:S(2)}, u32[]{:S(2)}) collective-permute-start(f32[3,256]{1,0:T(4,128)S(1)} %select_add_fusion), channel_id=1, source_target_pairs={{0,2},{1,3},{2,0},{3,1},{4,6},{5,7},{6,4},{7,5},{8,10},{9,11},{10,... | collective-permute-start | bytes 9224 | tf_op jit(solution)/shard_map/ppermute | solution.py:484
  60.4 3.7 %collective-permute-start.16 = (f32[3,256]{1,0:T(4,128)S(1)}, f32[3,256]{1,0:T(4,128)S(1)}, u32[]{:S(2)}, u32[]{:S(2)}) collective-permute-start(f32[3,256]{1,0:T(4,128)S(1)} %select_add_fusion), channel_id=1, source_target_pairs={{0,3},{1,2},{2,1},{3,0},{4,7},{5,6},{6,5},{7,4},{8,11},{9,10},{10,... | collective-permute-start | bytes 9224 | tf_op jit(solution)/shard_map/ppermute | solution.py:484
  64.1 0.2 collective-permute-done.15
  64.3 1.5 %collective-permute-done.16 = f32[3,256]{1,0:T(4,128)S(1)} collective-permute-done((f32[3,256]{1,0:T(4,128)S(1)}, f32[3,256]{1,0:T(4,128)S(1)}, u32[]{:S(2)}, u32[]{:S(2)}) %collective-permute-start.16) | collective-permute-done | bytes 3104 | tf_op jit(solution)/shard_map/ppermute | solution.py:484
  65.9 0.6 fusion.1
  (49 shorter events, 0.8 us)
Async XLA Ops:
  0.6 10.0 %copy-start.2 = (s32[64,128]{1,0:T(8,128)S(1)}, s32[64,128]{1,0:T(8,128)}, u32[]{:S(2)}) copy-start(s32[64,128]{1,0:T(8,128)} %refs_0_.1) | copy-start | bytes 98308
  1.4 12.9 %collective-permute-start = (f32[6,64]{1,0:T(8,128)S(1)}, f32[6,64]{1,0:T(8,128)S(1)}, u32[]{:S(2)}, u32[]{:S(2)}) collective-permute-start(f32[6,64]{1,0:T(8,128)S(1)} %pad_maximum_fusion), channel_id=1, source_target_pairs={{0,3},{1,2},{2,1},{3,0},{4,7},{5,6},{6,5},{7,4},{8,11},{9,10},{10,... | collective-permute-start | bytes 4616 | tf_op jit(solution)/shard_map/ppermute | solution.py:484
  6.5 7.7 %collective-permute-start.1 = (f32[6,64]{1,0:T(8,128)S(1)}, f32[6,64]{1,0:T(8,128)S(1)}, u32[]{:S(2)}, u32[]{:S(2)}) collective-permute-start(f32[6,64]{1,0:T(8,128)S(1)} %pad_maximum_fusion), channel_id=1, source_target_pairs={{0,2},{1,3},{2,0},{3,1},{4,6},{5,7},{6,4},{7,5},{8,10},{9,11},{10,... | collective-permute-start | bytes 4616 | tf_op jit(solution)/shard_map/ppermute | solution.py:484
  6.5 7.6 %collective-permute-start.2 = (f32[6,64]{1,0:T(8,128)S(1)}, f32[6,64]{1,0:T(8,128)S(1)}, u32[]{:S(2)}, u32[]{:S(2)}) collective-permute-start(f32[6,64]{1,0:T(8,128)S(1)} %pad_maximum_fusion), channel_id=1, source_target_pairs={{0,1},{1,0},{2,3},{3,2},{4,5},{5,4},{6,7},{7,6},{8,9},{9,8},{10,11... | collective-permute-start | bytes 4616 | tf_op jit(solution)/shard_map/ppermute | solution.py:484
  9.8 0.7 %copy-start.6 = (f32[240]{0:T(256)S(1)}, f32[240]{0:T(256)}, u32[]{:S(2)}) copy-start(f32[240]{0:T(256)} %param.28) | copy-start | bytes 2884
  9.8 0.7 %copy-start.7 = (f32[240]{0:T(256)S(1)}, f32[240]{0:T(256)}, u32[]{:S(2)}) copy-start(f32[240]{0:T(256)} %param.29) | copy-start | bytes 2884
  10.5 0.7 %copy-start.3 = (bf16[64,128]{1,0:T(8,128)(2,1)S(1)}, bf16[64,128]{1,0:T(8,128)(2,1)}, u32[]{:S(2)}) copy-start(bf16[64,128]{1,0:T(8,128)(2,1)} %refs_2_.1) | copy-start | bytes 49156
  10.6 0.7 %copy-start.4 = (bf16[32,64]{1,0:T(8,128)(2,1)S(1)}, bf16[32,64]{1,0:T(8,128)(2,1)}, u32[]{:S(2)}) copy-start(bf16[32,64]{1,0:T(8,128)(2,1)} %refs_1_.1) | copy-start | bytes 12292
  11.3 1.2 %copy-start = (bf16[2048,240]{0,1:T(8,128)(2,1)S(1)}, bf16[2048,240]{0,1:T(8,128)(2,1)}, u32[]{:S(2)}) copy-start(bf16[2048,240]{0,1:T(8,128)(2,1)} %param.25) | copy-start | bytes 2949124
  12.5 6.0 %copy-start.1 = (bf16[240,240]{1,0:T(8,128)(2,1)S(1)}, bf16[240,240]{1,0:T(8,128)(2,1)}, u32[]{:S(2)}) copy-start(bf16[240,240]{1,0:T(8,128)(2,1)} %f2_ref.1) | copy-start | bytes 345604
  14.3 2.8 %collective-permute-start.3 = (f32[3,256]{1,0:T(4,128)S(1)}, f32[3,256]{1,0:T(4,128)S(1)}, u32[]{:S(2)}, u32[]{:S(2)}) collective-permute-start(f32[3,256]{1,0:T(4,128)S(1)} %slice.12.brick_ref), channel_id=1, source_target_pairs={{0,4},{4,0},{8,12},{12,8},{16,20},{20,16},{24,28},{28,24},{1,5},{5... | collective-permute-start | bytes 9224 | tf_op jit(solution)/shard_map/ppermute | solution.py:521
  14.4 4.0 %collective-permute-start.4 = (f32[3,256]{1,0:T(4,128)S(1)}, f32[3,256]{1,0:T(4,128)S(1)}, u32[]{:S(2)}, u32[]{:S(2)}) collective-permute-start(f32[3,256]{1,0:T(4,128)S(1)} %slice.12.brick_ref), channel_id=1, source_target_pairs={{0,28},{4,8},{8,4},{12,16},{16,12},{20,24},{24,20},{28,0},{1,29},{... | collective-permute-start | bytes 9224 | tf_op jit(solution)/shard_map/ppermute | solution.py:523
  28.2 2.6 %collective-permute-start.5 = (f32[3,256]{1,0:T(4,128)S(1)}, f32[3,256]{1,0:T(4,128)S(1)}, u32[]{:S(2)}, u32[]{:S(2)}) collective-permute-start(f32[3,256]{1,0:T(4,128)S(1)} %get-tuple-element.88), channel_id=1, source_target_pairs={{0,4},{4,0},{8,12},{12,8},{16,20},{20,16},{24,28},{28,24},{1,5},{5... | collective-permute-start | bytes 9224 | tf_op jit(solution)/shard_map/ppermute | solution.py:521
  28.2 3.9 %collective-permute-start.6 = (f32[3,256]{1,0:T(4,128)S(1)}, f32[3,256]{1,0:T(4,128)S(1)}, u32[]{:S(2)}, u32[]{:S(2)}) collective-permute-start(f32[3,256]{1,0:T(4,128)S(1)} %get-tuple-element.89), channel_id=1, source_target_pairs={{0,28},{4,8},{8,4},{12,16},{16,12},{20,24},{24,20},{28,0},{1,29},{... | collective-permute-start | bytes 9224 | tf_op jit(solution)/shard_map/ppermute | solution.py:523
  32.2 4.4 %collective-permute-start.7 = (f32[3,256]{1,0:T(4,128)S(1)}, f32[3,256]{1,0:T(4,128)S(1)}, u32[]{:S(2)}, u32[]{:S(2)}) collective-permute-start(f32[3,256]{1,0:T(4,128)S(1)} %select_add_fusion.1), channel_id=1, source_target_pairs={{0,1},{1,0},{2,3},{3,2},{4,5},{5,4},{6,7},{7,6},{8,9},{9,8},{10,11... | collective-permute-start | bytes 9224 | tf_op jit(solution)/shard_map/ppermute | solution.py:484
  33.5 4.5 %collective-permute-start.8 = (f32[3,256]{1,0:T(4,128)S(1)}, f32[3,256]{1,0:T(4,128)S(1)}, u32[]{:S(2)}, u32[]{:S(2)}) collective-permute-start(f32[3,256]{1,0:T(4,128)S(1)} %select_add_fusion.1), channel_id=1, source_target_pairs={{0,2},{1,3},{2,0},{3,1},{4,6},{5,7},{6,4},{7,5},{8,10},{9,11},{10,... | collective-permute-start | bytes 9224 | tf_op jit(solution)/shard_map/ppermute | solution.py:484
  36.5 5.4 %collective-permute-start.9 = (f32[3,256]{1,0:T(4,128)S(1)}, f32[3,256]{1,0:T(4,128)S(1)}, u32[]{:S(2)}, u32[]{:S(2)}) collective-permute-start(f32[3,256]{1,0:T(4,128)S(1)} %select_add_fusion.1), channel_id=1, source_target_pairs={{0,3},{1,2},{2,1},{3,0},{4,7},{5,6},{6,5},{7,4},{8,11},{9,10},{10,... | collective-permute-start | bytes 9224 | tf_op jit(solution)/shard_map/ppermute | solution.py:484
  41.9 2.8 %collective-permute-start.10 = (f32[3,256]{1,0:T(4,128)S(1)}, f32[3,256]{1,0:T(4,128)S(1)}, u32[]{:S(2)}, u32[]{:S(2)}) collective-permute-start(f32[3,256]{1,0:T(4,128)S(1)} %get-tuple-element.80.brick_ref), channel_id=1, source_target_pairs={{0,4},{4,0},{8,12},{12,8},{16,20},{20,16},{24,28},{28,24},{1,5},{5... | collective-permute-start | bytes 9224 | tf_op jit(solution)/shard_map/ppermute | solution.py:521
  42.0 4.0 %collective-permute-start.11 = (f32[3,256]{1,0:T(4,128)S(1)}, f32[3,256]{1,0:T(4,128)S(1)}, u32[]{:S(2)}, u32[]{:S(2)}) collective-permute-start(f32[3,256]{1,0:T(4,128)S(1)} %get-tuple-element.80.brick_ref), channel_id=1, source_target_pairs={{0,28},{4,8},{8,4},{12,16},{16,12},{20,24},{24,20},{28,0},{1,29},{... | collective-permute-start | bytes 9224 | tf_op jit(solution)/shard_map/ppermute | solution.py:523
  44.1 0.6 copy-start.5
  55.7 2.0 %collective-permute-start.12 = (f32[3,256]{1,0:T(4,128)S(1)}, f32[3,256]{1,0:T(4,128)S(1)}, u32[]{:S(2)}, u32[]{:S(2)}) collective-permute-start(f32[3,256]{1,0:T(4,128)S(1)} %get-tuple-element.84), channel_id=1, source_target_pairs={{0,4},{4,0},{8,12},{12,8},{16,20},{20,16},{24,28},{28,24},{1,5},{5... | collective-permute-start | bytes 9224 | tf_op jit(solution)/shard_map/ppermute | solution.py:521
  55.8 3.9 %collective-permute-start.13 = (f32[3,256]{1,0:T(4,128)S(1)}, f32[3,256]{1,0:T(4,128)S(1)}, u32[]{:S(2)}, u32[]{:S(2)}) collective-permute-start(f32[3,256]{1,0:T(4,128)S(1)} %get-tuple-element.85), channel_id=1, source_target_pairs={{0,28},{4,8},{8,4},{12,16},{16,12},{20,24},{24,20},{28,0},{1,29},{... | collective-permute-start | bytes 9224 | tf_op jit(solution)/shard_map/ppermute | solution.py:523
  59.7 4.4 %collective-permute-start.14 = (f32[3,256]{1,0:T(4,128)S(1)}, f32[3,256]{1,0:T(4,128)S(1)}, u32[]{:S(2)}, u32[]{:S(2)}) collective-permute-start(f32[3,256]{1,0:T(4,128)S(1)} %select_add_fusion), channel_id=1, source_target_pairs={{0,1},{1,0},{2,3},{3,2},{4,5},{5,4},{6,7},{7,6},{8,9},{9,8},{10,11... | collective-permute-start | bytes 9224 | tf_op jit(solution)/shard_map/ppermute | solution.py:484
  59.7 4.6 %collective-permute-start.15 = (f32[3,256]{1,0:T(4,128)S(1)}, f32[3,256]{1,0:T(4,128)S(1)}, u32[]{:S(2)}, u32[]{:S(2)}) collective-permute-start(f32[3,256]{1,0:T(4,128)S(1)} %select_add_fusion), channel_id=1, source_target_pairs={{0,2},{1,3},{2,0},{3,1},{4,6},{5,7},{6,4},{7,5},{8,10},{9,11},{10,... | collective-permute-start | bytes 9224 | tf_op jit(solution)/shard_map/ppermute | solution.py:484
  60.4 5.4 %collective-permute-start.16 = (f32[3,256]{1,0:T(4,128)S(1)}, f32[3,256]{1,0:T(4,128)S(1)}, u32[]{:S(2)}, u32[]{:S(2)}) collective-permute-start(f32[3,256]{1,0:T(4,128)S(1)} %select_add_fusion), channel_id=1, source_target_pairs={{0,3},{1,2},{2,1},{3,0},{4,7},{5,6},{6,5},{7,4},{8,11},{9,10},{10,... | collective-permute-start | bytes 9224 | tf_op jit(solution)/shard_map/ppermute | solution.py:484

commit v4 on v3

--- a/solution.py
+++ b/solution.py
@@ -28,6 +28,14 @@
 def split2(x):
     high = x.astype(bf16).astype(f32)
     return high, x - high
+
+
+def column(row):
+    size = row.shape[1]
+    shape = (size, size)
+    same = lax.broadcasted_iota(jnp.int32, shape, 0) == lax.broadcasted_iota(jnp.int32, shape, 1)
+    picked = jnp.sum(jnp.where(same, jnp.broadcast_to(row, shape), 0.0), axis=1, keepdims=True)
+    return jnp.broadcast_to(picked, (size, LANES))
 
 
 def eval_kernel(
@@ -55,6 +63,8 @@
     to_before_ref,
     to_brick_ref,
     to_after_ref,
+    b2_s,
+    b3_s,
     s_s,
     r_s,
     t_s,
@@ -76,9 +86,9 @@
     atoms, slots = low_ref.shape
     brick_len = brick_ref.shape[1]
     per = brick_len // LANES
-    e1 = w1_ref.shape[0]
-    e2 = b2_ref.shape[0] // PAIRS
-    e3 = b3_ref.shape[0] // PAIRS
+    e1 = w1_ref.shape[1]
+    e2 = b2_ref.shape[1]
+    e3 = b3_ref.shape[1]
     m2 = f1_ref.shape[0] // e3
     inv_slots = 1.0 / slots
     pairs = atoms // 2
@@ -122,8 +132,10 @@
     groups = atoms // GROUP
     wide = 2 * slots
     half = 2 * e3
-    w1 = w1_ref[...]
-    b1 = b1_ref[...]
+    w1 = column(w1_ref[...])
+    b1 = column(b1_ref[...])
+    b2_s[...] = jnp.concatenate([column(b2_ref[...])] * PAIRS, axis=0)
+    b3_s[...] = jnp.concatenate([column(b3_ref[...])] * PAIRS, axis=0)
     row16 = lax.broadcasted_iota(jnp.int32, (16, LANES), 0)
     row32 = lax.broadcasted_iota(jnp.int32, (32, LANES), 0)
 
@@ -166,13 +178,13 @@
 
     def second_layer(j):
         h1 = h1_s[j]
-        t2 = jnp.tanh(mm(w2t_ref[...], h1.astype(bf16)) + twice(b2_ref[...]))
+        t2 = jnp.tanh(mm(w2t_ref[...], h1.astype(bf16)) + twice(b2_s[...]))
         h2_s[j] = stacked(h1, e1, 2) + t2
         u2_s[j] = 1.0 - t2 * t2
 
     def third_layer(j):
         h2 = h2_s[j]
-        t3 = jnp.tanh(mm(w3t_ref[...], h2.astype(bf16)) + twice(b3_ref[...]))
+        t3 = jnp.tanh(mm(w3t_ref[...], h2.astype(bf16)) + twice(b3_s[...]))
         g_s[j] = (stacked(h2, e2, 2) + t3).astype(bf16)
         u3_s[j] = 1.0 - t3 * t3
 
@@ -323,14 +335,6 @@
         target[...] = whole + placed if part == 1 else whole
 
 
-def column(row):
-    size = row.shape[1]
-    shape = (size, size)
-    same = lax.broadcasted_iota(jnp.int32, shape, 0) == lax.broadcasted_iota(jnp.int32, shape, 1)
-    picked = jnp.sum(jnp.where(same, jnp.broadcast_to(row, shape), 0.0), axis=1, keepdims=True)
-    return jnp.broadcast_to(picked, (size, LANES))
-
-
 def diagonal(target, block, copies):
     tall, long = block.shape
     target[...] = jnp.zeros(target.shape, target.dtype)
@@ -339,44 +343,27 @@
 
 
 def prepare_kernel(*refs):
-    count = 5
+    count = 4
     raw = refs[:count]
-    low_o, high_o, w1_o, b1_o, w2t_o, w2_o, b2_o, w3t_o, w3_o, b3_o, f1_o, c1_o, c2_o, out_o = refs[
-        count : count + 14
-    ]
-    here = refs[count + 14 : 2 * count + 14]
-    wide_s, sems = refs[2 * count + 14 :]
+    low_o, high_o, w2t_o, w2_o, w3t_o, w3_o, f1_o = refs[count : count + 7]
+    here = refs[count + 7 : 2 * count + 7]
+    wide_s, sems = refs[2 * count + 7 :]
     copies = [pltpu.make_async_copy(raw[i], here[i], sems.at[i]) for i in range(count)]
     for copy in copies:
         copy.start()
     for copy in copies:
         copy.wait()
-    nbr, w2, w3, f1, small = here
+    nbr, w2, w3, f1 = here
     index = nbr[...]
     low_o[...] = index & (LANES - 1)
     high_o[...] = lax.shift_right_arithmetic(index, 7)
-    e1, e2 = w2.shape
     e3 = w3.shape[1]
-    fit = f1.shape[0]
-    rows = f1.shape[1]
+    fit, rows = f1.shape
     m2 = rows // e3
-    vectors = []
-    start = 0
-    for size in (e1, e1, e2, e3, fit, fit, fit):
-        vectors.append(small[:, start : start + size])
-        start += size + -size % LANES
-    w1, b1, b2, b3, c1, c2, out = vectors
-    w1_o[...] = column(w1)
-    b1_o[...] = column(b1)
-    b2_o[...] = jnp.concatenate([column(b2)] * PAIRS, axis=0)
-    b3_o[...] = jnp.concatenate([column(b3)] * PAIRS, axis=0)
     diagonal(w2_o, w2[...], PAIRS)
     diagonal(w3_o, w3[...], PAIRS // 2)
     diagonal(w2t_o, w2[...].astype(f32).T.astype(bf16), PAIRS)
     diagonal(w3t_o, w3[...].astype(f32).T.astype(bf16), PAIRS)
-    c1_o[...] = c1
-    c2_o[...] = c2
-    out_o[...] = out
     for part in range(0, fit, LANES):
         upto = min(LANES, fit - part)
         for start in range(0, rows, LANES):
@@ -393,26 +380,16 @@
     w1, b1, w2, b2, w3, b3, f1, c1, f2, c2, out = weights
     e1, e2, e3 = w1.shape[0], w2.shape[1], w3.shape[1]
     fit = out.shape[0]
-    small = jnp.concatenate(
-        [jnp.pad(v, (0, -v.shape[0] % LANES)) for v in (w1, b1, b2, b3, c1, c2, out)]
-    )
-    raw = (neighbors, w2, w3, f1.T, small[None])
+    raw = (neighbors, w2, w3, f1.T)
     shape = jax.ShapeDtypeStruct
     outs = (
         shape(neighbors.shape, jnp.int32),
         shape(neighbors.shape, jnp.int32),
-        shape((e1, LANES), f32),
-        shape((e1, LANES), f32),
         shape((PAIRS * e2, PAIRS * e1), bf16),
         shape((PAIRS * e1, PAIRS * e2), bf16),
-        shape((PAIRS * e2, LANES), f32),
         shape((PAIRS * e3, PAIRS * e2), bf16),
         shape((PAIRS // 2 * e2, PAIRS // 2 * e3), bf16),
-        shape((PAIRS * e3, LANES), f32),
         shape((f1.shape[0], fit), bf16),
-        shape((1, fit), f32),
-        shape((1, fit), f32),
-        shape((1, fit), f32),
     )
     made = pl.pallas_call(
         prepare_kernel,
@@ -425,15 +402,30 @@
         cost_estimate=pl.CostEstimate(flops=4_000_000, bytes_accessed=2_500_000, transcendentals=0),
         name="prepare",
     )(*raw)
-    return (*made[:12], f2, *made[12:])
+    low, high, w2t, w2, w3t, w3, f1 = made
+    return (
+        low,
+        high,
+        w1[None],
+        b1[None],
+        w2t,
+        w2,
+        b2[None],
+        w3t,
+        w3,
+        b3[None],
+        f1,
+        c1[None],
+        f2,
+        c2[None],
+        out[None],
+    )
 
 
 def evaluate(rank, before, brick, after, own, prepared):
     atoms, slots = prepared[0].shape
     brick_len = brick.shape[1]
-    e1 = prepared[2].shape[0]
-    e2 = prepared[4].shape[0] // PAIRS
-    e3 = prepared[7].shape[0] // PAIRS
+    e1, e2, e3 = (prepared[i].shape[1] for i in (2, 6, 9))
     groups = atoms // GROUP
     wide = 2 * slots
     own = jnp.concatenate([own, own], axis=1)[:, :LANES]
@@ -445,6 +437,8 @@
         in_specs=[pl.BlockSpec(memory_space=pltpu.SMEM)] + [vmem] * (4 + len(prepared)),
         out_specs=[vmem] * 4,
         scratch_shapes=[
+            pltpu.VMEM((PAIRS * e2, LANES), f32),
+            pltpu.VMEM((PAIRS * e3, LANES), f32),
             pltpu.VMEM((atoms, slots), f32),
             pltpu.VMEM((4 * atoms, slots), f32),
             pltpu.VMEM((4 * atoms, e3), f32),
@@ -533,7 +527,8 @@
     speed = velocities + kick_scale * forces_in
     coords = positions + time_step * speed
     state = gather_help(jnp.concatenate([coords, speed], axis=0))
-    state, prepared = lax.optimization_barrier((state, prepared))
+    state, made = lax.optimization_barrier((state, prepared[:2]))
+    prepared = (*made, *prepared[2:])
     brick_pos, brick_speed = state[:3], state[3:]
     own = coords
     for md_step in range(STEPS):

time: 66.8 us -> 64.8 us (0.970)
  local copies, waits for them, and re-layouts: 6.43 us -> 4.5 us
    unnamed x22 -> x26, local copies, waits for them, and re-layouts: 5.75 us -> 3.83 us
  transfers between devices with their start and end apart: 17 -> 17, of which waited for: 8 -> 8; matrix products, arithmetic and copies ran while one was open for 6% -> 0% of each run, Pallas kernels for 2% -> 3%
where the time goes in v4:
time: 64.8 us; the launch traced here: 64.5 us
  starting transfers between devices  23.8 us (37%)
  Pallas kernels  21.2 us (33%)
  waiting for transfers between devices  13 us (20%)
  local copies, waits for them, and re-layouts  4.5 us (7%)
  other arithmetic  1.17 us (2%)
  between operations  0.76 us (1%)
    pallas_call x2, Pallas kernels, evaluate(): pl.pallas_call(eval_kernel, out_shape=(jax.ShapeDtypeStruct((1, atoms), f...  19.6 us
    ppermute x9, starting transfers between devices, from_others(): lax.ppermute(value, 'help', flip(size, k))  14.5 us
    ppermute x4, starting transfers between devices, exchange(): outer = lax.ppermute(jnp.where(odd, up, down), 'brick', pairs)  9.13 us
    ppermute x9, waiting for transfers between devices, from_others(): lax.ppermute(value, 'help', flip(size, k))  7.03 us
    ppermute x4, waiting for transfers between devices, exchange(): outer = lax.ppermute(jnp.where(odd, up, down), 'brick', pairs)  6 us
    unnamed x26, local copies, waits for them, and re-layouts  3.83 us
    pallas_call x1, Pallas kernels, prepare(): pl.pallas_call(prepare_kernel, out_shape=outs, in_specs=[pl.BlockSpec(mem...  1.62 us
  transfers between devices with their start and end apart: 17, of which 8 were waited for; matrix products, arithmetic and copies ran while one was open for 0% of the time, Pallas kernels for 3%

profile of v4, /device:TPU:0, one launch (start us, length us, event | category | flops | bytes accessed | tf_op | source)
XLA Modules:
  0.0 64.5 jit_solution(4857622001383455903)
XLA Ops:
  0.6 0.7 %multiply_add_fusion.2 = (f32[3,64]{1,0:T(4,128)S(1)}, f32[3,64]{1,0:T(4,128)S(1)}) fusion(f32[3,64]{1,0:T(4,128)} %param.15, f32[3,64]{1,0:T(4,128)} %param.16, f32[3,64]{1,0:T(4,128)} %param.17), kind=kLoop, calls=%fused_computation.15 | loop fusion | flops 768 | bytes 3840 | tf_op jit(solution)/shard_map/add | solution.py:528
  1.4 3.1 %collective-permute-start.2 = (f32[6,64]{1,0:T(8,128)S(1)}, f32[6,64]{1,0:T(8,128)S(1)}, u32[]{:S(2)}, u32[]{:S(2)}) collective-permute-start(f32[6,64]{1,0:T(8,128)S(1)} %pad_maximum_fusion), channel_id=1, source_target_pairs={{0,1},{1,0},{2,3},{3,2},{4,5},{5,4},{6,7},{7,6},{8,9},{9,8},{10,11... | collective-permute-start | bytes 4616 | tf_op jit(solution)/shard_map/ppermute | solution.py:478
  4.5 2.5 %collective-permute-start = (f32[6,64]{1,0:T(8,128)S(1)}, f32[6,64]{1,0:T(8,128)S(1)}, u32[]{:S(2)}, u32[]{:S(2)}) collective-permute-start(f32[6,64]{1,0:T(8,128)S(1)} %pad_maximum_fusion), channel_id=1, source_target_pairs={{0,3},{1,2},{2,1},{3,0},{4,7},{5,6},{6,5},{7,4},{8,11},{9,10},{10,... | collective-permute-start | bytes 4616 | tf_op jit(solution)/shard_map/ppermute | solution.py:478
  7.0 0.1 collective-permute-start.1
  7.1 1.2 %copy-done = bf16[2048,240]{0,1:T(8,128)(2,1)S(1)} copy-done((bf16[2048,240]{0,1:T(8,128)(2,1)S(1)}, bf16[2048,240]{0,1:T(8,128)(2,1)}, u32[]{:S(2)}) %copy-start) | copy-done | bytes 983064
  8.3 0.7 %copy-done.3 = bf16[64,128]{1,0:T(8,128)(2,1)S(1)} copy-done((bf16[64,128]{1,0:T(8,128)(2,1)S(1)}, bf16[64,128]{1,0:T(8,128)(2,1)}, u32[]{:S(2)}) %copy-start.3) | copy-done | bytes 16408
  9.0 0.7 %copy-done.4 = bf16[32,64]{1,0:T(8,128)(2,1)S(1)} copy-done((bf16[32,64]{1,0:T(8,128)(2,1)S(1)}, bf16[32,64]{1,0:T(8,128)(2,1)}, u32[]{:S(2)}) %copy-start.4) | copy-done | bytes 4120
  9.7 1.6 %prepare.1 = (s32[64,128]{1,0:T(8,128)S(1)}, s32[64,128]{1,0:T(8,128)S(1)}, bf16[256,128]{1,0:T(8,128)(2,1)S(1)}, bf16[128,256]{1,0:T(8,128)(2,1)S(1)}, bf16[512...) custom-call(s32[64,128]{1,0:T(8,128)S(1)} %copy-done.2, ...), custom_call_target="tpu_custom_call" | custom-call | flops 4000000 | bytes 2500000 | tf_op jit(solution)/shard_map/prepare/pallas_call | solution.py:394
  11.3 0.1 maximum_select_fusion.2
  11.6 2.5 %collective-permute-start.4 = (f32[3,256]{1,0:T(4,128)S(1)}, f32[3,256]{1,0:T(4,128)S(1)}, u32[]{:S(2)}, u32[]{:S(2)}) collective-permute-start(f32[3,256]{1,0:T(4,128)S(1)} %slice.12.brick_ref), channel_id=1, source_target_pairs={{0,28},{4,8},{8,4},{12,16},{16,12},{20,24},{24,20},{28,0},{1,29},{... | collective-permute-start | bytes 9224 | tf_op jit(solution)/shard_map/ppermute | solution.py:517
  14.3 1.4 %collective-permute-done.4 = f32[3,256]{1,0:T(4,128)S(1)} collective-permute-done((f32[3,256]{1,0:T(4,128)S(1)}, f32[3,256]{1,0:T(4,128)S(1)}, u32[]{:S(2)}, u32[]{:S(2)}) %collective-permute-start.4) | collective-permute-done | bytes 3104 | tf_op jit(solution)/shard_map/ppermute | solution.py:517
  15.7 0.6 copy-done.6
  16.4 9.8 %evaluate.2 = (f32[1,64]{1,0:T(1,128)}, f32[3,256]{1,0:T(4,128)S(1)}, f32[3,256]{1,0:T(4,128)S(1)}, f32[3,256]{1,0:T(4,128)S(1)}) custom-call(s32[1]{0:T(128)} %bitcast.1.rank_ref, f32[3,256]{1,0:T(4,128)S(1)} %get-tuple-element.51.before_ref, f32[3,256]{1,0:T(4,128)S(1)} %slice.12.brick_ref, f32[3,256]{1,0:T(4,128)S(1)} %get-tuple-element.50.after_ref, ...), custom_call_target="tpu_custom_call" | custom-call | tf_op jit(solution)/shard_map/evaluate/pallas_call | solution.py:434
  26.2 2.5 %collective-permute-start.6 = (f32[3,256]{1,0:T(4,128)S(1)}, f32[3,256]{1,0:T(4,128)S(1)}, u32[]{:S(2)}, u32[]{:S(2)}) collective-permute-start(f32[3,256]{1,0:T(4,128)S(1)} %get-tuple-element.49), channel_id=1, source_target_pairs={{0,28},{4,8},{8,4},{12,16},{16,12},{20,24},{24,20},{28,0},{1,29},{... | collective-permute-start | bytes 9224 | tf_op jit(solution)/shard_map/ppermute | solution.py:517
  28.7 1.4 %collective-permute-done.6 = f32[3,256]{1,0:T(4,128)S(1)} collective-permute-done((f32[3,256]{1,0:T(4,128)S(1)}, f32[3,256]{1,0:T(4,128)S(1)}, u32[]{:S(2)}, u32[]{:S(2)}) %collective-permute-start.6) | collective-permute-done | bytes 3104 | tf_op jit(solution)/shard_map/ppermute | solution.py:517
  30.2 1.8 %collective-permute-start.7 = (f32[3,256]{1,0:T(4,128)S(1)}, f32[3,256]{1,0:T(4,128)S(1)}, u32[]{:S(2)}, u32[]{:S(2)}) collective-permute-start(f32[3,256]{1,0:T(4,128)S(1)} %select_add_fusion.1), channel_id=1, source_target_pairs={{0,1},{1,0},{2,3},{3,2},{4,5},{5,4},{6,7},{7,6},{8,9},{9,8},{10,11... | collective-permute-start | bytes 9224 | tf_op jit(solution)/shard_map/ppermute | solution.py:478
  31.9 1.7 %collective-permute-start.8 = (f32[3,256]{1,0:T(4,128)S(1)}, f32[3,256]{1,0:T(4,128)S(1)}, u32[]{:S(2)}, u32[]{:S(2)}) collective-permute-start(f32[3,256]{1,0:T(4,128)S(1)} %select_add_fusion.1), channel_id=1, source_target_pairs={{0,2},{1,3},{2,0},{3,1},{4,6},{5,7},{6,4},{7,5},{8,10},{9,11},{10,... | collective-permute-start | bytes 9224 | tf_op jit(solution)/shard_map/ppermute | solution.py:478
  33.6 0.9 %collective-permute-start.9 = (f32[3,256]{1,0:T(4,128)S(1)}, f32[3,256]{1,0:T(4,128)S(1)}, u32[]{:S(2)}, u32[]{:S(2)}) collective-permute-start(f32[3,256]{1,0:T(4,128)S(1)} %select_add_fusion.1), channel_id=1, source_target_pairs={{0,3},{1,2},{2,1},{3,0},{4,7},{5,6},{6,5},{7,4},{8,11},{9,10},{10,... | collective-permute-start | bytes 9224 | tf_op jit(solution)/shard_map/ppermute | solution.py:478
  34.6 1.9 %collective-permute-done.8 = f32[3,256]{1,0:T(4,128)S(1)} collective-permute-done((f32[3,256]{1,0:T(4,128)S(1)}, f32[3,256]{1,0:T(4,128)S(1)}, u32[]{:S(2)}, u32[]{:S(2)}) %collective-permute-start.8) | collective-permute-done | bytes 3104 | tf_op jit(solution)/shard_map/ppermute | solution.py:478
  36.4 2.6 %collective-permute-done.9 = f32[3,256]{1,0:T(4,128)S(1)} collective-permute-done((f32[3,256]{1,0:T(4,128)S(1)}, f32[3,256]{1,0:T(4,128)S(1)}, u32[]{:S(2)}, u32[]{:S(2)}) %collective-permute-start.9) | collective-permute-done | bytes 3104 | tf_op jit(solution)/shard_map/ppermute | solution.py:478
  39.1 2.1 %collective-permute-start.11 = (f32[3,256]{1,0:T(4,128)S(1)}, f32[3,256]{1,0:T(4,128)S(1)}, u32[]{:S(2)}, u32[]{:S(2)}) collective-permute-start(f32[3,256]{1,0:T(4,128)S(1)} %get-tuple-element.40.brick_ref), channel_id=1, source_target_pairs={{0,28},{4,8},{8,4},{12,16},{16,12},{20,24},{24,20},{28,0},{1,29},{... | collective-permute-start | bytes 9224 | tf_op jit(solution)/shard_map/ppermute | solution.py:517
  41.3 0.5 copy-done.12
  41.8 1.3 %collective-permute-done.11 = f32[3,256]{1,0:T(4,128)S(1)} collective-permute-done((f32[3,256]{1,0:T(4,128)S(1)}, f32[3,256]{1,0:T(4,128)S(1)}, u32[]{:S(2)}, u32[]{:S(2)}) %collective-permute-start.11) | collective-permute-done | bytes 3104 | tf_op jit(solution)/shard_map/ppermute | solution.py:517
  43.1 9.8 %evaluate.3 = (f32[1,64]{1,0:T(1,128)}, f32[3,256]{1,0:T(4,128)S(1)}, f32[3,256]{1,0:T(4,128)S(1)}, f32[3,256]{1,0:T(4,128)S(1)}) custom-call(s32[1]{0:T(128)} %bitcast.1.rank_ref, f32[3,256]{1,0:T(4,128)S(1)} %get-tuple-element.47.before_ref, f32[3,256]{1,0:T(4,128)S(1)} %get-tuple-element.40.brick_ref, f32[3,256]{1,0:T(4,128)S(1)} %get-tuple-element.46.after_ref, ...), custom_call_target="tpu_custom_call" | custom-call | tf_op jit(solution)/shard_map/evaluate/pallas_call | solution.py:434
  52.9 2.0 %collective-permute-start.13 = (f32[3,256]{1,0:T(4,128)S(1)}, f32[3,256]{1,0:T(4,128)S(1)}, u32[]{:S(2)}, u32[]{:S(2)}) collective-permute-start(f32[3,256]{1,0:T(4,128)S(1)} %get-tuple-element.45), channel_id=1, source_target_pairs={{0,28},{4,8},{8,4},{12,16},{16,12},{20,24},{24,20},{28,0},{1,29},{... | collective-permute-start | bytes 9224 | tf_op jit(solution)/shard_map/ppermute | solution.py:517
  55.0 1.9 %collective-permute-done.13 = f32[3,256]{1,0:T(4,128)S(1)} collective-permute-done((f32[3,256]{1,0:T(4,128)S(1)}, f32[3,256]{1,0:T(4,128)S(1)}, u32[]{:S(2)}, u32[]{:S(2)}) %collective-permute-start.13) | collective-permute-done | bytes 3104 | tf_op jit(solution)/shard_map/ppermute | solution.py:517
  56.9 1.5 %collective-permute-start.15 = (f32[3,256]{1,0:T(4,128)S(1)}, f32[3,256]{1,0:T(4,128)S(1)}, u32[]{:S(2)}, u32[]{:S(2)}) collective-permute-start(f32[3,256]{1,0:T(4,128)S(1)} %select_add_fusion), channel_id=1, source_target_pairs={{0,2},{1,3},{2,0},{3,1},{4,6},{5,7},{6,4},{7,5},{8,10},{9,11},{10,... | collective-permute-start | bytes 9224 | tf_op jit(solution)/shard_map/ppermute | solution.py:478
  58.4 2.9 %collective-permute-start.16 = (f32[3,256]{1,0:T(4,128)S(1)}, f32[3,256]{1,0:T(4,128)S(1)}, u32[]{:S(2)}, u32[]{:S(2)}) collective-permute-start(f32[3,256]{1,0:T(4,128)S(1)} %select_add_fusion), channel_id=1, source_target_pairs={{0,3},{1,2},{2,1},{3,0},{4,7},{5,6},{6,5},{7,4},{8,11},{9,10},{10,... | collective-permute-start | bytes 9224 | tf_op jit(solution)/shard_map/ppermute | solution.py:478
  61.3 0.2 collective-permute-done.15
  61.5 2.3 %collective-permute-done.16 = f32[3,256]{1,0:T(4,128)S(1)} collective-permute-done((f32[3,256]{1,0:T(4,128)S(1)}, f32[3,256]{1,0:T(4,128)S(1)}, u32[]{:S(2)}, u32[]{:S(2)}) %collective-permute-start.16) | collective-permute-done | bytes 3104 | tf_op jit(solution)/shard_map/ppermute | solution.py:478
  63.8 0.1 fusion
  63.9 0.6 fusion.1
  (50 shorter events, 0.7 us)
Async XLA Ops:
  0.6 6.5 %copy-start.2 = (s32[64,128]{1,0:T(8,128)S(1)}, s32[64,128]{1,0:T(8,128)}, u32[]{:S(2)}) copy-start(s32[64,128]{1,0:T(8,128)} %refs_0_.1) | copy-start | bytes 98308
  1.4 10.0 %collective-permute-start.2 = (f32[6,64]{1,0:T(8,128)S(1)}, f32[6,64]{1,0:T(8,128)S(1)}, u32[]{:S(2)}, u32[]{:S(2)}) collective-permute-start(f32[6,64]{1,0:T(8,128)S(1)} %pad_maximum_fusion), channel_id=1, source_target_pairs={{0,1},{1,0},{2,3},{3,2},{4,5},{5,4},{6,7},{7,6},{8,9},{9,8},{10,11... | collective-permute-start | bytes 4616 | tf_op jit(solution)/shard_map/ppermute | solution.py:478
  4.5 6.9 %collective-permute-start = (f32[6,64]{1,0:T(8,128)S(1)}, f32[6,64]{1,0:T(8,128)S(1)}, u32[]{:S(2)}, u32[]{:S(2)}) collective-permute-start(f32[6,64]{1,0:T(8,128)S(1)} %pad_maximum_fusion), channel_id=1, source_target_pairs={{0,3},{1,2},{2,1},{3,0},{4,7},{5,6},{6,5},{7,4},{8,11},{9,10},{10,... | collective-permute-start | bytes 4616 | tf_op jit(solution)/shard_map/ppermute | solution.py:478
  7.0 4.5 %collective-permute-start.1 = (f32[6,64]{1,0:T(8,128)S(1)}, f32[6,64]{1,0:T(8,128)S(1)}, u32[]{:S(2)}, u32[]{:S(2)}) collective-permute-start(f32[6,64]{1,0:T(8,128)S(1)} %pad_maximum_fusion), channel_id=1, source_target_pairs={{0,2},{1,3},{2,0},{3,1},{4,6},{5,7},{6,4},{7,5},{8,10},{9,11},{10,... | collective-permute-start | bytes 4616 | tf_op jit(solution)/shard_map/ppermute | solution.py:478
  7.1 1.2 %copy-start = (bf16[2048,240]{0,1:T(8,128)(2,1)S(1)}, bf16[2048,240]{0,1:T(8,128)(2,1)}, u32[]{:S(2)}) copy-start(bf16[2048,240]{0,1:T(8,128)(2,1)} %param.25) | copy-start | bytes 2949124
  8.3 0.7 %copy-start.3 = (bf16[64,128]{1,0:T(8,128)(2,1)S(1)}, bf16[64,128]{1,0:T(8,128)(2,1)}, u32[]{:S(2)}) copy-start(bf16[64,128]{1,0:T(8,128)(2,1)} %refs_2_.1) | copy-start | bytes 49156
  9.0 0.7 %copy-start.4 = (bf16[32,64]{1,0:T(8,128)(2,1)S(1)}, bf16[32,64]{1,0:T(8,128)(2,1)}, u32[]{:S(2)}) copy-start(bf16[32,64]{1,0:T(8,128)(2,1)} %refs_1_.1) | copy-start | bytes 12292
  9.7 6.0 %copy-start.1 = (bf16[240,240]{1,0:T(8,128)(2,1)S(1)}, bf16[240,240]{1,0:T(8,128)(2,1)}, u32[]{:S(2)}) copy-start(bf16[240,240]{1,0:T(8,128)(2,1)} %f2_ref.3) | copy-start | bytes 345604
  11.6 2.7 %collective-permute-start.3 = (f32[3,256]{1,0:T(4,128)S(1)}, f32[3,256]{1,0:T(4,128)S(1)}, u32[]{:S(2)}, u32[]{:S(2)}) collective-permute-start(f32[3,256]{1,0:T(4,128)S(1)} %slice.12.brick_ref), channel_id=1, source_target_pairs={{0,4},{4,0},{8,12},{12,8},{16,20},{20,16},{24,28},{28,24},{1,5},{5... | collective-permute-start | bytes 9224 | tf_op jit(solution)/shard_map/ppermute | solution.py:515
  11.6 4.0 %collective-permute-start.4 = (f32[3,256]{1,0:T(4,128)S(1)}, f32[3,256]{1,0:T(4,128)S(1)}, u32[]{:S(2)}, u32[]{:S(2)}) collective-permute-start(f32[3,256]{1,0:T(4,128)S(1)} %slice.12.brick_ref), channel_id=1, source_target_pairs={{0,28},{4,8},{8,4},{12,16},{16,12},{20,24},{24,20},{28,0},{1,29},{... | collective-permute-start | bytes 9224 | tf_op jit(solution)/shard_map/ppermute | solution.py:517
  15.6 0.7 %copy-start.6 = (f32[240]{0:T(256)S(1)}, f32[240]{0:T(256)}, u32[]{:S(2)}) copy-start(f32[240]{0:T(256)} %param.28) | copy-start | bytes 2884
  15.6 0.7 %copy-start.7 = (f32[240]{0:T(256)S(1)}, f32[240]{0:T(256)}, u32[]{:S(2)}) copy-start(f32[240]{0:T(256)} %param.29) | copy-start | bytes 2884
  15.6 0.7 %copy-start.9 = (f32[32]{0:T(128)S(1)}, f32[32]{0:T(128)}, u32[]{:S(2)}) copy-start(f32[32]{0:T(128)} %param.20) | copy-start | bytes 388
  15.7 0.7 %copy-start.10 = (f32[64]{0:T(128)S(1)}, f32[64]{0:T(128)}, u32[]{:S(2)}) copy-start(f32[64]{0:T(128)} %param.22) | copy-start | bytes 772
  15.7 0.7 %copy-start.11 = (f32[128]{0:T(128)S(1)}, f32[128]{0:T(128)}, u32[]{:S(2)}) copy-start(f32[128]{0:T(128)} %param.24) | copy-start | bytes 1540
  15.7 0.7 %copy-start.5 = (f32[240]{0:T(256)S(1)}, f32[240]{0:T(256)}, u32[]{:S(2)}) copy-start(f32[240]{0:T(256)} %param.26) | copy-start | bytes 2884
  15.7 0.7 %copy-start.8 = (f32[32]{0:T(128)S(1)}, f32[32]{0:T(128)}, u32[]{:S(2)}) copy-start(f32[32]{0:T(128)} %param.19) | copy-start | bytes 388
  26.2 2.5 %collective-permute-start.5 = (f32[3,256]{1,0:T(4,128)S(1)}, f32[3,256]{1,0:T(4,128)S(1)}, u32[]{:S(2)}, u32[]{:S(2)}) collective-permute-start(f32[3,256]{1,0:T(4,128)S(1)} %get-tuple-element.48), channel_id=1, source_target_pairs={{0,4},{4,0},{8,12},{12,8},{16,20},{20,16},{24,28},{28,24},{1,5},{5... | collective-permute-start | bytes 9224 | tf_op jit(solution)/shard_map/ppermute | solution.py:515
  26.2 3.9 %collective-permute-start.6 = (f32[3,256]{1,0:T(4,128)S(1)}, f32[3,256]{1,0:T(4,128)S(1)}, u32[]{:S(2)}, u32[]{:S(2)}) collective-permute-start(f32[3,256]{1,0:T(4,128)S(1)} %get-tuple-element.49), channel_id=1, source_target_pairs={{0,28},{4,8},{8,4},{12,16},{16,12},{20,24},{24,20},{28,0},{1,29},{... | collective-permute-start | bytes 9224 | tf_op jit(solution)/shard_map/ppermute | solution.py:517
  30.2 4.4 %collective-permute-start.7 = (f32[3,256]{1,0:T(4,128)S(1)}, f32[3,256]{1,0:T(4,128)S(1)}, u32[]{:S(2)}, u32[]{:S(2)}) collective-permute-start(f32[3,256]{1,0:T(4,128)S(1)} %select_add_fusion.1), channel_id=1, source_target_pairs={{0,1},{1,0},{2,3},{3,2},{4,5},{5,4},{6,7},{7,6},{8,9},{9,8},{10,11... | collective-permute-start | bytes 9224 | tf_op jit(solution)/shard_map/ppermute | solution.py:478
  31.9 4.5 %collective-permute-start.8 = (f32[3,256]{1,0:T(4,128)S(1)}, f32[3,256]{1,0:T(4,128)S(1)}, u32[]{:S(2)}, u32[]{:S(2)}) collective-permute-start(f32[3,256]{1,0:T(4,128)S(1)} %select_add_fusion.1), channel_id=1, source_target_pairs={{0,2},{1,3},{2,0},{3,1},{4,6},{5,7},{6,4},{7,5},{8,10},{9,11},{10,... | collective-permute-start | bytes 9224 | tf_op jit(solution)/shard_map/ppermute | solution.py:478
  33.6 5.4 %collective-permute-start.9 = (f32[3,256]{1,0:T(4,128)S(1)}, f32[3,256]{1,0:T(4,128)S(1)}, u32[]{:S(2)}, u32[]{:S(2)}) collective-permute-start(f32[3,256]{1,0:T(4,128)S(1)} %select_add_fusion.1), channel_id=1, source_target_pairs={{0,3},{1,2},{2,1},{3,0},{4,7},{5,6},{6,5},{7,4},{8,11},{9,10},{10,... | collective-permute-start | bytes 9224 | tf_op jit(solution)/shard_map/ppermute | solution.py:478
  39.0 2.8 %collective-permute-start.10 = (f32[3,256]{1,0:T(4,128)S(1)}, f32[3,256]{1,0:T(4,128)S(1)}, u32[]{:S(2)}, u32[]{:S(2)}) collective-permute-start(f32[3,256]{1,0:T(4,128)S(1)} %get-tuple-element.40.brick_ref), channel_id=1, source_target_pairs={{0,4},{4,0},{8,12},{12,8},{16,20},{20,16},{24,28},{28,24},{1,5},{5... | collective-permute-start | bytes 9224 | tf_op jit(solution)/shard_map/ppermute | solution.py:515
  39.1 4.0 %collective-permute-start.11 = (f32[3,256]{1,0:T(4,128)S(1)}, f32[3,256]{1,0:T(4,128)S(1)}, u32[]{:S(2)}, u32[]{:S(2)}) collective-permute-start(f32[3,256]{1,0:T(4,128)S(1)} %get-tuple-element.40.brick_ref), channel_id=1, source_target_pairs={{0,28},{4,8},{8,4},{12,16},{16,12},{20,24},{24,20},{28,0},{1,29},{... | collective-permute-start | bytes 9224 | tf_op jit(solution)/shard_map/ppermute | solution.py:517
  41.3 0.6 copy-start.12
  52.9 2.0 %collective-permute-start.12 = (f32[3,256]{1,0:T(4,128)S(1)}, f32[3,256]{1,0:T(4,128)S(1)}, u32[]{:S(2)}, u32[]{:S(2)}) collective-permute-start(f32[3,256]{1,0:T(4,128)S(1)} %get-tuple-element.44), channel_id=1, source_target_pairs={{0,4},{4,0},{8,12},{12,8},{16,20},{20,16},{24,28},{28,24},{1,5},{5... | collective-permute-start | bytes 9224 | tf_op jit(solution)/shard_map/ppermute | solution.py:515
  52.9 3.9 %collective-permute-start.13 = (f32[3,256]{1,0:T(4,128)S(1)}, f32[3,256]{1,0:T(4,128)S(1)}, u32[]{:S(2)}, u32[]{:S(2)}) collective-permute-start(f32[3,256]{1,0:T(4,128)S(1)} %get-tuple-element.45), channel_id=1, source_target_pairs={{0,28},{4,8},{8,4},{12,16},{16,12},{20,24},{24,20},{28,0},{1,29},{... | collective-permute-start | bytes 9224 | tf_op jit(solution)/shard_map/ppermute | solution.py:517
  56.9 4.4 %collective-permute-start.14 = (f32[3,256]{1,0:T(4,128)S(1)}, f32[3,256]{1,0:T(4,128)S(1)}, u32[]{:S(2)}, u32[]{:S(2)}) collective-permute-start(f32[3,256]{1,0:T(4,128)S(1)} %select_add_fusion), channel_id=1, source_target_pairs={{0,1},{1,0},{2,3},{3,2},{4,5},{5,4},{6,7},{7,6},{8,9},{9,8},{10,11... | collective-permute-start | bytes 9224 | tf_op jit(solution)/shard_map/ppermute | solution.py:478
  56.9 4.6 %collective-permute-start.15 = (f32[3,256]{1,0:T(4,128)S(1)}, f32[3,256]{1,0:T(4,128)S(1)}, u32[]{:S(2)}, u32[]{:S(2)}) collective-permute-start(f32[3,256]{1,0:T(4,128)S(1)} %select_add_fusion), channel_id=1, source_target_pairs={{0,2},{1,3},{2,0},{3,1},{4,6},{5,7},{6,4},{7,5},{8,10},{9,11},{10,... | collective-permute-start | bytes 9224 | tf_op jit(solution)/shard_map/ppermute | solution.py:478
  58.4 5.4 %collective-permute-start.16 = (f32[3,256]{1,0:T(4,128)S(1)}, f32[3,256]{1,0:T(4,128)S(1)}, u32[]{:S(2)}, u32[]{:S(2)}) collective-permute-start(f32[3,256]{1,0:T(4,128)S(1)} %select_add_fusion), channel_id=1, source_target_pairs={{0,3},{1,2},{2,1},{3,0},{4,7},{5,6},{6,5},{7,4},{8,11},{9,10},{10,... | collective-permute-start | bytes 9224 | tf_op jit(solution)/shard_map/ppermute | solution.py:478

commit v5 on v4

--- a/solution.py
+++ b/solution.py
@@ -82,6 +82,9 @@
     dr_s,
     gr_s,
     des_s,
+    bc_s,
+    dd_s,
+    pull_s,
 ):
     atoms, slots = low_ref.shape
     brick_len = brick_ref.shape[1]
@@ -91,7 +94,6 @@
     e3 = b3_ref.shape[1]
     m2 = f1_ref.shape[0] // e3
     inv_slots = 1.0 / slots
-    pairs = atoms // 2
 
     low = low_ref[...]
     high = high_ref[...]
@@ -194,6 +196,21 @@
             t = mm(lhs, g_s[j, half * h : half * (h + 1), :], NT) * inv_slots
             t_s[rows(j, 16, 16 * h), :] = jnp.where(upper16, t[:, :e3], t[:, e3:])
 
+    def descriptor(j):
+        at = slice(GROUP * j, GROUP * (j + 1))
+        t = [t_s[pl.ds(4 * GROUP * j + c, GROUP, stride=4), :] for c in range(4)]
+        pair = []
+        for k in range(m2):
+            total = None
+            for c in range(4):
+                factor = jnp.broadcast_to(t[c][:, k : k + 1], (GROUP, e3))
+                bc_s[c * m2 + k, at, :] = factor
+                total = t[c] * factor if total is None else total + t[c] * factor
+            pair.append(total)
+            if len(pair) == 2:
+                des_s[at, (k - 1) * e3 : (k + 1) * e3] = jnp.concatenate(pair, axis=1).astype(bf16)
+                pair = []
+
     def pipeline(stages):
         depth = len(stages) - 1
 
@@ -202,25 +219,11 @@
                 if valid(lag):
                     stages[lag](step - lag)
 
-        for step in range(depth):
-            run(step, lambda lag: lag <= step)
-
-        def body(step, carry):
-            run(step, lambda lag: True)
-            return carry
-
-        lax.fori_loop(depth, groups, body, 0)
-        for step in range(groups, groups + depth):
-            run(step, lambda lag: step - lag < groups)
-
-    pipeline([first_layer, second_layer, third_layer, tensor])
-
-    tens = [t_s[pl.ds(c, atoms, stride=4), :] for c in range(4)]
-    for k in range(m2):
-        total = tens[0] * jnp.broadcast_to(tens[0][:, k : k + 1], (atoms, e3))
-        for c in range(1, 4):
-            total = total + tens[c] * jnp.broadcast_to(tens[c][:, k : k + 1], (atoms, e3))
-        des_s[:, k * e3 : (k + 1) * e3] = total.astype(bf16)
+        for step in range(groups + depth):
+            run(step, lambda lag: 0 <= step - lag < groups)
+
+    pipeline([first_layer, second_layer, third_layer, tensor, descriptor])
+
     readout = out_ref[...]
     y1 = jnp.tanh(mm(des_s[...], f1_ref[...]) + c1_ref[...])
     t4 = jnp.tanh(mm(y1.astype(bf16), f2_ref[...]) + c2_ref[...])
@@ -230,19 +233,24 @@
     dz2 = (readout * (1.0 - t4 * t4)).astype(bf16)
     dy1 = readout + mm(dz2, f2_ref[...], NT)
     dz1 = (dy1 * (1.0 - y1 * y1)).astype(bf16)
-    lane = lax.broadcasted_iota(jnp.int32, (atoms, e3), 1)
-    grads = [jnp.zeros((atoms, e3), f32)] * 4
-    for k in range(m2):
-        dd = mm(dz1, f1_ref[k * e3 : (k + 1) * e3, :], NT)
+    dd_s[...] = mm(dz1, f1_ref[...], NT)
+    lane = lax.broadcasted_iota(jnp.int32, (GROUP, e3), 1)
+
+    def tensor_back(j):
+        at = slice(GROUP * j, GROUP * (j + 1))
+        t = [t_s[pl.ds(4 * GROUP * j + c, GROUP, stride=4), :] for c in range(4)]
+        grads = [None] * 4
+        others = [jnp.zeros((GROUP, e3), f32)] * 4
+        for k in range(m2):
+            dd = dd_s[at, k * e3 : (k + 1) * e3]
+            for c in range(4):
+                other = jnp.sum(dd * t[c], axis=1, keepdims=True)
+                others[c] = jnp.where(lane == k, other, others[c])
+                term = dd * bc_s[c * m2 + k, at, :]
+                grads[c] = term if grads[c] is None else grads[c] + term
         for c in range(4):
-            other = jnp.sum(dd * tens[c], axis=1, keepdims=True)
-            grads[c] = (
-                grads[c]
-                + dd * jnp.broadcast_to(tens[c][:, k : k + 1], (atoms, e3))
-                + jnp.where(lane == k, other, 0.0)
-            )
-    for c in range(4):
-        d_s[pl.ds(c, atoms, stride=4), :] = grads[c].astype(bf16).astype(f32) * inv_slots
+            rounded = (grads[c] + others[c]).astype(bf16).astype(f32)
+            d_s[pl.ds(4 * GROUP * j + c, GROUP, stride=4), :] = rounded * inv_slots
 
     def third_back(j):
         dt = d_s[rows(j, 32), :]
@@ -278,49 +286,56 @@
                 start = (GROUP * j + 2 * q + a) * 8
                 z_s[pl.ds(start if isinstance(start, int) else pl.multiple_of(start, 8), 8), :] = z
 
-    pipeline([third_back, second_back, first_back])
-
-    ds = dr_s[pl.ds(0, atoms, stride=4), :]
-    for i in range(8):
-        ds = ds + z_s[pl.ds(i, atoms, stride=8), :]
-    drs = [dr_s[pl.ds(c + 1, atoms, stride=4), :] for c in range(3)]
-    radial = drs[0] * disp[0] + drs[1] * disp[1] + drs[2] * disp[2]
-    factor = -ds / (radius * quad) - 2.0 * radial * (inv_quad * inv_quad)
     ones = jnp.ones((8, LANES), bf16)
-    zero = jnp.zeros((atoms, LANES), f32)
-    sums = []
-    for c in range(3):
-        pull = mask * (disp[c] * factor + drs[c] * inv_quad)
-        upper, lower = split2(pull)
-        gr_s[pl.ds(c, atoms, stride=8), :] = upper
-        gr_s[pl.ds(c + 3, atoms, stride=8), :] = lower
-        both_parts = mm(ones, upper.astype(bf16), NT) + mm(ones, lower.astype(bf16), NT)
-        sums.append(both_parts[0:1])
-    gr_s[pl.ds(6, atoms, stride=8), :] = zero
-    gr_s[pl.ds(7, atoms, stride=8), :] = zero
-    mine = jnp.concatenate(sums, axis=0)
-
     place = lax.broadcasted_iota(jnp.int32, (LANES, LANES), 0)
     chunks = 3 * per
-
-    def scatter(p, total):
-        rows = []
-        hots = []
-        for i in range(2):
-            atom = 2 * p + i
-            values = gr_s[pl.ds(pl.multiple_of(atom * 8, 8), 8), :]
-            upper = jnp.broadcast_to(high_ref[pl.ds(atom, 1), :], (8, LANES))
-            lower = jnp.broadcast_to(low_ref[pl.ds(atom, 1), :], (LANES, LANES))
-            rows.append(
-                jnp.concatenate(
-                    [jnp.where(upper == a, values, 0.0) for a in range(chunks)], axis=0
+    mine = []
+    found = [jnp.zeros((8 * chunks, LANES), f32)]
+
+    def pulls(j):
+        at = slice(GROUP * j, GROUP * (j + 1))
+        drs = [dr_s[pl.ds(4 * GROUP * j + c, GROUP, stride=4), :] for c in range(4)]
+        ds = drs[0]
+        for i in range(8):
+            ds = ds + z_s[pl.ds(8 * GROUP * j + i, GROUP, stride=8), :]
+        d = [disp[c][at] for c in range(3)]
+        q, iq = quad[at], inv_quad[at]
+        radial = drs[1] * d[0] + drs[2] * d[1] + drs[3] * d[2]
+        factor = -ds / (radius[at] * q) - 2.0 * radial * (iq * iq)
+        for c in range(3):
+            pull = mask[at] * (d[c] * factor + drs[c + 1] * iq)
+            upper, lower = split2(pull)
+            gr_s[pl.ds(8 * GROUP * j + c, GROUP, stride=8), :] = upper
+            gr_s[pl.ds(8 * GROUP * j + c + 3, GROUP, stride=8), :] = lower
+            pull_s[c, at, :] = upper
+            pull_s[c + 3, at, :] = lower
+        for c in (6, 7):
+            gr_s[pl.ds(8 * GROUP * j + c, GROUP, stride=8), :] = jnp.zeros((GROUP, LANES), f32)
+
+    def scatter(j):
+        for q in range(PAIRS):
+            rows_of = []
+            hots = []
+            for a in range(2):
+                atom = GROUP * j + 2 * q + a
+                values = gr_s[8 * atom : 8 * atom + 8, :]
+                upper = jnp.broadcast_to(high_ref[atom : atom + 1, :], (8, LANES))
+                lower = jnp.broadcast_to(low_ref[atom : atom + 1, :], (LANES, LANES))
+                rows_of.append(
+                    jnp.concatenate(
+                        [jnp.where(upper == i, values, 0.0) for i in range(chunks)], axis=0
+                    )
                 )
-            )
-            hots.append(jnp.where(lower == place, 1.0, 0.0).astype(bf16))
-        lhs = jnp.concatenate(rows, axis=1).astype(bf16)
-        return total + mm(lhs, jnp.concatenate(hots, axis=1), NT)
-
-    total = lax.fori_loop(0, pairs, scatter, jnp.zeros((8 * chunks, LANES), f32), unroll=4)
+                hots.append(jnp.where(lower == place, 1.0, 0.0).astype(bf16))
+            lhs = jnp.concatenate(rows_of, axis=1).astype(bf16)
+            found[0] = found[0] + mm(lhs, jnp.concatenate(hots, axis=1), NT)
+
+    pipeline([tensor_back, third_back, second_back, first_back, pulls, scatter])
+    for c in range(3):
+        sums = mm(ones, pull_s[c].astype(bf16), NT) + mm(ones, pull_s[c + 3].astype(bf16), NT)
+        mine.append(sums[0:1])
+    mine = jnp.concatenate(mine, axis=0)
+    total = found[0]
     rank = rank_ref[0]
     spot = lax.broadcasted_iota(jnp.int32, (3, brick_len), 1) // atoms
     placed = jnp.where(
@@ -456,6 +471,9 @@
             pltpu.VMEM((4 * atoms, slots), f32),
             pltpu.VMEM((8 * atoms, slots), f32),
             pltpu.VMEM((atoms, prepared[10].shape[0]), bf16),
+            pltpu.VMEM((4 * prepared[10].shape[0] // e3, atoms, e3), f32),
+            pltpu.VMEM((atoms, prepared[10].shape[0]), f32),
+            pltpu.VMEM((6, atoms, LANES), f32),
         ],
         compiler_params=pltpu.CompilerParams(vmem_limit_bytes=40 * 1024 * 1024),
         name="evaluate",

time: 64.8 us -> 59.4 us (0.917)
  Pallas kernels: 21.2 us -> 15.6 us
    pallas_call x2, Pallas kernels: 19.6 us -> 14 us  [evaluate(): pl.pallas_call(eval_kernel, out_shape=(jax.ShapeDtypeStruct((1, atoms), f...]
  transfers between devices with their start and end apart: 17 -> 17, of which waited for: 8 -> 8; matrix products, arithmetic and copies ran while one was open for 0% -> 1% of each run, Pallas kernels for 3% -> 3%
where the time goes in v5:
time: 59.4 us; the launch traced here: 59 us
  starting transfers between devices  23.8 us (40%)
  Pallas kernels  15.6 us (26%)
  waiting for transfers between devices  13.2 us (22%)
  local copies, waits for them, and re-layouts  4.5 us (8%)
  other arithmetic  1.17 us (2%)
  between operations  0.77 us (1%)
    ppermute x9, starting transfers between devices, from_others(): lax.ppermute(value, 'help', flip(size, k))  14.5 us
    pallas_call x2, Pallas kernels, evaluate(): pl.pallas_call(eval_kernel, out_shape=(jax.ShapeDtypeStruct((1, atoms), f...  14 us
    ppermute x4, starting transfers between devices, exchange(): outer = lax.ppermute(jnp.where(odd, up, down), 'brick', pairs)  9.1 us
    ppermute x9, waiting for transfers between devices, from_others(): lax.ppermute(value, 'help', flip(size, k))  7.04 us
    ppermute x4, waiting for transfers between devices, exchange(): outer = lax.ppermute(jnp.where(odd, up, down), 'brick', pairs)  6.15 us
    unnamed x26, local copies, waits for them, and re-layouts  3.83 us
    pallas_call x1, Pallas kernels, prepare(): pl.pallas_call(prepare_kernel, out_shape=outs, in_specs=[pl.BlockSpec(mem...  1.62 us
  transfers between devices with their start and end apart: 17, of which 8 were waited for; matrix products, arithmetic and copies ran while one was open for 1% of the time, Pallas kernels for 3%

profile of v5, /device:TPU:0, one launch (start us, length us, event | category | flops | bytes accessed | tf_op | source)
XLA Modules:
  0.0 59.0 jit_solution(17333870774469121029)
XLA Ops:
  0.6 0.7 %multiply_add_fusion.2 = (f32[3,64]{1,0:T(4,128)S(1)}, f32[3,64]{1,0:T(4,128)S(1)}) fusion(f32[3,64]{1,0:T(4,128)} %param.15, f32[3,64]{1,0:T(4,128)} %param.16, f32[3,64]{1,0:T(4,128)} %param.17), kind=kLoop, calls=%fused_computation.15 | loop fusion | flops 768 | bytes 3840 | tf_op jit(solution)/shard_map/add | solution.py:546
  1.4 3.1 %collective-permute-start.2 = (f32[6,64]{1,0:T(8,128)S(1)}, f32[6,64]{1,0:T(8,128)S(1)}, u32[]{:S(2)}, u32[]{:S(2)}) collective-permute-start(f32[6,64]{1,0:T(8,128)S(1)} %pad_maximum_fusion), channel_id=1, source_target_pairs={{0,1},{1,0},{2,3},{3,2},{4,5},{5,4},{6,7},{7,6},{8,9},{9,8},{10,11... | collective-permute-start | bytes 4616 | tf_op jit(solution)/shard_map/ppermute | solution.py:496
  4.5 2.5 %collective-permute-start = (f32[6,64]{1,0:T(8,128)S(1)}, f32[6,64]{1,0:T(8,128)S(1)}, u32[]{:S(2)}, u32[]{:S(2)}) collective-permute-start(f32[6,64]{1,0:T(8,128)S(1)} %pad_maximum_fusion), channel_id=1, source_target_pairs={{0,3},{1,2},{2,1},{3,0},{4,7},{5,6},{6,5},{7,4},{8,11},{9,10},{10,... | collective-permute-start | bytes 4616 | tf_op jit(solution)/shard_map/ppermute | solution.py:496
  7.0 0.1 collective-permute-start.1
  7.1 1.2 %copy-done = bf16[2048,240]{0,1:T(8,128)(2,1)S(1)} copy-done((bf16[2048,240]{0,1:T(8,128)(2,1)S(1)}, bf16[2048,240]{0,1:T(8,128)(2,1)}, u32[]{:S(2)}) %copy-start) | copy-done | bytes 983064
  8.3 0.7 %copy-done.3 = bf16[64,128]{1,0:T(8,128)(2,1)S(1)} copy-done((bf16[64,128]{1,0:T(8,128)(2,1)S(1)}, bf16[64,128]{1,0:T(8,128)(2,1)}, u32[]{:S(2)}) %copy-start.3) | copy-done | bytes 16408
  9.0 0.7 %copy-done.4 = bf16[32,64]{1,0:T(8,128)(2,1)S(1)} copy-done((bf16[32,64]{1,0:T(8,128)(2,1)S(1)}, bf16[32,64]{1,0:T(8,128)(2,1)}, u32[]{:S(2)}) %copy-start.4) | copy-done | bytes 4120
  9.7 1.6 %prepare.1 = (s32[64,128]{1,0:T(8,128)S(1)}, s32[64,128]{1,0:T(8,128)S(1)}, bf16[256,128]{1,0:T(8,128)(2,1)S(1)}, bf16[128,256]{1,0:T(8,128)(2,1)S(1)}, bf16[512...) custom-call(s32[64,128]{1,0:T(8,128)S(1)} %copy-done.2, ...), custom_call_target="tpu_custom_call" | custom-call | flops 4000000 | bytes 2500000 | tf_op jit(solution)/shard_map/prepare/pallas_call | solution.py:409
  11.3 0.1 maximum_select_fusion.2
  11.5 0.1 maximum_select_fusion.1
  11.6 2.5 %collective-permute-start.4 = (f32[3,256]{1,0:T(4,128)S(1)}, f32[3,256]{1,0:T(4,128)S(1)}, u32[]{:S(2)}, u32[]{:S(2)}) collective-permute-start(f32[3,256]{1,0:T(4,128)S(1)} %slice.12.brick_ref), channel_id=1, source_target_pairs={{0,28},{4,8},{8,4},{12,16},{16,12},{20,24},{24,20},{28,0},{1,29},{... | collective-permute-start | bytes 9224 | tf_op jit(solution)/shard_map/ppermute | solution.py:535
  14.3 1.4 %collective-permute-done.4 = f32[3,256]{1,0:T(4,128)S(1)} collective-permute-done((f32[3,256]{1,0:T(4,128)S(1)}, f32[3,256]{1,0:T(4,128)S(1)}, u32[]{:S(2)}, u32[]{:S(2)}) %collective-permute-start.4) | collective-permute-done | bytes 3104 | tf_op jit(solution)/shard_map/ppermute | solution.py:535
  15.7 0.6 %copy-done.6 = f32[240]{0:T(256)S(1)} copy-done((f32[240]{0:T(256)S(1)}, f32[240]{0:T(256)}, u32[]{:S(2)}) %copy-start.6) | copy-done | bytes 984
  16.4 7.0 %evaluate.2 = (f32[1,64]{1,0:T(1,128)}, f32[3,256]{1,0:T(4,128)S(1)}, f32[3,256]{1,0:T(4,128)S(1)}, f32[3,256]{1,0:T(4,128)S(1)}) custom-call(s32[1]{0:T(128)} %bitcast.1.rank_ref, f32[3,256]{1,0:T(4,128)S(1)} %get-tuple-element.51.before_ref, f32[3,256]{1,0:T(4,128)S(1)} %slice.12.brick_ref, f32[3,256]{1,0:T(4,128)S(1)} %get-tuple-element.50.after_ref, ...), custom_call_target="tpu_custom_call" | custom-call | tf_op jit(solution)/shard_map/evaluate/pallas_call | solution.py:449
  23.5 2.5 %collective-permute-start.6 = (f32[3,256]{1,0:T(4,128)S(1)}, f32[3,256]{1,0:T(4,128)S(1)}, u32[]{:S(2)}, u32[]{:S(2)}) collective-permute-start(f32[3,256]{1,0:T(4,128)S(1)} %get-tuple-element.49), channel_id=1, source_target_pairs={{0,28},{4,8},{8,4},{12,16},{16,12},{20,24},{24,20},{28,0},{1,29},{... | collective-permute-start | bytes 9224 | tf_op jit(solution)/shard_map/ppermute | solution.py:535
  26.0 1.4 %collective-permute-done.6 = f32[3,256]{1,0:T(4,128)S(1)} collective-permute-done((f32[3,256]{1,0:T(4,128)S(1)}, f32[3,256]{1,0:T(4,128)S(1)}, u32[]{:S(2)}, u32[]{:S(2)}) %collective-permute-start.6) | collective-permute-done | bytes 3104 | tf_op jit(solution)/shard_map/ppermute | solution.py:535
  27.5 1.8 %collective-permute-start.7 = (f32[3,256]{1,0:T(4,128)S(1)}, f32[3,256]{1,0:T(4,128)S(1)}, u32[]{:S(2)}, u32[]{:S(2)}) collective-permute-start(f32[3,256]{1,0:T(4,128)S(1)} %select_add_fusion.1), channel_id=1, source_target_pairs={{0,1},{1,0},{2,3},{3,2},{4,5},{5,4},{6,7},{7,6},{8,9},{9,8},{10,11... | collective-permute-start | bytes 9224 | tf_op jit(solution)/shard_map/ppermute | solution.py:496
  29.2 1.7 %collective-permute-start.8 = (f32[3,256]{1,0:T(4,128)S(1)}, f32[3,256]{1,0:T(4,128)S(1)}, u32[]{:S(2)}, u32[]{:S(2)}) collective-permute-start(f32[3,256]{1,0:T(4,128)S(1)} %select_add_fusion.1), channel_id=1, source_target_pairs={{0,2},{1,3},{2,0},{3,1},{4,6},{5,7},{6,4},{7,5},{8,10},{9,11},{10,... | collective-permute-start | bytes 9224 | tf_op jit(solution)/shard_map/ppermute | solution.py:496
  30.9 0.9 %collective-permute-start.9 = (f32[3,256]{1,0:T(4,128)S(1)}, f32[3,256]{1,0:T(4,128)S(1)}, u32[]{:S(2)}, u32[]{:S(2)}) collective-permute-start(f32[3,256]{1,0:T(4,128)S(1)} %select_add_fusion.1), channel_id=1, source_target_pairs={{0,3},{1,2},{2,1},{3,0},{4,7},{5,6},{6,5},{7,4},{8,11},{9,10},{10,... | collective-permute-start | bytes 9224 | tf_op jit(solution)/shard_map/ppermute | solution.py:496
  31.8 1.9 %collective-permute-done.8 = f32[3,256]{1,0:T(4,128)S(1)} collective-permute-done((f32[3,256]{1,0:T(4,128)S(1)}, f32[3,256]{1,0:T(4,128)S(1)}, u32[]{:S(2)}, u32[]{:S(2)}) %collective-permute-start.8) | collective-permute-done | bytes 3104 | tf_op jit(solution)/shard_map/ppermute | solution.py:496
  33.7 2.6 %collective-permute-done.9 = f32[3,256]{1,0:T(4,128)S(1)} collective-permute-done((f32[3,256]{1,0:T(4,128)S(1)}, f32[3,256]{1,0:T(4,128)S(1)}, u32[]{:S(2)}, u32[]{:S(2)}) %collective-permute-start.9) | collective-permute-done | bytes 3104 | tf_op jit(solution)/shard_map/ppermute | solution.py:496
  36.4 2.0 %collective-permute-start.11 = (f32[3,256]{1,0:T(4,128)S(1)}, f32[3,256]{1,0:T(4,128)S(1)}, u32[]{:S(2)}, u32[]{:S(2)}) collective-permute-start(f32[3,256]{1,0:T(4,128)S(1)} %get-tuple-element.40.brick_ref), channel_id=1, source_target_pairs={{0,28},{4,8},{8,4},{12,16},{16,12},{20,24},{24,20},{28,0},{1,29},{... | collective-permute-start | bytes 9224 | tf_op jit(solution)/shard_map/ppermute | solution.py:535
  38.6 0.5 copy-done.12
  39.1 1.3 %collective-permute-done.11 = f32[3,256]{1,0:T(4,128)S(1)} collective-permute-done((f32[3,256]{1,0:T(4,128)S(1)}, f32[3,256]{1,0:T(4,128)S(1)}, u32[]{:S(2)}, u32[]{:S(2)}) %collective-permute-start.11) | collective-permute-done | bytes 3104 | tf_op jit(solution)/shard_map/ppermute | solution.py:535
  40.4 7.0 %evaluate.3 = (f32[1,64]{1,0:T(1,128)}, f32[3,256]{1,0:T(4,128)S(1)}, f32[3,256]{1,0:T(4,128)S(1)}, f32[3,256]{1,0:T(4,128)S(1)}) custom-call(s32[1]{0:T(128)} %bitcast.1.rank_ref, f32[3,256]{1,0:T(4,128)S(1)} %get-tuple-element.47.before_ref, f32[3,256]{1,0:T(4,128)S(1)} %get-tuple-element.40.brick_ref, f32[3,256]{1,0:T(4,128)S(1)} %get-tuple-element.46.after_ref, ...), custom_call_target="tpu_custom_call" | custom-call | tf_op jit(solution)/shard_map/evaluate/pallas_call | solution.py:449
  47.5 2.0 %collective-permute-start.13 = (f32[3,256]{1,0:T(4,128)S(1)}, f32[3,256]{1,0:T(4,128)S(1)}, u32[]{:S(2)}, u32[]{:S(2)}) collective-permute-start(f32[3,256]{1,0:T(4,128)S(1)} %get-tuple-element.45), channel_id=1, source_target_pairs={{0,28},{4,8},{8,4},{12,16},{16,12},{20,24},{24,20},{28,0},{1,29},{... | collective-permute-start | bytes 9224 | tf_op jit(solution)/shard_map/ppermute | solution.py:535
  49.5 2.0 %collective-permute-done.13 = f32[3,256]{1,0:T(4,128)S(1)} collective-permute-done((f32[3,256]{1,0:T(4,128)S(1)}, f32[3,256]{1,0:T(4,128)S(1)}, u32[]{:S(2)}, u32[]{:S(2)}) %collective-permute-start.13) | collective-permute-done | bytes 3104 | tf_op jit(solution)/shard_map/ppermute | solution.py:535
  51.5 1.5 %collective-permute-start.15 = (f32[3,256]{1,0:T(4,128)S(1)}, f32[3,256]{1,0:T(4,128)S(1)}, u32[]{:S(2)}, u32[]{:S(2)}) collective-permute-start(f32[3,256]{1,0:T(4,128)S(1)} %select_add_fusion), channel_id=1, source_target_pairs={{0,2},{1,3},{2,0},{3,1},{4,6},{5,7},{6,4},{7,5},{8,10},{9,11},{10,... | collective-permute-start | bytes 9224 | tf_op jit(solution)/shard_map/ppermute | solution.py:496
  53.0 2.9 %collective-permute-start.16 = (f32[3,256]{1,0:T(4,128)S(1)}, f32[3,256]{1,0:T(4,128)S(1)}, u32[]{:S(2)}, u32[]{:S(2)}) collective-permute-start(f32[3,256]{1,0:T(4,128)S(1)} %select_add_fusion), channel_id=1, source_target_pairs={{0,3},{1,2},{2,1},{3,0},{4,7},{5,6},{6,5},{7,4},{8,11},{9,10},{10,... | collective-permute-start | bytes 9224 | tf_op jit(solution)/shard_map/ppermute | solution.py:496
  55.9 0.2 collective-permute-done.15
  56.1 2.3 %collective-permute-done.16 = f32[3,256]{1,0:T(4,128)S(1)} collective-permute-done((f32[3,256]{1,0:T(4,128)S(1)}, f32[3,256]{1,0:T(4,128)S(1)}, u32[]{:S(2)}, u32[]{:S(2)}) %collective-permute-start.16) | collective-permute-done | bytes 3104 | tf_op jit(solution)/shard_map/ppermute | solution.py:496
  58.5 0.6 %fusion.1 = (f32[3,64]{1,0:T(4,128)}, f32[3,64]{1,0:T(4,128)}) fusion(f32[6,64]{1,0:T(8,128)S(1)} %fusion), kind=kLoop, calls=%fused_computation.26 | loop fusion | bytes 3072 | tf_op jit(solution)/shard_map/slice | solution.py:567
  (50 shorter events, 0.8 us)
Async XLA Ops:
  0.6 6.5 %copy-start.2 = (s32[64,128]{1,0:T(8,128)S(1)}, s32[64,128]{1,0:T(8,128)}, u32[]{:S(2)}) copy-start(s32[64,128]{1,0:T(8,128)} %refs_0_.1) | copy-start | bytes 98308
  1.4 10.0 %collective-permute-start.2 = (f32[6,64]{1,0:T(8,128)S(1)}, f32[6,64]{1,0:T(8,128)S(1)}, u32[]{:S(2)}, u32[]{:S(2)}) collective-permute-start(f32[6,64]{1,0:T(8,128)S(1)} %pad_maximum_fusion), channel_id=1, source_target_pairs={{0,1},{1,0},{2,3},{3,2},{4,5},{5,4},{6,7},{7,6},{8,9},{9,8},{10,11... | collective-permute-start | bytes 4616 | tf_op jit(solution)/shard_map/ppermute | solution.py:496
  4.5 6.9 %collective-permute-start = (f32[6,64]{1,0:T(8,128)S(1)}, f32[6,64]{1,0:T(8,128)S(1)}, u32[]{:S(2)}, u32[]{:S(2)}) collective-permute-start(f32[6,64]{1,0:T(8,128)S(1)} %pad_maximum_fusion), channel_id=1, source_target_pairs={{0,3},{1,2},{2,1},{3,0},{4,7},{5,6},{6,5},{7,4},{8,11},{9,10},{10,... | collective-permute-start | bytes 4616 | tf_op jit(solution)/shard_map/ppermute | solution.py:496
  7.0 4.5 %collective-permute-start.1 = (f32[6,64]{1,0:T(8,128)S(1)}, f32[6,64]{1,0:T(8,128)S(1)}, u32[]{:S(2)}, u32[]{:S(2)}) collective-permute-start(f32[6,64]{1,0:T(8,128)S(1)} %pad_maximum_fusion), channel_id=1, source_target_pairs={{0,2},{1,3},{2,0},{3,1},{4,6},{5,7},{6,4},{7,5},{8,10},{9,11},{10,... | collective-permute-start | bytes 4616 | tf_op jit(solution)/shard_map/ppermute | solution.py:496
  7.1 1.2 %copy-start = (bf16[2048,240]{0,1:T(8,128)(2,1)S(1)}, bf16[2048,240]{0,1:T(8,128)(2,1)}, u32[]{:S(2)}) copy-start(bf16[2048,240]{0,1:T(8,128)(2,1)} %param.25) | copy-start | bytes 2949124
  8.3 0.7 %copy-start.3 = (bf16[64,128]{1,0:T(8,128)(2,1)S(1)}, bf16[64,128]{1,0:T(8,128)(2,1)}, u32[]{:S(2)}) copy-start(bf16[64,128]{1,0:T(8,128)(2,1)} %refs_2_.1) | copy-start | bytes 49156
  9.0 0.7 %copy-start.4 = (bf16[32,64]{1,0:T(8,128)(2,1)S(1)}, bf16[32,64]{1,0:T(8,128)(2,1)}, u32[]{:S(2)}) copy-start(bf16[32,64]{1,0:T(8,128)(2,1)} %refs_1_.1) | copy-start | bytes 12292
  9.7 6.0 %copy-start.1 = (bf16[240,240]{1,0:T(8,128)(2,1)S(1)}, bf16[240,240]{1,0:T(8,128)(2,1)}, u32[]{:S(2)}) copy-start(bf16[240,240]{1,0:T(8,128)(2,1)} %f2_ref.3) | copy-start | bytes 345604
  11.6 2.7 %collective-permute-start.3 = (f32[3,256]{1,0:T(4,128)S(1)}, f32[3,256]{1,0:T(4,128)S(1)}, u32[]{:S(2)}, u32[]{:S(2)}) collective-permute-start(f32[3,256]{1,0:T(4,128)S(1)} %slice.12.brick_ref), channel_id=1, source_target_pairs={{0,4},{4,0},{8,12},{12,8},{16,20},{20,16},{24,28},{28,24},{1,5},{5... | collective-permute-start | bytes 9224 | tf_op jit(solution)/shard_map/ppermute | solution.py:533
  11.6 4.0 %collective-permute-start.4 = (f32[3,256]{1,0:T(4,128)S(1)}, f32[3,256]{1,0:T(4,128)S(1)}, u32[]{:S(2)}, u32[]{:S(2)}) collective-permute-start(f32[3,256]{1,0:T(4,128)S(1)} %slice.12.brick_ref), channel_id=1, source_target_pairs={{0,28},{4,8},{8,4},{12,16},{16,12},{20,24},{24,20},{28,0},{1,29},{... | collective-permute-start | bytes 9224 | tf_op jit(solution)/shard_map/ppermute | solution.py:535
  15.6 0.7 %copy-start.6 = (f32[240]{0:T(256)S(1)}, f32[240]{0:T(256)}, u32[]{:S(2)}) copy-start(f32[240]{0:T(256)} %param.28) | copy-start | bytes 2884
  15.6 0.7 %copy-start.7 = (f32[240]{0:T(256)S(1)}, f32[240]{0:T(256)}, u32[]{:S(2)}) copy-start(f32[240]{0:T(256)} %param.29) | copy-start | bytes 2884
  15.6 0.7 %copy-start.9 = (f32[32]{0:T(128)S(1)}, f32[32]{0:T(128)}, u32[]{:S(2)}) copy-start(f32[32]{0:T(128)} %param.20) | copy-start | bytes 388
  15.7 0.7 %copy-start.10 = (f32[64]{0:T(128)S(1)}, f32[64]{0:T(128)}, u32[]{:S(2)}) copy-start(f32[64]{0:T(128)} %param.22) | copy-start | bytes 772
  15.7 0.7 %copy-start.11 = (f32[128]{0:T(128)S(1)}, f32[128]{0:T(128)}, u32[]{:S(2)}) copy-start(f32[128]{0:T(128)} %param.24) | copy-start | bytes 1540
  15.7 0.7 %copy-start.5 = (f32[240]{0:T(256)S(1)}, f32[240]{0:T(256)}, u32[]{:S(2)}) copy-start(f32[240]{0:T(256)} %param.26) | copy-start | bytes 2884
  15.7 0.7 %copy-start.8 = (f32[32]{0:T(128)S(1)}, f32[32]{0:T(128)}, u32[]{:S(2)}) copy-start(f32[32]{0:T(128)} %param.19) | copy-start | bytes 388
  23.4 2.6 %collective-permute-start.5 = (f32[3,256]{1,0:T(4,128)S(1)}, f32[3,256]{1,0:T(4,128)S(1)}, u32[]{:S(2)}, u32[]{:S(2)}) collective-permute-start(f32[3,256]{1,0:T(4,128)S(1)} %get-tuple-element.48), channel_id=1, source_target_pairs={{0,4},{4,0},{8,12},{12,8},{16,20},{20,16},{24,28},{28,24},{1,5},{5... | collective-permute-start | bytes 9224 | tf_op jit(solution)/shard_map/ppermute | solution.py:533
  23.5 4.0 %collective-permute-start.6 = (f32[3,256]{1,0:T(4,128)S(1)}, f32[3,256]{1,0:T(4,128)S(1)}, u32[]{:S(2)}, u32[]{:S(2)}) collective-permute-start(f32[3,256]{1,0:T(4,128)S(1)} %get-tuple-element.49), channel_id=1, source_target_pairs={{0,28},{4,8},{8,4},{12,16},{16,12},{20,24},{24,20},{28,0},{1,29},{... | collective-permute-start | bytes 9224 | tf_op jit(solution)/shard_map/ppermute | solution.py:535
  27.5 4.4 %collective-permute-start.7 = (f32[3,256]{1,0:T(4,128)S(1)}, f32[3,256]{1,0:T(4,128)S(1)}, u32[]{:S(2)}, u32[]{:S(2)}) collective-permute-start(f32[3,256]{1,0:T(4,128)S(1)} %select_add_fusion.1), channel_id=1, source_target_pairs={{0,1},{1,0},{2,3},{3,2},{4,5},{5,4},{6,7},{7,6},{8,9},{9,8},{10,11... | collective-permute-start | bytes 9224 | tf_op jit(solution)/shard_map/ppermute | solution.py:496
  29.2 4.5 %collective-permute-start.8 = (f32[3,256]{1,0:T(4,128)S(1)}, f32[3,256]{1,0:T(4,128)S(1)}, u32[]{:S(2)}, u32[]{:S(2)}) collective-permute-start(f32[3,256]{1,0:T(4,128)S(1)} %select_add_fusion.1), channel_id=1, source_target_pairs={{0,2},{1,3},{2,0},{3,1},{4,6},{5,7},{6,4},{7,5},{8,10},{9,11},{10,... | collective-permute-start | bytes 9224 | tf_op jit(solution)/shard_map/ppermute | solution.py:496
  30.9 5.4 %collective-permute-start.9 = (f32[3,256]{1,0:T(4,128)S(1)}, f32[3,256]{1,0:T(4,128)S(1)}, u32[]{:S(2)}, u32[]{:S(2)}) collective-permute-start(f32[3,256]{1,0:T(4,128)S(1)} %select_add_fusion.1), channel_id=1, source_target_pairs={{0,3},{1,2},{2,1},{3,0},{4,7},{5,6},{6,5},{7,4},{8,11},{9,10},{10,... | collective-permute-start | bytes 9224 | tf_op jit(solution)/shard_map/ppermute | solution.py:496
  36.3 2.7 %collective-permute-start.10 = (f32[3,256]{1,0:T(4,128)S(1)}, f32[3,256]{1,0:T(4,128)S(1)}, u32[]{:S(2)}, u32[]{:S(2)}) collective-permute-start(f32[3,256]{1,0:T(4,128)S(1)} %get-tuple-element.40.brick_ref), channel_id=1, source_target_pairs={{0,4},{4,0},{8,12},{12,8},{16,20},{20,16},{24,28},{28,24},{1,5},{5... | collective-permute-start | bytes 9224 | tf_op jit(solution)/shard_map/ppermute | solution.py:533
  36.4 4.0 %collective-permute-start.11 = (f32[3,256]{1,0:T(4,128)S(1)}, f32[3,256]{1,0:T(4,128)S(1)}, u32[]{:S(2)}, u32[]{:S(2)}) collective-permute-start(f32[3,256]{1,0:T(4,128)S(1)} %get-tuple-element.40.brick_ref), channel_id=1, source_target_pairs={{0,28},{4,8},{8,4},{12,16},{16,12},{20,24},{24,20},{28,0},{1,29},{... | collective-permute-start | bytes 9224 | tf_op jit(solution)/shard_map/ppermute | solution.py:535
  38.5 0.6 copy-start.12
  47.4 2.1 %collective-permute-start.12 = (f32[3,256]{1,0:T(4,128)S(1)}, f32[3,256]{1,0:T(4,128)S(1)}, u32[]{:S(2)}, u32[]{:S(2)}) collective-permute-start(f32[3,256]{1,0:T(4,128)S(1)} %get-tuple-element.44), channel_id=1, source_target_pairs={{0,4},{4,0},{8,12},{12,8},{16,20},{20,16},{24,28},{28,24},{1,5},{5... | collective-permute-start | bytes 9224 | tf_op jit(solution)/shard_map/ppermute | solution.py:533
  47.5 4.0 %collective-permute-start.13 = (f32[3,256]{1,0:T(4,128)S(1)}, f32[3,256]{1,0:T(4,128)S(1)}, u32[]{:S(2)}, u32[]{:S(2)}) collective-permute-start(f32[3,256]{1,0:T(4,128)S(1)} %get-tuple-element.45), channel_id=1, source_target_pairs={{0,28},{4,8},{8,4},{12,16},{16,12},{20,24},{24,20},{28,0},{1,29},{... | collective-permute-start | bytes 9224 | tf_op jit(solution)/shard_map/ppermute | solution.py:535
  51.5 4.4 %collective-permute-start.14 = (f32[3,256]{1,0:T(4,128)S(1)}, f32[3,256]{1,0:T(4,128)S(1)}, u32[]{:S(2)}, u32[]{:S(2)}) collective-permute-start(f32[3,256]{1,0:T(4,128)S(1)} %select_add_fusion), channel_id=1, source_target_pairs={{0,1},{1,0},{2,3},{3,2},{4,5},{5,4},{6,7},{7,6},{8,9},{9,8},{10,11... | collective-permute-start | bytes 9224 | tf_op jit(solution)/shard_map/ppermute | solution.py:496
  51.5 4.6 %collective-permute-start.15 = (f32[3,256]{1,0:T(4,128)S(1)}, f32[3,256]{1,0:T(4,128)S(1)}, u32[]{:S(2)}, u32[]{:S(2)}) collective-permute-start(f32[3,256]{1,0:T(4,128)S(1)} %select_add_fusion), channel_id=1, source_target_pairs={{0,2},{1,3},{2,0},{3,1},{4,6},{5,7},{6,4},{7,5},{8,10},{9,11},{10,... | collective-permute-start | bytes 9224 | tf_op jit(solution)/shard_map/ppermute | solution.py:496
  53.0 5.4 %collective-permute-start.16 = (f32[3,256]{1,0:T(4,128)S(1)}, f32[3,256]{1,0:T(4,128)S(1)}, u32[]{:S(2)}, u32[]{:S(2)}) collective-permute-start(f32[3,256]{1,0:T(4,128)S(1)} %select_add_fusion), channel_id=1, source_target_pairs={{0,3},{1,2},{2,1},{3,0},{4,7},{5,6},{6,5},{7,4},{8,11},{9,10},{10,... | collective-permute-start | bytes 9224 | tf_op jit(solution)/shard_map/ppermute | solution.py:496
